TPU v7x, 256 devices: a whole 4x4x8 slice. The times are simulated.
256 devices in a mesh: req: 64 (over z, x, core), tp: 4 (over y).
Axes of the slice: x: 4, y: 4, z: 8, core: 2. Of those that a mesh axis runs over, the one named last changes fastest.
Arguments:
- patches: bfloat16 [65536, 1408], P('req')
- segment_ids: int32 [65536], P('req'), may hold values from 0 to 15, as said below
- grid_sides: int32 [65536], P('req'), may hold values from 8 to 32, as said below
- split_plan: int32 [64, 2], P('req'), may hold values from 0 to 960, as said below
- owner_dev: int32 [16384], P('req'), may hold values from 0 to 63, as said below
- dest_row: int32 [16384], P('req'), may hold values from 0 to 255, as said below
- ln_gain: float32 [1408], replicated, may hold values from 0.25 to 1.75
- ln_bias: float32 [1408], replicated, may hold values from -3 to 3
- w_qkv: bfloat16 [3, 1408, 1408], P(None, 'tp')
- w_out: bfloat16 [1408, 1408], P('tp'), may hold values from -0.625 to 0.625
- w_proj: bfloat16 [5632, 2048], P(None, 'tp'), may hold values from -0.078125 to 0.078125
Outputs:
- vision_tokens: bfloat16 [16384, 2048], P('req', 'tp')
Inputs may be any that keep to these rules, and one draw needn't show every extreme that they name: `segment_ids`: within each packed row the ids start at 0, never fall, and one id's patches are contiguous; an image with grid side s has s * s patches (the last image of the whole packing may be cut short) and lies in at most two neighbouring rows. `grid_sides`: all patches of one image share its grid side, a multiple of 8. split_plan[r, 0] is the number of patches of row r's first image that lie in row r - 1, split_plan[r, 1] the number of patches of row r's last image that lie in row r + 1; both are 0 where no image crosses. `owner_dev`: the merged tokens of one row form blocks of 8 consecutive merged tokens; each block goes whole to one owner, a row's blocks go to different owners, and every owner receives 1024 // 4 merged tokens. `dest_row`: every row of every owner's output receives exactly one merged token.
All inputs are finite; a program needn't handle non-finite values.
Results may differ from a plain program's by a relative error of at most 0.019.
Values may be sent and summed in bfloat16 or wider, within the bound.
No kernel may reach another device: no remote copies, remote signals or barrier semaphores. Data moves between devices by JAX's collectives and lax.ppermute only.
A program may use at most 128 MiB of HBM per device.

v0:
```python
import jax
import jax.numpy as jnp
from jax import lax
from jax.sharding import PartitionSpec as P

HD = 88


def extended(value, sides, width):
    for axis, dim in sides:
        count, length = (lax.axis_size(axis), value.shape[dim])
        up = [(i, (i + 1) % count) for i in range(count - 1)]
        down = [(j, i) for i, j in up]
        last = lax.slice_in_dim(value, length - width, length, axis=dim)
        leading = lax.slice_in_dim(value, 0, width, axis=dim)
        before = lax.ppermute(last, axis, up)
        after = lax.ppermute(leading, axis, down)
        value = jnp.concatenate([before, value, after], axis=dim)
    return value


def layer_norm(inputs, scale_vec, shift_vec):
    widened = inputs.astype(jnp.float32)
    centred = widened - jnp.mean(widened, axis=-1, keepdims=True)
    variance = jnp.mean(centred * centred, axis=-1, keepdims=True)
    return (centred * lax.rsqrt(variance + 1e-06) * scale_vec + shift_vec).astype(jnp.bfloat16)


def grid_positions(seg_row, side_row, first_offset):
    row_len = seg_row.shape[0]
    tok_index = jnp.arange(row_len, dtype=jnp.int32)
    boundary = jnp.concatenate([jnp.ones((1,), dtype=bool), seg_row[1:] != seg_row[:-1]])
    seg_start = lax.cummax(jnp.where(boundary, tok_index, 0), axis=0)
    offset = tok_index - seg_start + jnp.where(seg_row == 0, first_offset, 0)
    half_side = side_row // 2
    window = offset // 4
    corner = offset % 4
    return (2 * (window // half_side) + corner // 2, 2 * (window % half_side) + corner % 2)


def key_labels(seg_row, plan_row):
    row_len = seg_row.shape[0]
    tok_index = jnp.arange(row_len, dtype=jnp.int32)
    before = jnp.where(tok_index >= row_len - plan_row[0], 0, -1).astype(jnp.int32)
    after_keys = jnp.where(tok_index < plan_row[1], seg_row[row_len - 1], -1)
    return jnp.concatenate([before, seg_row, after_keys])


def rotate_pairs(channels, angles, axis_pos):
    quarter = channels.shape[axis_pos] // 2
    first_half = lax.slice_in_dim(channels, 0, quarter, axis=axis_pos)
    second_half = lax.slice_in_dim(channels, quarter, 2 * quarter, axis=axis_pos)
    cosine = jnp.cos(angles)
    sine_tab = jnp.sin(angles)
    return jnp.concatenate(
        [
            first_half * cosine - second_half * sine_tab,
            second_half * cosine + first_half * sine_tab,
        ],
        axis=axis_pos,
    )


def apply_rope(channels, row_angles, col_angles, axis_pos):
    half_width = channels.shape[axis_pos] // 2
    row_part = rotate_pairs(
        lax.slice_in_dim(channels, 0, half_width, axis=axis_pos), row_angles, axis_pos
    )
    col_part = rotate_pairs(
        lax.slice_in_dim(channels, half_width, 2 * half_width, axis=axis_pos), col_angles, axis_pos
    )
    return jnp.concatenate([row_part, col_part], axis=axis_pos)


def on_device(
    patches,
    segment_ids,
    grid_sides,
    split_plan,
    owner_dev,
    dest_row,
    ln_gain,
    ln_bias,
    w_qkv,
    w_out,
    w_proj,
):
    tok_count = patches.shape[0]
    feat_width = patches.shape[1]
    local_width = w_qkv.shape[1]
    local_heads = local_width // HD
    normed = layer_norm(patches, ln_gain, ln_bias)
    mixed_qkv = jnp.einsum("td,kcd->kct", normed, w_qkv, preferred_element_type=jnp.float32)
    grid_row, grid_col = grid_positions(segment_ids, grid_sides, split_plan[0, 0])
    quarter = HD // 4
    frequency = 10000.0 ** (-jnp.arange(quarter, dtype=jnp.float32) / quarter)
    row_angles = frequency[:, None] * grid_row.astype(jnp.float32)[None, :]
    col_angles = frequency[:, None] * grid_col.astype(jnp.float32)[None, :]
    shaped = mixed_qkv.reshape(3, local_heads, HD, tok_count)
    queries = apply_rope(shaped[0], row_angles, col_angles, 1).astype(jnp.bfloat16)
    key_rot = apply_rope(shaped[1], row_angles, col_angles, 1)
    key_value = jnp.stack([key_rot, shaped[2]]).astype(jnp.bfloat16)
    near_kv = extended(key_value, (("req", 3),), tok_count)
    near_keys = near_kv[0]
    near_values = near_kv[1]
    labels = key_labels(segment_ids, split_plan[0])
    block_rows = min(512, tok_count)
    w_heads = w_out.reshape(local_heads, HD, feat_width)

    def attend_block(first_row):
        q_block = lax.dynamic_slice_in_dim(queries, first_row, block_rows, 2)
        seg_block = lax.dynamic_slice_in_dim(segment_ids, first_row, block_rows, 0)
        allowed = seg_block[:, None] == labels[None, :]
        scores = jnp.einsum(
            "hcq,hck->hqk", q_block, near_keys, preferred_element_type=jnp.float32
        ) * HD ** (-0.5)
        scores = jnp.where(allowed[None], scores, -1e30)
        largest = jnp.max(scores, axis=-1, keepdims=True)
        weights = jnp.exp(scores - largest)
        attn_probs = (weights / jnp.sum(weights, axis=-1, keepdims=True)).astype(jnp.bfloat16)
        heads_out = jnp.einsum(
            "hqk,hck->hcq", attn_probs, near_values, preferred_element_type=jnp.float32
        ).astype(jnp.bfloat16)
        return jnp.einsum("hcq,hcd->qd", heads_out, w_heads, preferred_element_type=jnp.float32)

    block_starts = jnp.arange(tok_count // block_rows, dtype=jnp.int32) * block_rows
    partial_value = lax.map(attend_block, block_starts).reshape(tok_count, feat_width)
    attn_sum = lax.psum(partial_value.astype(jnp.bfloat16), "tp").astype(jnp.float32)
    mixed_rows = (patches.astype(jnp.float32) + attn_sum).astype(jnp.bfloat16)
    merged = mixed_rows.reshape(tok_count // 4, 4 * feat_width)
    projected = jnp.dot(merged, w_proj, preferred_element_type=jnp.float32).astype(jnp.bfloat16)
    per_owner = owner_dev.shape[0]
    peer_count = lax.axis_size("req")
    owner_slots = 2 * per_owner // peer_count
    matches = (owner_dev[:, None] == jnp.arange(peer_count, dtype=jnp.int32)[None, :]).astype(
        jnp.int32
    )
    arrival = jnp.sum(jnp.cumsum(matches, axis=0) * matches, axis=1) - 1
    send_slot = owner_dev * owner_slots + arrival
    out_cols = projected.shape[1]
    send_rows = (
        jnp.zeros((peer_count * owner_slots, out_cols), jnp.bfloat16).at[send_slot].set(projected)
    )
    send_dest = (
        jnp.full((peer_count * owner_slots,), per_owner, jnp.int32).at[send_slot].set(dest_row)
    )
    got_rows, got_dest = (
        lax.all_to_all(send_rows, "req", split_axis=0, concat_axis=0, tiled=True),
        lax.all_to_all(send_dest, "req", split_axis=0, concat_axis=0, tiled=True),
    )
    return jnp.zeros((per_owner, out_cols), jnp.bfloat16).at[got_dest].set(got_rows, mode="drop")


def solution(mesh):
    placed = (
        P("req", None),
        P("req"),
        P("req"),
        P("req", None),
        P("req"),
        P("req"),
        P(),
        P(),
        P(None, "tp", None),
        P("tp", None),
        P(None, "tp"),
    )
    return jax.shard_map(
        on_device, mesh=mesh, in_specs=placed, out_specs=P("req", "tp"), check_vma=False
    )
```

profile of v0, /device:TPU:1, one launch (start us, length us, event | category | flops | bytes accessed | tf_op | source)
XLA Modules:
  0.0 257.5 jit_solution(7537347584126004869)
XLA Ops:
  6.6 2.4 convert_reduce_fusion
  10.3 3.8 %fusion.38 = f32[3,352,1024]{2,1,0:T(8,128)S(1)} fusion(bf16[3,352,1408]{2,1,0:T(8,128)(2,1)S(1)} %copy-done, bf16[1024,1408]{1,0:T(8,128)(2,1)S(1)} %copy-done.2, f32[1408]{0:T(1024)S(1)} %copy-done.9, f32[1408]{0:T(1024)S(1)} %copy-done.10, f32[1024]{0:T(1024)S(1)} %add_rsqrt_fusion, f32[1024]{0:T(1024)S(1)} %broadcast_multiply_fusion), kind=kOutput, calls=%fused_computation.42 | convolution fusion | flops 3053715456 | bytes 10202112 | tf_op jit(solution)/shard_map/td,kcd->kct/dot_general | solution.py:93
  18.6 1.8 subtract_convert_fusion.1
  21.8 4.5 %collective-permute-start = (bf16[2,4,88,1024]{3,2,1,0:T(8,128)(2,1)}, bf16[2,4,88,1024]{3,2,1,0:T(8,128)(2,1)}, u32[]{:S(2)}, u32[]{:S(2)}) collective-permute-start(bf16[2,4,88,1024]{3,2,1,0:T(8,128)(2,1)} %pad_maximum_fusion.1), channel_id=1, source_target_pairs={{0,4},{4,8},{8,12},{12,16},{16,20},{20,24},{24,28},{28,32},{32,36}... | collective-permute-start | bytes 4325384 | tf_op jit(solution)/shard_map/ppermute | solution.py:16
  26.3 3.0 %collective-permute-start.1 = (bf16[2,4,88,1024]{3,2,1,0:T(8,128)(2,1)}, bf16[2,4,88,1024]{3,2,1,0:T(8,128)(2,1)}, u32[]{:S(2)}, u32[]{:S(2)}) collective-permute-start(bf16[2,4,88,1024]{3,2,1,0:T(8,128)(2,1)} %pad_maximum_fusion.1), channel_id=1, source_target_pairs={{4,0},{8,4},{12,8},{16,12},{20,16},{24,20},{28,24},{32,28},{36,32}... | collective-permute-start | bytes 4325384 | tf_op jit(solution)/shard_map/ppermute | solution.py:17
  33.2 9.4 %collective-permute-done = bf16[2,4,88,1024]{3,2,1,0:T(8,128)(2,1)} collective-permute-done((bf16[2,4,88,1024]{3,2,1,0:T(8,128)(2,1)}, bf16[2,4,88,1024]{3,2,1,0:T(8,128)(2,1)}, u32[]{:S(2)}, u32[]{:S(2)}) %collective-permute-start) | collective-permute-done | bytes 1441824 | tf_op jit(solution)/shard_map/ppermute | solution.py:16
  42.5 4.4 %collective-permute-done.1 = bf16[2,4,88,1024]{3,2,1,0:T(8,128)(2,1)} collective-permute-done((bf16[2,4,88,1024]{3,2,1,0:T(8,128)(2,1)}, bf16[2,4,88,1024]{3,2,1,0:T(8,128)(2,1)}, u32[]{:S(2)}, u32[]{:S(2)}) %collective-permute-start.1) | collective-permute-done | bytes 1441824 | tf_op jit(solution)/shard_map/ppermute | solution.py:17
  46.9 2.0 pad_maximum_fusion
  48.9 2.5 slice_bitcast_fusion
  51.4 69.2 %while.10 = (s32[]{:T(128)}, bf16[2,512,1408]{2,1,0:T(8,128)(2,1)}, s32[2]{0:T(128)S(1)}, s32[1024]{0:T(1024)S(1)}, s32[3072]{0:T(1024)S(1)}, /*index=5*/bf16[4,...) while((s32[]{:T(128)}, bf16[2,512,1408]{2,1,0:T(8,128)(2,1)}, ...), condition=%wide.region_11.12_spmd, body=%wide.region_8.11_spmd.sunk | while | flops 2761608192 | bytes 62073512 | solution.py:127
  55.1 15.8 %fusion.91 = (f32[4,512]{1,0:T(4,128)S(1)}, f32[4,512,3072]{2,1,0:T(8,128)}) fusion(pred[512,3072]{1,0:T(8,128)(4,1)S(1)} %broadcast_compare_fusion.2, bf16[4,88,3072]{2,1,0:T(8,128)(2,1)} %get-tuple-element.190, bf16[4,88,1024]{2,1,0:T(8,128)(2,1)S(1)} %get-tuple-element.189, s32[]{:T(128)S(6)} %select_n.147), kind=kOutput, calls=%fused_computation.129.clone.1 | convolution fusion | flops 1132465152 | bytes 29270020 | tf_op jit(solution)/shard_map/while/body/eval_jaxpr/sub | solution.py:119
  70.9 15.1 %fusion.92 = bf16[2,512,1408]{2,1,0:T(8,128)(2,1)} fusion(bf16[2,512,1408]{2,1,0:T(8,128)(2,1)} %get-tuple-element.173, s32[]{:T(128)} %get-tuple-element.172, bf16[4,88,1408]{2,1,0:T(8,128)(2,1)} %get-tuple-element.192, bf16[4,88,3072]{2,1,0:T(8,128)(2,1)} %get-tuple-element.191, f32[4,512,3072]{2,1,0:T(8,128)} %get-tuple-element.158, ...), kind=kOutput, calls=%fused_computation.13.clone.1 | convolution fusion | flops 1627570176 | bytes 31212032 | tf_op jit(solution)/shard_map/while/body/eval_jaxpr/hcq,hcd->qd/dot_general | solution.py:124
  89.8 15.8 %fusion.91 = (f32[4,512]{1,0:T(4,128)S(1)}, f32[4,512,3072]{2,1,0:T(8,128)}) fusion(pred[512,3072]{1,0:T(8,128)(4,1)S(1)} %broadcast_compare_fusion.2, bf16[4,88,3072]{2,1,0:T(8,128)(2,1)} %get-tuple-element.190, bf16[4,88,1024]{2,1,0:T(8,128)(2,1)S(1)} %get-tuple-element.189, s32[]{:T(128)S(6)} %select_n.147), kind=kOutput, calls=%fused_computation.129.clone.1 | convolution fusion | flops 1132465152 | bytes 29270020 | tf_op jit(solution)/shard_map/while/body/eval_jaxpr/sub | solution.py:119
  105.6 15.0 %fusion.92 = bf16[2,512,1408]{2,1,0:T(8,128)(2,1)} fusion(bf16[2,512,1408]{2,1,0:T(8,128)(2,1)} %get-tuple-element.173, s32[]{:T(128)} %get-tuple-element.172, bf16[4,88,1408]{2,1,0:T(8,128)(2,1)} %get-tuple-element.192, bf16[4,88,3072]{2,1,0:T(8,128)(2,1)} %get-tuple-element.191, f32[4,512,3072]{2,1,0:T(8,128)} %get-tuple-element.158, ...), kind=kOutput, calls=%fused_computation.13.clone.1 | convolution fusion | flops 1627570176 | bytes 31212032 | tf_op jit(solution)/shard_map/while/body/eval_jaxpr/hcq,hcd->qd/dot_general | solution.py:124
  122.2 1.6 scatter_custom_fusion
  124.5 13.9 %all-to-all-start = ((s32[64,8,1]{1,2,0:T(1,128)}), s32[64,8,1]{1,2,0:T(1,128)S(1)}, u32[]{:S(2)}, u32[]{:S(2)}) async-start(s32[64,8,1]{1,2,0:T(1,128)} %bitcast.6), calls=%async_computation | async-start | bytes 65536 | tf_op jit(solution)/shard_map/all_to_all | solution.py:149
  138.3 63.5 %all-reduce.2.cloned.1.call-done = bf16[1024,1408]{1,0:T(8,128)(2,1)} async-done(((bf16[1024,1408]{1,0:T(8,128)(2,1)}), bf16[1024,1408]{1,0:T(8,128)(2,1)}) %all-reduce.2.cloned.1.call-update) | async-done | bytes 2883600 | tf_op jit(solution)/shard_map/psum | solution.py:128
  201.9 4.1 %fusion.30 = bf16[1024,1408]{1,0:T(8,128)(2,1)} fusion(bf16[1024,1408]{1,0:T(8,128)(2,1)S(1)} %copy-done.3, bf16[1024,1408]{1,0:T(8,128)(2,1)} %all-reduce.2.cloned.1.call-done), kind=kLoop, calls=%fused_computation.34 | loop fusion | flops 5767168 | bytes 8650752 | tf_op jit(solution)/shard_map/convert_element_type | solution.py:129
  206.0 5.6 %reshape.244 = bf16[256,5632]{1,0:T(8,128)(2,1)} reshape(bf16[1024,1408]{1,0:T(8,128)(2,1)} %fusion.30) | data formatting | bytes 5767168 | tf_op jit(solution)/shard_map/reshape | solution.py:130
  211.6 5.3 %convolution_convert_fusion = bf16[256,512]{1,0:T(8,128)(2,1)S(1)} fusion(bf16[256,5632]{1,0:T(8,128)(2,1)} %reshape.244, bf16[5632,512]{1,0:T(8,128)(2,1)} %param.23), kind=kOutput, calls=%fused_computation.47 | convolution fusion | flops 1476526080 | bytes 8912896 | tf_op jit(solution)/shard_map/dot_general | solution.py:131
  216.9 2.3 scatter_custom_fusion.1
  219.3 10.7 %all-to-all-start.1 = ((bf16[64,8,512]{2,1,0:T(8,128)(2,1)}), bf16[64,8,512]{2,1,0:T(8,128)(2,1)S(1)}, u32[]{:S(2)}, u32[]{:S(2)}) async-start(bf16[64,8,512]{2,1,0:T(8,128)(2,1)} %bitcast.23), calls=%async_computation.1 | async-start | bytes 1048576 | tf_op jit(solution)/shard_map/all_to_all | solution.py:148
  232.8 14.9 %all-to-all-done.1 = bf16[64,8,512]{2,1,0:T(8,128)(2,1)S(1)} async-done(((bf16[64,8,512]{2,1,0:T(8,128)(2,1)}), bf16[64,8,512]{2,1,0:T(8,128)(2,1)S(1)}, u32[]{:S(2)}, u32[]{:S(2)}) %all-to-all-start.1) | async-done | bytes 524320 | tf_op jit(solution)/shard_map/all_to_all | solution.py:148
  247.6 3.0 %scatter_custom_fusion.2 = bf16[256,512]{1,0:T(8,128)(2,1)} fusion(s32[512]{0:T(512)S(1)} %bitcast.91, bf16[64,8,512]{2,1,0:T(8,128)(2,1)S(1)} %all-to-all-done.1, bf16[]{:T(256)} %constant.105.clone.1), kind=kCustom, calls=%fused_computation.50 | custom fusion | bytes 786434 | tf_op jit(solution)/shard_map/scatter | solution.py:151
  (67 shorter events, 18.8 us)
Async XLA Ops:
  6.5 3.7 %copy-start = (bf16[3,352,1408]{2,1,0:T(8,128)(2,1)S(1)}, bf16[3,352,1408]{2,1,0:T(8,128)(2,1)}, u32[]{:S(2)}) copy-start(bf16[3,352,1408]{2,1,0:T(8,128)(2,1)} %param.21) | copy-start | bytes 8921092
  6.5 195.3 %all-reduce.2.cloned.1.call-start = ((), (), s32[]{:S(2)}) async-start(), calls=%async_computation.2 | async-start | bytes 5767168 | tf_op jit(solution)/shard_map/psum | solution.py:128
  6.5 2.8 %copy-start.2 = (bf16[1024,1408]{1,0:T(8,128)(2,1)S(1)}, bf16[1024,1408]{1,0:T(8,128)(2,1)}, u32[]{:S(2)}) copy-start(bf16[1024,1408]{1,0:T(8,128)(2,1)} %param.13) | copy-start | bytes 8650756
  6.6 3.7 %copy-start.9 = (f32[1408]{0:T(1024)S(1)}, f32[1408]{0:T(1024)}, u32[]{:S(2)}) copy-start(f32[1408]{0:T(1024)} %param.20) | copy-start | bytes 16900
  6.6 3.7 %copy-start.10 = (f32[1408]{0:T(1024)S(1)}, f32[1408]{0:T(1024)}, u32[]{:S(2)}) copy-start(f32[1408]{0:T(1024)} %param.19) | copy-start | bytes 16900
  14.1 1.5 copy-start.8
  14.1 2.1 copy-start.5
  14.1 2.8 %copy-start.7 = (s32[1024]{0:T(1024)S(1)}, s32[1024]{0:T(1024)}, u32[]{:S(2)}) copy-start(s32[1024]{0:T(1024)} %param.15) | copy-start | bytes 12292
  21.8 20.8 %collective-permute-start = (bf16[2,4,88,1024]{3,2,1,0:T(8,128)(2,1)}, bf16[2,4,88,1024]{3,2,1,0:T(8,128)(2,1)}, u32[]{:S(2)}, u32[]{:S(2)}) collective-permute-start(bf16[2,4,88,1024]{3,2,1,0:T(8,128)(2,1)} %pad_maximum_fusion.1), channel_id=1, source_target_pairs={{0,4},{4,8},{8,12},{12,16},{16,20},{20,24},{24,28},{28,32},{32,36}... | collective-permute-start | bytes 4325384 | tf_op jit(solution)/shard_map/ppermute | solution.py:16
  26.3 20.6 %collective-permute-start.1 = (bf16[2,4,88,1024]{3,2,1,0:T(8,128)(2,1)}, bf16[2,4,88,1024]{3,2,1,0:T(8,128)(2,1)}, u32[]{:S(2)}, u32[]{:S(2)}) collective-permute-start(bf16[2,4,88,1024]{3,2,1,0:T(8,128)(2,1)} %pad_maximum_fusion.1), channel_id=1, source_target_pairs={{4,0},{8,4},{12,8},{16,12},{20,16},{24,20},{28,24},{32,28},{36,32}... | collective-permute-start | bytes 4325384 | tf_op jit(solution)/shard_map/ppermute | solution.py:17
  48.9 2.5 copy-start.4
  120.5 0.7 copy-start.6
  120.6 81.3 %copy-start.3 = (bf16[1024,1408]{1,0:T(8,128)(2,1)S(1)}, bf16[1024,1408]{1,0:T(8,128)(2,1)}, u32[]{:S(2)}) copy-start(bf16[1024,1408]{1,0:T(8,128)(2,1)} %param.13) | copy-start | bytes 8650756
  124.5 94.8 %all-to-all-start = ((s32[64,8,1]{1,2,0:T(1,128)}), s32[64,8,1]{1,2,0:T(1,128)S(1)}, u32[]{:S(2)}, u32[]{:S(2)}) async-start(s32[64,8,1]{1,2,0:T(1,128)} %bitcast.6), calls=%async_computation | async-start | bytes 65536 | tf_op jit(solution)/shard_map/all_to_all | solution.py:149
  211.6 39.0 %copy-start.1 = (bf16[3,352,1408]{2,1,0:T(8,128)(2,1)S(1)}, bf16[3,352,1408]{2,1,0:T(8,128)(2,1)}, u32[]{:S(2)}) copy-start(bf16[3,352,1408]{2,1,0:T(8,128)(2,1)} %param.21) | copy-start | bytes 8921092
  219.3 28.4 %all-to-all-start.1 = ((bf16[64,8,512]{2,1,0:T(8,128)(2,1)}), bf16[64,8,512]{2,1,0:T(8,128)(2,1)S(1)}, u32[]{:S(2)}, u32[]{:S(2)}) async-start(bf16[64,8,512]{2,1,0:T(8,128)(2,1)} %bitcast.23), calls=%async_computation.1 | async-start | bytes 1048576 | tf_op jit(solution)/shard_map/all_to_all | solution.py:148
Sparse Core Ops, SparseCore 0:
  120.7 81.1 all-reduce.1
where the time goes:
time: 258 us
  waiting for transfers between devices  92.2 us (36%)
  matrix products  70.8 us (27%)
  starting transfers between devices  32 us (12%)
  local copies, waits for them, and re-layouts  22.7 us (9%)
  other arithmetic  21.3 us (8%)
  between operations  14.3 us (6%)
  loops' own time  4.17 us (2%)
    psum x1, waiting for transfers between devices, on_device(): lax.psum(partial_value.astype(jnp.bfloat16), 'tp').astype(jnp.float32)  63.5 us
    sub x2, matrix products, attend_block(): weights = jnp.exp(scores - largest)  31.7 us
    dot_general x2, matrix products, attend_block(): jnp.einsum('hcq,hcd->qd', heads_out, w_heads, preferred_element_type=jnp....  30.1 us
    all_to_all x1, waiting for transfers between devices, on_device(): lax.all_to_all(send_rows, 'req', split_axis=0, concat_axis=0, tiled=True)  14.9 us
    all_to_all x1, starting transfers between devices, on_device(): lax.all_to_all(send_dest, 'req', split_axis=0, concat_axis=0, tiled=True)  13.9 us
    all_to_all x1, starting transfers between devices, on_device(): lax.all_to_all(send_rows, 'req', split_axis=0, concat_axis=0, tiled=True)  10.7 us
    ppermute x1, waiting for transfers between devices, extended(): before = lax.ppermute(last, axis, up)  9.36 us
    reshape x1, local copies, waits for them, and re-layouts, on_device(): merged = mixed_rows.reshape(tok_count // 4, 4 * feat_width)  5.62 us
  transfers between devices with their start and end apart: 5, of which 4 were waited for; matrix products, arithmetic and copies ran while one was open for 10% of the time, Pallas kernels for 0%

commit v1 on v0

v1 whole, which is shorter than its diff:
```python
import functools

import jax
import jax.numpy as jnp
import numpy as np
from jax import lax
from jax.experimental import pallas as pl
from jax.experimental.pallas import tpu as pltpu
from jax.sharding import PartitionSpec as P

HD = 88
QUARTER = HD // 4
SIDE_MAX = 32
AUG = 128
VAUG = 96
BIG = 1e30
TILE = 256
BLK = 256
F32 = jnp.float32
BF16 = jnp.bfloat16
NT = (((1,), (1,)), ((), ()))
NN = (((1,), (0,)), ((), ()))
TN = (((0,), (0,)), ((), ()))
LOG2E = 1.4426950408889634


def rope_table():
    freq = 10000.0 ** (-np.arange(QUARTER, dtype=np.float64) / QUARTER)
    chan = np.arange(HD)
    pos = np.arange(SIDE_MAX, dtype=np.float64)
    angle = freq[chan % QUARTER][:, None] * pos[None, :]
    sign = np.where(chan % (2 * QUARTER) < QUARTER, -1.0, 1.0)[:, None]
    in_row = (chan < 2 * QUARTER)[:, None]
    halves = []
    for part in (np.cos(angle), sign * np.sin(angle)):
        halves.append(np.concatenate([np.where(in_row, part, 0.0), np.where(in_row, 0.0, part)], axis=1))
    table = np.concatenate(halves, axis=0).astype(np.float32)
    terms = []
    for _ in range(3):
        term = table.astype(jnp.bfloat16)
        terms.append(term)
        table = table - term.astype(np.float32)
    return np.concatenate(terms, axis=1)


def seg_counts(seg):
    ids = lax.broadcasted_iota(jnp.int32, (16, seg.shape[1]), 0)
    below = jnp.sum((seg < ids).astype(F32), axis=1, keepdims=True)
    return below


def label_rows(label):
    ids = lax.broadcasted_iota(jnp.int32, (AUG - HD, label.shape[1]), 0)
    return (ids == jnp.where(label < 0, 16, label)).astype(F32)


def qkv_kernel(plan_ref, table_ref, seg_ref, segt_ref, side_ref, x_ref, gain_ref, bias_ref, w_ref, q_ref, kv_ref):
    heads = q_ref.shape[0]
    step = pl.program_id(0)
    x = x_ref[...].astype(F32)
    centred = x - jnp.mean(x, axis=1, keepdims=True)
    variance = jnp.mean(centred * centred, axis=1, keepdims=True)
    normed = (centred * lax.rsqrt(variance + 1e-6) * gain_ref[...] + bias_ref[...]).astype(BF16)

    below = seg_counts(seg_ref[...])
    seg = segt_ref[...]
    ids = lax.broadcasted_iota(jnp.int32, (16, TILE), 0)
    start = jnp.sum(jnp.where(ids == seg, below, 0.0), axis=0, keepdims=True).astype(jnp.int32)
    token = lax.broadcasted_iota(jnp.int32, (1, TILE), 1) + step * TILE
    offset = token - start + jnp.where(seg == 0, plan_ref[0, 0], 0)
    window = lax.shift_right_logical(offset, 2)
    corner = offset & 3
    half = lax.shift_right_logical(side_ref[...], 1)
    down = jnp.floor((window.astype(F32) + 0.5) / half.astype(F32)).astype(jnp.int32)
    grid_row = 2 * down + lax.shift_right_logical(corner, 1)
    grid_col = 2 * (window - down * half) + (corner & 1)
    pos = lax.broadcasted_iota(jnp.int32, (2 * SIDE_MAX, TILE), 0)
    hot = ((pos == grid_row) | (pos == grid_col + SIDE_MAX)).astype(F32).astype(BF16)
    hot = jnp.concatenate([hot, hot, hot], axis=0)
    angles = lax.dot_general(table_ref[...], hot, NN, preferred_element_type=F32)
    cosine, sine = angles[:HD], angles[HD:]
    first = lax.broadcasted_iota(jnp.int32, (HD, TILE), 0) % (2 * QUARTER) < QUARTER

    def rotated(value):
        partner = jnp.where(first, pltpu.roll(value, HD - QUARTER, 0), pltpu.roll(value, QUARTER, 0))
        return value * cosine + partner * sine

    aug = lax.broadcasted_iota(jnp.int32, (AUG - HD, TILE), 0)
    barred = jnp.where(aug == jnp.broadcast_to(seg, aug.shape), 0.0, jnp.where(aug <= 16, -BIG, 0.0))
    queries = lax.dot_general(w_ref[0], normed, NT, preferred_element_type=F32)
    keys = lax.dot_general(w_ref[1], normed, NT, preferred_element_type=F32)
    values = lax.dot_general(w_ref[2], normed, NT, preferred_element_type=F32)
    for h in range(heads):
        span = slice(h * HD, (h + 1) * HD)
        query = rotated(queries[span]) * (HD**-0.5 * LOG2E)
        q_ref[h] = jnp.concatenate([query, barred], axis=0).astype(BF16)
        kv_ref[0, h] = rotated(keys[span]).astype(BF16)
        kv_ref[1, h] = values[span].astype(BF16)


def qkv_call(patches, seg, sides, plan, gain, bias, w_qkv, table):
    count, width = patches.shape
    local = w_qkv.shape[1]
    heads = local // HD
    whole = lambda *shape: pl.BlockSpec(shape, lambda i: (0,) * len(shape))
    return pl.pallas_call(
        qkv_kernel,
        grid=(count // TILE,),
        in_specs=[
            pl.BlockSpec(memory_space=pltpu.SMEM),
            whole(*table.shape),
            whole(1, count),
            pl.BlockSpec((1, TILE), lambda i: (0, i)),
            pl.BlockSpec((1, TILE), lambda i: (0, i)),
            pl.BlockSpec((TILE, width), lambda i: (i, 0)),
            whole(1, width),
            whole(1, width),
            whole(3, local, width),
        ],
        out_specs=[
            pl.BlockSpec((heads, AUG, TILE), lambda i: (0, 0, i)),
            pl.BlockSpec((2, heads, HD, TILE), lambda i: (0, 0, 0, i)),
        ],
        out_shape=[
            jax.ShapeDtypeStruct((heads, AUG, count), BF16),
            jax.ShapeDtypeStruct((2, heads, HD, count), BF16),
        ],
        compiler_params=pltpu.CompilerParams(vmem_limit_bytes=48 << 20),
        cost_estimate=pl.CostEstimate(flops=6 * count * width * local, bytes_accessed=10 << 20, transcendentals=0),
        name="qkv",
    )(plan, table, seg, seg, sides, patches, gain, bias, w_qkv)


def prepare_block(kv_ref, label, keys, values, base):
    heads = keys.shape[0]
    rows = label_rows(label)
    extra = VAUG - HD
    ones = (lax.broadcasted_iota(jnp.int32, (extra, BLK), 0) == 0).astype(F32)
    for h in range(heads):
        block = jnp.concatenate([kv_ref[0, h, :, pl.ds(base, BLK)].astype(F32), rows], axis=0)
        keys[h, pl.ds(base, BLK), :] = block.T.astype(BF16)
        block = jnp.concatenate([kv_ref[1, h, :, pl.ds(base, BLK)].astype(F32), ones], axis=0)
        values[h, :, pl.ds(base, BLK)] = block.astype(BF16)


def attend(q_ref, keys, values, acc, top, q_base, k_base):
    heads = keys.shape[0]
    for h in range(heads):
        query = q_ref[h, :, pl.ds(q_base, BLK)]
        scores = lax.dot_general(keys[h, pl.ds(k_base, BLK), :], query, NN, preferred_element_type=F32)
        old = top[h : h + 1, pl.ds(q_base, BLK)]
        new = jnp.maximum(old, jnp.max(scores, axis=0, keepdims=True))
        weights = jnp.exp2(scores - new).astype(BF16)
        part = lax.dot_general(values[h, :, pl.ds(k_base, BLK)], weights, NN, preferred_element_type=F32)
        acc[h, :, pl.ds(q_base, BLK)] = acc[h, :, pl.ds(q_base, BLK)] * jnp.exp2(old - new) + part
        top[h : h + 1, pl.ds(q_base, BLK)] = new


def own_kernel(sseg_ref, seg_ref, q_ref, kv_ref, acc_ref, top_ref, keys, values):
    count = seg_ref.shape[1]
    seg = seg_ref[...]
    for b in range(count // BLK):
        prepare_block(kv_ref, seg[:, b * BLK : (b + 1) * BLK], keys, values, b * BLK)
    acc_ref[...] = jnp.zeros_like(acc_ref)
    top_ref[...] = jnp.full_like(top_ref, -BIG)

    def block(b, carry):
        q_base = pl.multiple_of(b * BLK, BLK)
        low = jnp.sum((seg < sseg_ref[0, q_base]).astype(jnp.int32))
        high = jnp.sum((seg <= sseg_ref[0, q_base + BLK - 1]).astype(jnp.int32))

        def inner(k, c):
            attend(q_ref, keys, values, acc_ref, top_ref, q_base, pl.multiple_of(k * BLK, BLK))
            return c

        return lax.fori_loop(low // BLK, (high + BLK - 1) // BLK, inner, carry)

    lax.fori_loop(0, count // BLK, block, 0)


def own_call(seg, q, kv):
    heads, _, count = q.shape
    vmem = pl.BlockSpec(memory_space=pltpu.VMEM)
    return pl.pallas_call(
        own_kernel,
        in_specs=[pl.BlockSpec(memory_space=pltpu.SMEM), vmem, vmem, vmem],
        out_specs=[vmem, vmem],
        out_shape=[
            jax.ShapeDtypeStruct((heads, VAUG, count), F32),
            jax.ShapeDtypeStruct((8, count), F32),
        ],
        scratch_shapes=[pltpu.VMEM((heads, count, AUG), BF16), pltpu.VMEM((heads, VAUG, count), BF16)],
        compiler_params=pltpu.CompilerParams(vmem_limit_bytes=48 << 20),
        cost_estimate=pl.CostEstimate(flops=8 << 30, bytes_accessed=8 << 20, transcendentals=4 << 20),
        name="own_keys",
    )(seg, seg, q, kv)


def halo_kernel(plan_ref, sseg_ref, q_ref, acc_in, top_in, before_ref, after_ref, out_ref, acc, top, keys, values):
    heads, _, count = q_ref.shape
    acc[...] = acc_in[...]
    top[...] = top_in[...]
    lead, trail = plan_ref[0, 0], plan_ref[0, 1]
    last = sseg_ref[0, count - 1]
    token = lax.broadcasted_iota(jnp.int32, (1, BLK), 1)

    def before_block(k, carry):
        base = pl.multiple_of(k * BLK, BLK)
        label = jnp.where(token + base >= count - lead, 0, -1)
        prepare_block(before_ref, label, keys, values, base)

        def inner(b, c):
            q_base = pl.multiple_of(b * BLK, BLK)

            @pl.when(sseg_ref[0, q_base] == 0)
            def _():
                attend(q_ref, keys, values, acc, top, q_base, base)

            return c

        return lax.fori_loop(0, count // BLK, inner, carry)

    lax.fori_loop((count - lead) // BLK, count // BLK, before_block, 0)

    def after_block(k, carry):
        base = pl.multiple_of(k * BLK, BLK)
        label = jnp.where(token + base < trail, last, -1)
        prepare_block(after_ref, label, keys, values, base)

        def inner(b, c):
            q_base = pl.multiple_of(b * BLK, BLK)

            @pl.when(sseg_ref[0, q_base + BLK - 1] == last)
            def _():
                attend(q_ref, keys, values, acc, top, q_base, base)

            return c

        return lax.fori_loop(0, count // BLK, inner, carry)

    lax.fori_loop(0, (trail + BLK - 1) // BLK, after_block, 0)
    for h in range(heads):
        out_ref[pl.ds(h * HD, HD), :] = (acc[h, :HD, :] / acc[h, HD : HD + 1, :]).astype(BF16)


def halo_call(plan, seg, q, acc, top, before, after):
    heads, _, count = q.shape
    vmem = pl.BlockSpec(memory_space=pltpu.VMEM)
    smem = pl.BlockSpec(memory_space=pltpu.SMEM)
    return pl.pallas_call(
        halo_kernel,
        in_specs=[smem, smem, vmem, vmem, vmem, vmem, vmem],
        out_specs=vmem,
        out_shape=jax.ShapeDtypeStruct((heads * HD, count), BF16),
        scratch_shapes=[
            pltpu.VMEM(acc.shape, F32),
            pltpu.VMEM(top.shape, F32),
            pltpu.VMEM((heads, count, AUG), BF16),
            pltpu.VMEM((heads, VAUG, count), BF16),
        ],
        compiler_params=pltpu.CompilerParams(vmem_limit_bytes=48 << 20),
        cost_estimate=pl.CostEstimate(flops=8 << 30, bytes_accessed=8 << 20, transcendentals=4 << 20),
        name="halo_keys",
    )(plan, seg, q, acc, top, before, after)


def out_kernel(slot_ref, dest_ref, x_ref, own_ref, left_ref, right_ref, far_ref, w_own, w_left, w_right, w_far, proj_hbm, send_ref, mixed, proj, sem):
    step = pl.program_id(0)
    width = x_ref.shape[1]
    copy = pltpu.make_async_copy(proj_hbm, proj, sem)

    @pl.when(step == 0)
    def _():
        copy.start()

    total = x_ref[...].astype(F32)
    for h_ref, w_ref in ((own_ref, w_own), (left_ref, w_left), (right_ref, w_right), (far_ref, w_far)):
        total += lax.dot_general(h_ref[...], w_ref[...], TN, preferred_element_type=F32)
    chunks = width // 128
    base = pl.multiple_of(step * TILE, TILE)
    for c in range(chunks):
        mixed[c, pl.ds(base, TILE), :] = total[:, c * 128 : (c + 1) * 128]

    @pl.when(step == pl.num_programs(0) - 1)
    def _():
        copy.wait()
        rows = mixed.shape[1] // 4
        result = jnp.zeros((rows, proj.shape[1]), F32)
        for j in range(4):
            part = jnp.concatenate([mixed[c, pl.ds(j, rows, stride=4), :] for c in range(chunks)], axis=1).astype(BF16)
            result += lax.dot_general(part, proj[j * width : (j + 1) * width, :], NN, preferred_element_type=F32)
        slots = lax.broadcasted_iota(jnp.int32, (send_ref.shape[0], rows), 0)
        pick = (slots == slot_ref[...]).astype(F32)
        cols = proj.shape[1]
        send_ref[:, :cols] = lax.dot_general(
            pick.astype(BF16), result.astype(BF16), NN, preferred_element_type=F32
        ).astype(BF16)
        dest = jnp.sum(pick * dest_ref[...].astype(F32), axis=1, keepdims=True)
        send_ref[:, cols:] = jnp.broadcast_to(dest, (send_ref.shape[0], 128)).astype(BF16)


def out_call(slot, dest, patches, heads_parts, w_parts, w_proj, slots):
    count, width = patches.shape
    local = heads_parts[0].shape[0]
    cols = w_proj.shape[1]
    whole = lambda *shape: pl.BlockSpec(shape, lambda i: (0,) * len(shape))
    return pl.pallas_call(
        out_kernel,
        grid=(count // TILE,),
        in_specs=[whole(*slot.shape), whole(*dest.shape), pl.BlockSpec((TILE, width), lambda i: (i, 0))]
        + [pl.BlockSpec((local, TILE), lambda i: (0, i))] * 4
        + [whole(local, width)] * 4
        + [pl.BlockSpec(memory_space=pl.ANY)],
        out_specs=whole(slots, cols + 128),
        out_shape=jax.ShapeDtypeStruct((slots, cols + 128), BF16),
        scratch_shapes=[
            pltpu.VMEM((width // 128, count, 128), F32),
            pltpu.VMEM(w_proj.shape, BF16),
            pltpu.SemaphoreType.DMA,
        ],
        compiler_params=pltpu.CompilerParams(vmem_limit_bytes=56 << 20),
        cost_estimate=pl.CostEstimate(flops=6 << 30, bytes_accessed=18 << 20, transcendentals=0),
        name="project",
    )(slot, dest, patches, *heads_parts, *w_parts, w_proj)


def place_kernel(got_ref, out_ref):
    cols = out_ref.shape[1]
    dest = got_ref[:, cols:].astype(F32).astype(jnp.int32)
    dest = jnp.concatenate([dest] * (out_ref.shape[0] // 128), axis=1)
    rows = lax.broadcasted_iota(jnp.int32, dest.shape, 1)
    pick = (rows == dest).astype(F32).astype(BF16)
    out_ref[...] = lax.dot_general(pick, got_ref[:, :cols], TN, preferred_element_type=F32).astype(BF16)


def place_call(got, rows, cols):
    vmem = pl.BlockSpec(memory_space=pltpu.VMEM)
    return pl.pallas_call(
        place_kernel,
        in_specs=[vmem],
        out_specs=vmem,
        out_shape=jax.ShapeDtypeStruct((rows, cols), BF16),
        name="place",
    )(got)


def ring(axis, shift):
    size = lax.axis_size(axis)
    return [(i, (i + shift) % size) for i in range(size)]


def around(block, axis):
    half = block.shape[0] // 2
    left = lax.ppermute(block, axis, ring(axis, 1))
    right = lax.ppermute(block, axis, ring(axis, -1))
    far = jnp.concatenate(
        [
            lax.ppermute(left[:half], axis, ring(axis, 1)),
            lax.ppermute(right[half:], axis, ring(axis, -1)),
        ],
        axis=0,
    )
    return [block, left, right, far]


def on_device(patches, segment_ids, grid_sides, split_plan, owner_dev, dest_row, ln_gain, ln_bias, w_qkv, w_out, w_proj):
    count, width = patches.shape
    rows_out = owner_dev.shape[0]
    peers = lax.axis_size("req")
    lanes = 2 * rows_out // peers
    seg = segment_ids.reshape(1, count)
    table = jnp.asarray(rope_table())
    w_parts = around(w_out, "tp")
    q, kv = qkv_call(
        patches, seg, grid_sides.reshape(1, count), split_plan, ln_gain.reshape(1, width), ln_bias.reshape(1, width), w_qkv, table
    )
    up = [(i, i + 1) for i in range(peers - 1)]
    down = [(j, i) for i, j in up]
    before = lax.ppermute(kv, "req", up)
    after = lax.ppermute(kv, "req", down)
    acc, top = own_call(seg, q, kv)
    heads_out = halo_call(split_plan, seg, q, acc, top, before, after)
    heads_parts = around(heads_out, "tp")
    within = jnp.arange(rows_out, dtype=jnp.int32) % lanes
    slot = (owner_dev * lanes + within).reshape(1, rows_out)
    send = out_call(slot, dest_row.reshape(1, rows_out), patches, heads_parts, w_parts, w_proj, peers * lanes)
    cols = send.shape[1]
    got = lax.all_to_all(send.reshape(peers, lanes, cols), "req", split_axis=0, concat_axis=0, tiled=True)
    return place_call(got.reshape(peers * lanes, cols), rows_out, w_proj.shape[1])


def solution(mesh):
    placed = (
        P("req", None),
        P("req"),
        P("req"),
        P("req", None),
        P("req"),
        P("req"),
        P(),
        P(),
        P(None, "tp", None),
        P("tp", None),
        P(None, "tp"),
    )
    return jax.shard_map(on_device, mesh=mesh, in_specs=placed, out_specs=P("req", "tp"), check_vma=False)
```

time: 258 us -> 143 us (0.55)
  matrix products: 70.8 us -> 0 us
  waiting for transfers between devices: 92.2 us -> 29.4 us
  blocking collectives: 0 us -> 47.5 us
  Pallas kernels: 0 us -> 36.7 us
  other arithmetic: 21.3 us -> 2.53 us
  local copies, waits for them, and re-layouts: 22.7 us -> 7.45 us
  between operations: 14.3 us -> 0.16 us
  starting transfers between devices: 32 us -> 19.3 us
  loops' own time: 4.17 us -> 0 us
    psum x1 -> x0, waiting for transfers between devices: 63.5 us -> none  [on_device(): lax.psum(partial_value.astype(jnp.bfloat16), 'tp').astype(jnp.float32)]
    all_to_all x0 -> x1, blocking collectives: none -> 47.5 us  [on_device(): lax.all_to_all(send.reshape(peers, lanes, cols), 'req', split_axis=0, con...]
    dot_general x4 -> x0, matrix products: 39.2 us -> none  [the longest x2 30.1 us: attend_block(): jnp.einsum('hcq,hcd->qd', heads_out, w_heads, preferred_element_type=jnp....]
    pallas_call x0 -> x5, Pallas kernels: none -> 36.7 us  [the longest x1 12.9 us: out_call(): pl.pallas_call(out_kernel, grid=(count // TILE,), in_specs=[whole(*slot.s...]
    sub x2 -> x0, matrix products: 31.7 us -> none  [attend_block(): weights = jnp.exp(scores - largest)]
    all_to_all x2 -> x0, starting transfers between devices: 24.5 us -> none  [the longest x1 13.9 us: on_device(): lax.all_to_all(send_dest, 'req', split_axis=0, concat_axis=0, tiled=True)]
    ppermute x2 -> x10, waiting for transfers between devices: 13.8 us -> 29.4 us  [the longest x2 11.2 us: around(): lax.ppermute(left[:half], axis, ring(axis, 1))]
    all_to_all x2 -> x0, waiting for transfers between devices: 14.9 us -> none  [the longest x1 14.9 us: on_device(): lax.all_to_all(send_rows, 'req', split_axis=0, concat_axis=0, tiled=True)]
  transfers between devices with their start and end apart: 5 -> 10, of which waited for: 4 -> 7; matrix products, arithmetic and copies ran while one was open for 10% -> 1% of each run, Pallas kernels for 0% -> 10%
where the time goes in v1:
time: 143 us
  blocking collectives  47.5 us (33%)
  Pallas kernels  36.7 us (26%)
  waiting for transfers between devices  29.4 us (21%)
  starting transfers between devices  19.3 us (13%)
  local copies, waits for them, and re-layouts  7.45 us (5%)
  other arithmetic  2.53 us (2%)
    all_to_all x1, blocking collectives, on_device(): lax.all_to_all(send.reshape(peers, lanes, cols), 'req', split_axis=0, con...  47.5 us
    pallas_call x1, Pallas kernels, out_call(): pl.pallas_call(out_kernel, grid=(count // TILE,), in_specs=[whole(*slot.s...  12.9 us
    ppermute x2, waiting for transfers between devices, around(): lax.ppermute(left[:half], axis, ring(axis, 1))  11.2 us
    pallas_call x1, Pallas kernels, qkv_call(): pl.pallas_call(qkv_kernel, grid=(count // TILE,), in_specs=[pl.BlockSpec(...  8.09 us
    ppermute x2, waiting for transfers between devices, around(): left = lax.ppermute(block, axis, ring(axis, 1))  7.71 us
    pallas_call x1, Pallas kernels, halo_call(): pl.pallas_call(halo_kernel, in_specs=[smem, smem, vmem, vmem, vmem, vmem,...  7.21 us
    pallas_call x1, Pallas kernels, own_call(): pl.pallas_call(own_kernel, in_specs=[pl.BlockSpec(memory_space=pltpu.SMEM...  6.42 us
    unnamed x28, local copies, waits for them, and re-layouts  5.93 us
  transfers between devices with their start and end apart: 10, of which 7 were waited for; matrix products, arithmetic and copies ran while one was open for 1% of the time, Pallas kernels for 10%

profile of v1, /device:TPU:1, one launch (start us, length us, event | category | flops | bytes accessed | tf_op | source)
XLA Modules:
  0.0 143.1 jit_solution(1004000682799202949)
XLA Ops:
  1.4 1.8 %copy-done = bf16[1024,1408]{1,0:T(8,128)(2,1)S(1)} copy-done((bf16[1024,1408]{1,0:T(8,128)(2,1)S(1)}, bf16[1024,1408]{1,0:T(8,128)(2,1)}, u32[]{:S(2)}) %copy-start) | copy-done | bytes 2883608
  6.1 8.1 %qkv.1 = (bf16[4,128,1024]{2,1,0:T(8,128)(2,1)S(1)}, bf16[2,4,88,1024]{3,2,1,0:T(8,128)(2,1)S(1)}) custom-call(s32[1,2]{1,0:T(1,128)S(1)} %copy-done.5, bf16[176,192]{1,0:T(8,128)(2,1)S(1)} %copy-done.6, s32[1,1024]{1,0:T(1,128)S(1)} %bitcast.7, s32[1,1024]{1,0:T(1,128)S(1)} %bitcast.8, s32[1,1024]{1,0:T(1,128)S(1)} %bitcast.6, ...), custom_call_target="tpu_custom_call" | custom-call | flops 3045064704 | bytes 10485760 | tf_op jit(solution)/shard_map/qkv/pallas_call | solution.py:106
  14.2 4.5 %collective-permute-start = (bf16[2,4,88,1024]{3,2,1,0:T(8,128)(2,1)S(1)}, bf16[2,4,88,1024]{3,2,1,0:T(8,128)(2,1)S(1)}, u32[]{:S(2)}, u32[]{:S(2)}) collective-permute-start(bf16[2,4,88,1024]{3,2,1,0:T(8,128)(2,1)S(1)} %get-tuple-element.10.kv_ref), channel_id=1, source_target_pairs={{0,4},{4,8},{8,12},{12,16},{16,20},{20,24},{24,28},{28,32},{32,36}... | collective-permute-start | bytes 4325384 | tf_op jit(solution)/shard_map/ppermute | solution.py:379
  18.8 2.0 %collective-permute-start.1 = (bf16[2,4,88,1024]{3,2,1,0:T(8,128)(2,1)S(1)}, bf16[2,4,88,1024]{3,2,1,0:T(8,128)(2,1)S(1)}, u32[]{:S(2)}, u32[]{:S(2)}) collective-permute-start(bf16[2,4,88,1024]{3,2,1,0:T(8,128)(2,1)S(1)} %get-tuple-element.10.kv_ref), channel_id=1, source_target_pairs={{4,0},{8,4},{12,8},{16,12},{20,16},{24,20},{28,24},{32,28},{36,32}... | collective-permute-start | bytes 4325384 | tf_op jit(solution)/shard_map/ppermute | solution.py:380
  20.8 1.3 collective-permute-start.6
  22.1 1.5 %collective-permute-start.7 = (bf16[352,1408]{1,0:T(8,128)(2,1)S(1)}, bf16[352,1408]{1,0:T(8,128)(2,1)S(1)}, u32[]{:S(2)}, u32[]{:S(2)}) collective-permute-start(bf16[352,1408]{1,0:T(8,128)(2,1)S(1)} %copy-done.13), channel_id=1, source_target_pairs={{0,3},{1,0},{2,1},{3,2},{4,7},{5,4},{6,5},{7,6},{8,11},{9,8},{10,9... | collective-permute-start | bytes 2973704 | tf_op jit(solution)/shard_map/ppermute | solution.py:355
  23.6 6.4 %own_keys.1 = (f32[4,96,1024]{2,1,0:T(8,128)S(1)}, f32[8,1024]{1,0:T(8,128)S(1)}) custom-call(s32[1,1024]{1,0:T(1,128)S(1)} %bitcast.9, s32[1,1024]{1,0:T(1,128)S(1)} %bitcast.10, bf16[4,128,1024]{2,1,0:T(8,128)(2,1)S(1)} %get-tuple-element.9.q_ref, bf16[2,4,88,1024]{3,2,1,0:T(8,128)(2,1)S(1)} %get-tuple-element.10.kv_ref), custom_call_target="tpu_custom_call" | custom-call | flops 8589934592 | bytes 8388608 | tf_op jit(solution)/shard_map/own_keys/pallas_call | solution.py:184
  30.0 1.2 copy-done.7
  31.2 3.5 %collective-permute-done.before_ref = bf16[2,4,88,1024]{3,2,1,0:T(8,128)(2,1)S(1)} collective-permute-done((bf16[2,4,88,1024]{3,2,1,0:T(8,128)(2,1)S(1)}, bf16[2,4,88,1024]{3,2,1,0:T(8,128)(2,1)S(1)}, u32[]{:S(2)}, u32[]{:S(2)}) %collective-permute-start) | collective-permute-done | bytes 1441824 | tf_op jit(solution)/shard_map/ppermute | solution.py:379
  34.7 4.7 %collective-permute-done.1.after_ref = bf16[2,4,88,1024]{3,2,1,0:T(8,128)(2,1)S(1)} collective-permute-done((bf16[2,4,88,1024]{3,2,1,0:T(8,128)(2,1)S(1)}, bf16[2,4,88,1024]{3,2,1,0:T(8,128)(2,1)S(1)}, u32[]{:S(2)}, u32[]{:S(2)}) %collective-permute-start.1) | collective-permute-done | bytes 1441824 | tf_op jit(solution)/shard_map/ppermute | solution.py:380
  39.4 7.2 %halo_keys.1.own_ref = bf16[352,1024]{1,0:T(8,128)(2,1)S(1)} custom-call(s32[1,2]{1,0:T(1,128)S(1)} %copy-done.5, s32[1,1024]{1,0:T(1,128)S(1)} %bitcast.11, bf16[4,128,1024]{2,1,0:T(8,128)(2,1)S(1)} %get-tuple-element.9.q_ref, f32[4,96,1024]{2,1,0:T(8,128)} %copy-done.7, f32[8,1024]{1,0:T(8,128)S(1)} %get-tuple-element.12.top_in, ...), custom_call_target="tpu_custom_call" | custom-call | flops 8589934592 | bytes 8388608 | tf_op jit(solution)/shard_map/halo_keys/pallas_call | solution.py:250
  46.6 1.4 collective-permute-start.2
  48.0 1.5 %collective-permute-start.3 = (bf16[352,1024]{1,0:T(8,128)(2,1)S(1)}, bf16[352,1024]{1,0:T(8,128)(2,1)S(1)}, u32[]{:S(2)}, u32[]{:S(2)}) collective-permute-start(bf16[352,1024]{1,0:T(8,128)(2,1)S(1)} %halo_keys.1.own_ref), channel_id=1, source_target_pairs={{0,3},{1,0},{2,1},{3,2},{4,7},{5,4},{6,5},{7,6},{8,11},{9,8},{10,9... | collective-permute-start | bytes 2162696 | tf_op jit(solution)/shard_map/ppermute | solution.py:355
  49.7 2.7 %collective-permute-start.9 = (bf16[176,1408]{1,0:T(8,128)(2,1)S(1)}, bf16[176,1408]{1,0:T(8,128)(2,1)S(1)}, u32[]{:S(2)}, u32[]{:S(2)}) collective-permute-start(bf16[176,1408]{1,0:T(8,128)(2,1)S(1)} %slice.19), channel_id=1, source_target_pairs={{0,3},{1,0},{2,1},{3,2},{4,7},{5,4},{6,5},{7,6},{8,11},{9,8},{10,9... | collective-permute-start | bytes 1486856 | tf_op jit(solution)/shard_map/ppermute | solution.py:359
  52.5 7.7 %collective-permute-done.2.left_ref = bf16[352,1024]{1,0:T(8,128)(2,1)S(1)} collective-permute-done((bf16[352,1024]{1,0:T(8,128)(2,1)S(1)}, bf16[352,1024]{1,0:T(8,128)(2,1)S(1)}, u32[]{:S(2)}, u32[]{:S(2)}) %collective-permute-start.2) | collective-permute-done | bytes 720928 | tf_op jit(solution)/shard_map/ppermute | solution.py:354
  60.2 1.6 %collective-permute-start.4 = (bf16[176,1024]{1,0:T(8,128)(2,1)S(1)}, bf16[176,1024]{1,0:T(8,128)(2,1)S(1)}, u32[]{:S(2)}, u32[]{:S(2)}) collective-permute-start(bf16[176,1024]{1,0:T(8,128)(2,1)S(1)} %slice.16), channel_id=1, source_target_pairs={{0,1},{1,2},{2,3},{3,0},{4,5},{5,6},{6,7},{7,4},{8,9},{9,10},{10,1... | collective-permute-start | bytes 1081352 | tf_op jit(solution)/shard_map/ppermute | solution.py:358
  61.9 2.6 %collective-permute-start.5 = (bf16[176,1024]{1,0:T(8,128)(2,1)S(1)}, bf16[176,1024]{1,0:T(8,128)(2,1)S(1)}, u32[]{:S(2)}, u32[]{:S(2)}) collective-permute-start(bf16[176,1024]{1,0:T(8,128)(2,1)S(1)} %slice.17), channel_id=1, source_target_pairs={{0,3},{1,0},{2,1},{3,2},{4,7},{5,4},{6,5},{7,6},{8,11},{9,8},{10,9... | collective-permute-start | bytes 1081352 | tf_op jit(solution)/shard_map/ppermute | solution.py:359
  65.1 5.7 %collective-permute-done.8 = bf16[176,1408]{1,0:T(8,128)(2,1)S(1)} collective-permute-done((bf16[176,1408]{1,0:T(8,128)(2,1)S(1)}, bf16[176,1408]{1,0:T(8,128)(2,1)S(1)}, u32[]{:S(2)}, u32[]{:S(2)}) %collective-permute-start.8) | collective-permute-done | bytes 495648 | tf_op jit(solution)/shard_map/ppermute | solution.py:358
  70.8 1.2 collective-permute-done.9
  73.0 5.5 %collective-permute-done.4 = bf16[176,1024]{1,0:T(8,128)(2,1)S(1)} collective-permute-done((bf16[176,1024]{1,0:T(8,128)(2,1)S(1)}, bf16[176,1024]{1,0:T(8,128)(2,1)S(1)}, u32[]{:S(2)}, u32[]{:S(2)}) %collective-permute-start.4) | collective-permute-done | bytes 360480 | tf_op jit(solution)/shard_map/ppermute | solution.py:358
  78.5 1.2 collective-permute-done.5
  80.6 12.9 %project.1 = bf16[512,640]{1,0:T(8,128)(2,1)} custom-call(s32[1,256]{1,0:T(1,128)} %bitcast.14, s32[1,256]{1,0:T(1,128)} %bitcast.15, bf16[1024,1408]{1,0:T(8,128)(2,1)} %x_ref.3, bf16[352,1024]{1,0:T(8,128)(2,1)} %copy-done.1, bf16[352,1024]{1,0:T(8,128)(2,1)} %copy-done.10, bf16[352,1024]{1,0:T(8,128)(2,1)} %copy-done.11, ...), custom_call_target="tpu_custom_call" | custom-call | flops 6442450944 | bytes 18874368 | tf_op jit(solution)/shard_map/project/pallas_call | solution.py:307
  93.5 47.5 %all_to_all.5 = bf16[64,8,640]{2,1,0:T(8,128)(2,1)} all-to-all(bf16[64,8,640]{2,1,0:T(8,128)(2,1)} %bitcast.13), channel_id=1, replica_groups=mesh['req'=64,'tp'=4] {'req'}, dimensions={0} | all-to-all | bytes 1310720 | tf_op jit(solution)/shard_map/all_to_all | solution.py:388
  141.0 2.1 %place.1 = bf16[256,512]{1,0:T(8,128)(2,1)} custom-call(bf16[512,640]{1,0:T(8,128)(2,1)} %bitcast.12), custom_call_target="tpu_custom_call" | custom-call | tf_op jit(solution)/shard_map/place/pallas_call | solution.py:338
  (39 shorter events, 7.1 us)
Async XLA Ops:
  1.4 1.8 %copy-start = (bf16[1024,1408]{1,0:T(8,128)(2,1)S(1)}, bf16[1024,1408]{1,0:T(8,128)(2,1)}, u32[]{:S(2)}) copy-start(bf16[1024,1408]{1,0:T(8,128)(2,1)} %x_ref.3) | copy-start | bytes 8650756
  3.2 0.7 copy-start.2
  3.9 0.7 copy-start.3
  4.6 0.7 copy-start.5
  5.2 0.9 copy-start.6
  6.1 14.6 %copy-start.13 = (bf16[352,1408]{1,0:T(8,128)(2,1)S(1)}, bf16[352,1408]{1,0:T(8,128)(2,1)}, u32[]{:S(2)}) copy-start(bf16[352,1408]{1,0:T(8,128)(2,1)} %w_own.1) | copy-start | bytes 2973700
  6.1 17.5 %copy-start.4 = (s32[1024]{0:T(1024)S(1)}, s32[1024]{0:T(1024)}, u32[]{:S(2)}) copy-start(s32[1024]{0:T(1024)} %param.13) | copy-start | bytes 12292
  14.2 20.5 %collective-permute-start = (bf16[2,4,88,1024]{3,2,1,0:T(8,128)(2,1)S(1)}, bf16[2,4,88,1024]{3,2,1,0:T(8,128)(2,1)S(1)}, u32[]{:S(2)}, u32[]{:S(2)}) collective-permute-start(bf16[2,4,88,1024]{3,2,1,0:T(8,128)(2,1)S(1)} %get-tuple-element.10.kv_ref), channel_id=1, source_target_pairs={{0,4},{4,8},{8,12},{12,16},{16,20},{20,24},{24,28},{28,32},{32,36}... | collective-permute-start | bytes 4325384 | tf_op jit(solution)/shard_map/ppermute | solution.py:379
  18.8 20.6 %collective-permute-start.1 = (bf16[2,4,88,1024]{3,2,1,0:T(8,128)(2,1)S(1)}, bf16[2,4,88,1024]{3,2,1,0:T(8,128)(2,1)S(1)}, u32[]{:S(2)}, u32[]{:S(2)}) collective-permute-start(bf16[2,4,88,1024]{3,2,1,0:T(8,128)(2,1)S(1)} %get-tuple-element.10.kv_ref), channel_id=1, source_target_pairs={{4,0},{8,4},{12,8},{16,12},{20,16},{24,20},{28,24},{32,28},{36,32}... | collective-permute-start | bytes 4325384 | tf_op jit(solution)/shard_map/ppermute | solution.py:380
  20.8 28.7 %collective-permute-start.6 = (bf16[352,1408]{1,0:T(8,128)(2,1)S(1)}, bf16[352,1408]{1,0:T(8,128)(2,1)S(1)}, u32[]{:S(2)}, u32[]{:S(2)}) collective-permute-start(bf16[352,1408]{1,0:T(8,128)(2,1)S(1)} %copy-done.13), channel_id=1, source_target_pairs={{0,1},{1,2},{2,3},{3,0},{4,5},{5,6},{6,7},{7,4},{8,9},{9,10},{10,1... | collective-permute-start | bytes 2973704 | tf_op jit(solution)/shard_map/ppermute | solution.py:354
  22.1 27.6 %collective-permute-start.7 = (bf16[352,1408]{1,0:T(8,128)(2,1)S(1)}, bf16[352,1408]{1,0:T(8,128)(2,1)S(1)}, u32[]{:S(2)}, u32[]{:S(2)}) collective-permute-start(bf16[352,1408]{1,0:T(8,128)(2,1)S(1)} %copy-done.13), channel_id=1, source_target_pairs={{0,3},{1,0},{2,1},{3,2},{4,7},{5,4},{6,5},{7,6},{8,11},{9,8},{10,9... | collective-permute-start | bytes 2973704 | tf_op jit(solution)/shard_map/ppermute | solution.py:355
  30.0 1.2 copy-start.7
  46.6 15.3 %copy-start.1 = (bf16[352,1024]{1,0:T(8,128)(2,1)}, bf16[352,1024]{1,0:T(8,128)(2,1)S(1)}, u32[]{:S(2)}) copy-start(bf16[352,1024]{1,0:T(8,128)(2,1)S(1)} %halo_keys.1.own_ref) | copy-start | bytes 2162692
  46.6 17.9 %copy-start.12 = (s32[256]{0:T(256)S(1)}, s32[256]{0:T(256)}, u32[]{:S(2)}) copy-start(s32[256]{0:T(256)} %param.16) | copy-start | bytes 3076
  46.6 13.5 %collective-permute-start.2 = (bf16[352,1024]{1,0:T(8,128)(2,1)S(1)}, bf16[352,1024]{1,0:T(8,128)(2,1)S(1)}, u32[]{:S(2)}, u32[]{:S(2)}) collective-permute-start(bf16[352,1024]{1,0:T(8,128)(2,1)S(1)} %halo_keys.1.own_ref), channel_id=1, source_target_pairs={{0,1},{1,2},{2,3},{3,0},{4,5},{5,6},{6,7},{7,4},{8,9},{9,10},{10,1... | collective-permute-start | bytes 2162696 | tf_op jit(solution)/shard_map/ppermute | solution.py:354
  48.0 13.8 %collective-permute-start.3 = (bf16[352,1024]{1,0:T(8,128)(2,1)S(1)}, bf16[352,1024]{1,0:T(8,128)(2,1)S(1)}, u32[]{:S(2)}, u32[]{:S(2)}) collective-permute-start(bf16[352,1024]{1,0:T(8,128)(2,1)S(1)} %halo_keys.1.own_ref), channel_id=1, source_target_pairs={{0,3},{1,0},{2,1},{3,2},{4,7},{5,4},{6,5},{7,6},{8,11},{9,8},{10,9... | collective-permute-start | bytes 2162696 | tf_op jit(solution)/shard_map/ppermute | solution.py:355
  49.5 12.3 %copy-start.8 = (bf16[352,1408]{1,0:T(8,128)(2,1)}, bf16[352,1408]{1,0:T(8,128)(2,1)S(1)}, u32[]{:S(2)}) copy-start(bf16[352,1408]{1,0:T(8,128)(2,1)S(1)} %collective-permute-done.6.w_left) | copy-start | bytes 2973700
  49.6 21.2 %collective-permute-start.8 = (bf16[176,1408]{1,0:T(8,128)(2,1)S(1)}, bf16[176,1408]{1,0:T(8,128)(2,1)S(1)}, u32[]{:S(2)}, u32[]{:S(2)}) collective-permute-start(bf16[176,1408]{1,0:T(8,128)(2,1)S(1)} %slice.18), channel_id=1, source_target_pairs={{0,1},{1,2},{2,3},{3,0},{4,5},{5,6},{6,7},{7,4},{8,9},{9,10},{10,1... | collective-permute-start | bytes 1486856 | tf_op jit(solution)/shard_map/ppermute | solution.py:358
  49.7 23.3 %copy-start.9 = (bf16[352,1408]{1,0:T(8,128)(2,1)}, bf16[352,1408]{1,0:T(8,128)(2,1)S(1)}, u32[]{:S(2)}) copy-start(bf16[352,1408]{1,0:T(8,128)(2,1)S(1)} %collective-permute-done.7.w_right) | copy-start | bytes 2973700
  49.7 22.2 %collective-permute-start.9 = (bf16[176,1408]{1,0:T(8,128)(2,1)S(1)}, bf16[176,1408]{1,0:T(8,128)(2,1)S(1)}, u32[]{:S(2)}, u32[]{:S(2)}) collective-permute-start(bf16[176,1408]{1,0:T(8,128)(2,1)S(1)} %slice.19), channel_id=1, source_target_pairs={{0,3},{1,0},{2,1},{3,2},{4,7},{5,4},{6,5},{7,6},{8,11},{9,8},{10,9... | collective-permute-start | bytes 1486856 | tf_op jit(solution)/shard_map/ppermute | solution.py:359
  60.2 12.8 %copy-start.10 = (bf16[352,1024]{1,0:T(8,128)(2,1)}, bf16[352,1024]{1,0:T(8,128)(2,1)S(1)}, u32[]{:S(2)}) copy-start(bf16[352,1024]{1,0:T(8,128)(2,1)S(1)} %collective-permute-done.2.left_ref) | copy-start | bytes 2162692
  60.2 18.3 %collective-permute-start.4 = (bf16[176,1024]{1,0:T(8,128)(2,1)S(1)}, bf16[176,1024]{1,0:T(8,128)(2,1)S(1)}, u32[]{:S(2)}, u32[]{:S(2)}) collective-permute-start(bf16[176,1024]{1,0:T(8,128)(2,1)S(1)} %slice.16), channel_id=1, source_target_pairs={{0,1},{1,2},{2,3},{3,0},{4,5},{5,6},{6,7},{7,4},{8,9},{9,10},{10,1... | collective-permute-start | bytes 1081352 | tf_op jit(solution)/shard_map/ppermute | solution.py:358
  61.8 18.8 %copy-start.11 = (bf16[352,1024]{1,0:T(8,128)(2,1)}, bf16[352,1024]{1,0:T(8,128)(2,1)S(1)}, u32[]{:S(2)}) copy-start(bf16[352,1024]{1,0:T(8,128)(2,1)S(1)} %collective-permute-done.3.right_ref) | copy-start | bytes 2162692
  61.9 17.8 %collective-permute-start.5 = (bf16[176,1024]{1,0:T(8,128)(2,1)S(1)}, bf16[176,1024]{1,0:T(8,128)(2,1)S(1)}, u32[]{:S(2)}, u32[]{:S(2)}) collective-permute-start(bf16[176,1024]{1,0:T(8,128)(2,1)S(1)} %slice.17), channel_id=1, source_target_pairs={{0,3},{1,0},{2,1},{3,2},{4,7},{5,4},{6,5},{7,6},{8,11},{9,8},{10,9... | collective-permute-start | bytes 1081352 | tf_op jit(solution)/shard_map/ppermute | solution.py:359

commit v2 on v1

--- a/solution.py
+++ b/solution.py
@@ -15,7 +15,8 @@
 VAUG = 96
 BIG = 1e30
 TILE = 256
-BLK = 256
+QB = 512
+KB = 256
 F32 = jnp.float32
 BF16 = jnp.bfloat16
 NT = (((1,), (1,)), ((), ()))
@@ -60,7 +61,7 @@
     x = x_ref[...].astype(F32)
     centred = x - jnp.mean(x, axis=1, keepdims=True)
     variance = jnp.mean(centred * centred, axis=1, keepdims=True)
-    normed = (centred * lax.rsqrt(variance + 1e-6) * gain_ref[...] + bias_ref[...]).astype(BF16)
+    normed = (centred * lax.rsqrt(variance + 1e-6) * gain_ref[...].reshape(1, -1) + bias_ref[...].reshape(1, -1)).astype(BF16)
 
     below = seg_counts(seg_ref[...])
     seg = segt_ref[...]
@@ -113,8 +114,8 @@
             pl.BlockSpec((1, TILE), lambda i: (0, i)),
             pl.BlockSpec((1, TILE), lambda i: (0, i)),
             pl.BlockSpec((TILE, width), lambda i: (i, 0)),
-            whole(1, width),
-            whole(1, width),
+            whole(width),
+            whole(width),
             whole(3, local, width),
         ],
         out_specs=[
@@ -125,57 +126,64 @@
             jax.ShapeDtypeStruct((heads, AUG, count), BF16),
             jax.ShapeDtypeStruct((2, heads, HD, count), BF16),
         ],
-        compiler_params=pltpu.CompilerParams(vmem_limit_bytes=48 << 20),
+        compiler_params=pltpu.CompilerParams(vmem_limit_bytes=30 << 20),
         cost_estimate=pl.CostEstimate(flops=6 * count * width * local, bytes_accessed=10 << 20, transcendentals=0),
         name="qkv",
-    )(plan, table, seg, seg, sides, patches, gain, bias, w_qkv)
+    )(*[pltpu.with_memory_space_constraint(v, pltpu.HBM) for v in (plan, table, seg, seg, sides, patches, gain, bias, w_qkv)])
 
 
 def prepare_block(kv_ref, label, keys, values, base):
     heads = keys.shape[0]
     rows = label_rows(label)
     extra = VAUG - HD
-    ones = (lax.broadcasted_iota(jnp.int32, (extra, BLK), 0) == 0).astype(F32)
+    ones = (lax.broadcasted_iota(jnp.int32, (extra, KB), 0) == 0).astype(F32)
     for h in range(heads):
-        block = jnp.concatenate([kv_ref[0, h, :, pl.ds(base, BLK)].astype(F32), rows], axis=0)
-        keys[h, pl.ds(base, BLK), :] = block.T.astype(BF16)
-        block = jnp.concatenate([kv_ref[1, h, :, pl.ds(base, BLK)].astype(F32), ones], axis=0)
-        values[h, :, pl.ds(base, BLK)] = block.astype(BF16)
+        block = jnp.concatenate([kv_ref[0, h, :, pl.ds(base, KB)].astype(F32), rows], axis=0)
+        keys[h, pl.ds(base, KB), :] = block.astype(BF16).T
+        block = jnp.concatenate([kv_ref[1, h, :, pl.ds(base, KB)].astype(F32), ones], axis=0)
+        values[h, :, pl.ds(base, KB)] = block.astype(BF16)
 
 
 def attend(q_ref, keys, values, acc, top, q_base, k_base):
     heads = keys.shape[0]
+    span = pl.ds(q_base, QB)
+    old = [top[h : h + 1, span] for h in range(heads)]
+    scores = [
+        lax.dot_general(keys[h, pl.ds(k_base, KB), :], q_ref[h, :, span], NN, preferred_element_type=F32)
+        for h in range(heads)
+    ]
+    new = [jnp.maximum(old[h], jnp.max(scores[h], axis=0, keepdims=True)) for h in range(heads)]
+    weights = [jnp.exp2(scores[h] - new[h]).astype(BF16) for h in range(heads)]
+    parts = [
+        lax.dot_general(values[h, :, pl.ds(k_base, KB)], weights[h], NN, preferred_element_type=F32)
+        for h in range(heads)
+    ]
+    sums = [acc[h, :, span] * jnp.exp2(old[h] - new[h]) + parts[h] for h in range(heads)]
     for h in range(heads):
-        query = q_ref[h, :, pl.ds(q_base, BLK)]
-        scores = lax.dot_general(keys[h, pl.ds(k_base, BLK), :], query, NN, preferred_element_type=F32)
-        old = top[h : h + 1, pl.ds(q_base, BLK)]
-        new = jnp.maximum(old, jnp.max(scores, axis=0, keepdims=True))
-        weights = jnp.exp2(scores - new).astype(BF16)
-        part = lax.dot_general(values[h, :, pl.ds(k_base, BLK)], weights, NN, preferred_element_type=F32)
-        acc[h, :, pl.ds(q_base, BLK)] = acc[h, :, pl.ds(q_base, BLK)] * jnp.exp2(old - new) + part
-        top[h : h + 1, pl.ds(q_base, BLK)] = new
+        acc[h, :, span] = sums[h]
+        top[h : h + 1, span] = new[h]
 
 
 def own_kernel(sseg_ref, seg_ref, q_ref, kv_ref, acc_ref, top_ref, keys, values):
     count = seg_ref.shape[1]
     seg = seg_ref[...]
-    for b in range(count // BLK):
-        prepare_block(kv_ref, seg[:, b * BLK : (b + 1) * BLK], keys, values, b * BLK)
+    for b in range(count // KB):
+        prepare_block(kv_ref, seg[:, b * KB : (b + 1) * KB], keys, values, b * KB)
     acc_ref[...] = jnp.zeros_like(acc_ref)
     top_ref[...] = jnp.full_like(top_ref, -BIG)
 
     def block(b, carry):
-        q_base = pl.multiple_of(b * BLK, BLK)
+        q_base = pl.multiple_of(b * QB, QB)
         low = jnp.sum((seg < sseg_ref[0, q_base]).astype(jnp.int32))
-        high = jnp.sum((seg <= sseg_ref[0, q_base + BLK - 1]).astype(jnp.int32))
+        high = jnp.sum((seg <= sseg_ref[0, q_base + QB - 1]).astype(jnp.int32))
 
         def inner(k, c):
-            attend(q_ref, keys, values, acc_ref, top_ref, q_base, pl.multiple_of(k * BLK, BLK))
+            attend(q_ref, keys, values, acc_ref, top_ref, q_base, pl.multiple_of(k * KB, KB))
             return c
 
-        return lax.fori_loop(low // BLK, (high + BLK - 1) // BLK, inner, carry)
-
-    lax.fori_loop(0, count // BLK, block, 0)
+        return lax.fori_loop(low // KB, (high + KB - 1) // KB, inner, carry)
+
+    lax.fori_loop(0, count // QB, block, 0)
 
 
 def own_call(seg, q, kv):
@@ -190,7 +198,7 @@
             jax.ShapeDtypeStruct((8, count), F32),
         ],
         scratch_shapes=[pltpu.VMEM((heads, count, AUG), BF16), pltpu.VMEM((heads, VAUG, count), BF16)],
-        compiler_params=pltpu.CompilerParams(vmem_limit_bytes=48 << 20),
+        compiler_params=pltpu.CompilerParams(vmem_limit_bytes=20 << 20),
         cost_estimate=pl.CostEstimate(flops=8 << 30, bytes_accessed=8 << 20, transcendentals=4 << 20),
         name="own_keys",
     )(seg, seg, q, kv)
@@ -202,15 +210,15 @@
     top[...] = top_in[...]
     lead, trail = plan_ref[0, 0], plan_ref[0, 1]
     last = sseg_ref[0, count - 1]
-    token = lax.broadcasted_iota(jnp.int32, (1, BLK), 1)
+    token = lax.broadcasted_iota(jnp.int32, (1, KB), 1)
 
     def before_block(k, carry):
-        base = pl.multiple_of(k * BLK, BLK)
+        base = pl.multiple_of(k * KB, KB)
         label = jnp.where(token + base >= count - lead, 0, -1)
         prepare_block(before_ref, label, keys, values, base)
 
         def inner(b, c):
-            q_base = pl.multiple_of(b * BLK, BLK)
+            q_base = pl.multiple_of(b * QB, QB)
 
             @pl.when(sseg_ref[0, q_base] == 0)
             def _():
@@ -218,27 +226,27 @@
 
             return c
 
-        return lax.fori_loop(0, count // BLK, inner, carry)
-
-    lax.fori_loop((count - lead) // BLK, count // BLK, before_block, 0)
+        return lax.fori_loop(0, count // QB, inner, carry)
+
+    lax.fori_loop((count - lead) // KB, count // KB, before_block, 0)
 
     def after_block(k, carry):
-        base = pl.multiple_of(k * BLK, BLK)
+        base = pl.multiple_of(k * KB, KB)
         label = jnp.where(token + base < trail, last, -1)
         prepare_block(after_ref, label, keys, values, base)
 
         def inner(b, c):
-            q_base = pl.multiple_of(b * BLK, BLK)
-
-            @pl.when(sseg_ref[0, q_base + BLK - 1] == last)
+            q_base = pl.multiple_of(b * QB, QB)
+
+            @pl.when(sseg_ref[0, q_base + QB - 1] == last)
             def _():
                 attend(q_ref, keys, values, acc, top, q_base, base)
 
             return c
 
-        return lax.fori_loop(0, count // BLK, inner, carry)
-
-    lax.fori_loop(0, (trail + BLK - 1) // BLK, after_block, 0)
+        return lax.fori_loop(0, count // QB, inner, carry)
+
+    lax.fori_loop(0, (trail + KB - 1) // KB, after_block, 0)
     for h in range(heads):
         out_ref[pl.ds(h * HD, HD), :] = (acc[h, :HD, :] / acc[h, HD : HD + 1, :]).astype(BF16)
 
@@ -258,70 +266,78 @@
             pltpu.VMEM((heads, count, AUG), BF16),
             pltpu.VMEM((heads, VAUG, count), BF16),
         ],
-        compiler_params=pltpu.CompilerParams(vmem_limit_bytes=48 << 20),
+        compiler_params=pltpu.CompilerParams(vmem_limit_bytes=20 << 20),
         cost_estimate=pl.CostEstimate(flops=8 << 30, bytes_accessed=8 << 20, transcendentals=4 << 20),
         name="halo_keys",
     )(plan, seg, q, acc, top, before, after)
 
 
-def out_kernel(slot_ref, dest_ref, x_ref, own_ref, left_ref, right_ref, far_ref, w_own, w_left, w_right, w_far, proj_hbm, send_ref, mixed, proj, sem):
-    step = pl.program_id(0)
-    width = x_ref.shape[1]
-    copy = pltpu.make_async_copy(proj_hbm, proj, sem)
-
-    @pl.when(step == 0)
-    def _():
-        copy.start()
-
-    total = x_ref[...].astype(F32)
-    for h_ref, w_ref in ((own_ref, w_own), (left_ref, w_left), (right_ref, w_right), (far_ref, w_far)):
-        total += lax.dot_general(h_ref[...], w_ref[...], TN, preferred_element_type=F32)
+def gather_kernel(parts, base_ref, *refs):
+    out_ref = refs[-1]
+    for start in range(0, out_ref.shape[0], TILE):
+        span = slice(start, start + TILE)
+        total = base_ref[span].astype(F32)
+        for h_ref, w_ref in zip(refs[:parts], refs[parts : 2 * parts]):
+            total += lax.dot_general(h_ref[:, span], w_ref[...], TN, preferred_element_type=F32)
+        out_ref[span] = total
+
+
+def gather_call(base, heads_parts, w_parts):
+    vmem = pl.BlockSpec(memory_space=pltpu.VMEM)
+    parts = len(heads_parts)
+    flops = 2 * base.shape[0] * base.shape[1] * sum(h.shape[0] for h in heads_parts)
+    return pl.pallas_call(
+        functools.partial(gather_kernel, parts),
+        in_specs=[vmem] * (1 + 2 * parts),
+        out_specs=vmem,
+        out_shape=jax.ShapeDtypeStruct(base.shape, F32),
+        compiler_params=pltpu.CompilerParams(vmem_limit_bytes=16 << 20),
+        cost_estimate=pl.CostEstimate(flops=flops, bytes_accessed=4 << 20, transcendentals=0),
+        name="output",
+    )(base, *heads_parts, *w_parts)
+
+
+def project_kernel(parts, slot_ref, dest_ref, base_ref, *refs):
+    proj, send_ref, mixed = refs[2 * parts :]
+    count, width = base_ref.shape
     chunks = width // 128
-    base = pl.multiple_of(step * TILE, TILE)
-    for c in range(chunks):
-        mixed[c, pl.ds(base, TILE), :] = total[:, c * 128 : (c + 1) * 128]
-
-    @pl.when(step == pl.num_programs(0) - 1)
-    def _():
-        copy.wait()
-        rows = mixed.shape[1] // 4
-        result = jnp.zeros((rows, proj.shape[1]), F32)
-        for j in range(4):
-            part = jnp.concatenate([mixed[c, pl.ds(j, rows, stride=4), :] for c in range(chunks)], axis=1).astype(BF16)
-            result += lax.dot_general(part, proj[j * width : (j + 1) * width, :], NN, preferred_element_type=F32)
-        slots = lax.broadcasted_iota(jnp.int32, (send_ref.shape[0], rows), 0)
-        pick = (slots == slot_ref[...]).astype(F32)
-        cols = proj.shape[1]
-        send_ref[:, :cols] = lax.dot_general(
-            pick.astype(BF16), result.astype(BF16), NN, preferred_element_type=F32
-        ).astype(BF16)
-        dest = jnp.sum(pick * dest_ref[...].astype(F32), axis=1, keepdims=True)
-        send_ref[:, cols:] = jnp.broadcast_to(dest, (send_ref.shape[0], 128)).astype(BF16)
-
-
-def out_call(slot, dest, patches, heads_parts, w_parts, w_proj, slots):
-    count, width = patches.shape
-    local = heads_parts[0].shape[0]
+    for start in range(0, count, TILE):
+        span = slice(start, start + TILE)
+        total = base_ref[span]
+        for h_ref, w_ref in zip(refs[:parts], refs[parts : 2 * parts]):
+            total += lax.dot_general(h_ref[:, span], w_ref[...], TN, preferred_element_type=F32)
+        for c in range(chunks):
+            mixed[c, span, :] = total[:, c * 128 : (c + 1) * 128]
+    rows = count // 4
+    result = jnp.zeros((rows, proj.shape[1]), F32)
+    for j in range(4):
+        part = jnp.concatenate([mixed[c, pl.ds(j, rows, stride=4), :] for c in range(chunks)], axis=1).astype(BF16)
+        result += lax.dot_general(part, proj[j * width : (j + 1) * width, :], NN, preferred_element_type=F32)
+    slots = lax.broadcasted_iota(jnp.int32, (send_ref.shape[0], rows), 0)
+    pick = (slots == slot_ref[...]).astype(F32)
+    cols = proj.shape[1]
+    send_ref[:, :cols] = lax.dot_general(
+        pick.astype(BF16), result.astype(BF16), NN, preferred_element_type=F32
+    ).astype(BF16)
+    dest = jnp.sum(pick * dest_ref[...].astype(F32), axis=1, keepdims=True)
+    send_ref[:, cols:] = jnp.broadcast_to(dest, (send_ref.shape[0], 128)).astype(BF16)
+
+
+def project_call(slot, dest, base, heads_parts, w_parts, w_proj, slots):
+    vmem = pl.BlockSpec(memory_space=pltpu.VMEM)
+    parts = len(heads_parts)
+    count, width = base.shape
     cols = w_proj.shape[1]
-    whole = lambda *shape: pl.BlockSpec(shape, lambda i: (0,) * len(shape))
-    return pl.pallas_call(
-        out_kernel,
-        grid=(count // TILE,),
-        in_specs=[whole(*slot.shape), whole(*dest.shape), pl.BlockSpec((TILE, width), lambda i: (i, 0))]
-        + [pl.BlockSpec((local, TILE), lambda i: (0, i))] * 4
-        + [whole(local, width)] * 4
-        + [pl.BlockSpec(memory_space=pl.ANY)],
-        out_specs=whole(slots, cols + 128),
+    return pl.pallas_call(
+        functools.partial(project_kernel, parts),
+        in_specs=[vmem] * (4 + 2 * parts),
+        out_specs=vmem,
         out_shape=jax.ShapeDtypeStruct((slots, cols + 128), BF16),
-        scratch_shapes=[
-            pltpu.VMEM((width // 128, count, 128), F32),
-            pltpu.VMEM(w_proj.shape, BF16),
-            pltpu.SemaphoreType.DMA,
-        ],
-        compiler_params=pltpu.CompilerParams(vmem_limit_bytes=56 << 20),
-        cost_estimate=pl.CostEstimate(flops=6 << 30, bytes_accessed=18 << 20, transcendentals=0),
+        scratch_shapes=[pltpu.VMEM((width // 128, count, 128), F32)],
+        compiler_params=pltpu.CompilerParams(vmem_limit_bytes=24 << 20),
+        cost_estimate=pl.CostEstimate(flops=3 << 30, bytes_accessed=8 << 20, transcendentals=0),
         name="project",
-    )(slot, dest, patches, *heads_parts, *w_parts, w_proj)
+    )(slot, dest, base, *heads_parts, *w_parts, w_proj)
 
 
 def place_kernel(got_ref, out_ref):
@@ -353,14 +369,9 @@
     half = block.shape[0] // 2
     left = lax.ppermute(block, axis, ring(axis, 1))
     right = lax.ppermute(block, axis, ring(axis, -1))
-    far = jnp.concatenate(
-        [
-            lax.ppermute(left[:half], axis, ring(axis, 1)),
-            lax.ppermute(right[half:], axis, ring(axis, -1)),
-        ],
-        axis=0,
-    )
-    return [block, left, right, far]
+    far_top = lax.ppermute(left[:half], axis, ring(axis, 1))
+    far_end = lax.ppermute(right[half:], axis, ring(axis, -1))
+    return left, right, far_top, far_end
 
 
 def on_device(patches, segment_ids, grid_sides, split_plan, owner_dev, dest_row, ln_gain, ln_bias, w_qkv, w_out, w_proj):
@@ -370,20 +381,27 @@
     lanes = 2 * rows_out // peers
     seg = segment_ids.reshape(1, count)
     table = jnp.asarray(rope_table())
-    w_parts = around(w_out, "tp")
+    w_left, w_right, w_top, w_end = around(w_out, "tp")
     q, kv = qkv_call(
-        patches, seg, grid_sides.reshape(1, count), split_plan, ln_gain.reshape(1, width), ln_bias.reshape(1, width), w_qkv, table
+        patches, seg, grid_sides.reshape(1, count), split_plan, ln_gain, ln_bias, w_qkv, table
     )
     up = [(i, i + 1) for i in range(peers - 1)]
     down = [(j, i) for i, j in up]
     before = lax.ppermute(kv, "req", up)
     after = lax.ppermute(kv, "req", down)
     acc, top = own_call(seg, q, kv)
+    before, after, w_left, w_right, w_top, w_end = lax.optimization_barrier(
+        (before, after, w_left, w_right, w_top, w_end)
+    )
     heads_out = halo_call(split_plan, seg, q, acc, top, before, after)
-    heads_parts = around(heads_out, "tp")
+    left, right, far_top, far_end = around(heads_out, "tp")
     within = jnp.arange(rows_out, dtype=jnp.int32) % lanes
     slot = (owner_dev * lanes + within).reshape(1, rows_out)
-    send = out_call(slot, dest_row.reshape(1, rows_out), patches, heads_parts, w_parts, w_proj, peers * lanes)
+    base = gather_call(patches, [heads_out], [w_out])
+    base = gather_call(base, [left, right], [w_left, w_right])
+    send = project_call(
+        slot, dest_row.reshape(1, rows_out), base, [far_top, far_end], [w_top, w_end], w_proj, peers * lanes
+    )
     cols = send.shape[1]
     got = lax.all_to_all(send.reshape(peers, lanes, cols), "req", split_axis=0, concat_axis=0, tiled=True)
     return place_call(got.reshape(peers * lanes, cols), rows_out, w_proj.shape[1])

time: 143 us -> 112 us (0.78)
  blocking collectives: 47.5 us -> 34.8 us
  Pallas kernels: 36.7 us -> 28.5 us
  local copies, waits for them, and re-layouts: 7.45 us -> 0.17 us
  other arithmetic: 2.53 us -> 0.01 us
    ppermute x2, waiting for transfers between devices: 7.71 us -> 21.4 us  [around(): left = lax.ppermute(block, axis, ring(axis, 1))]
    all_to_all x1, blocking collectives: 47.5 us -> 34.8 us  [on_device(): lax.all_to_all(send.reshape(peers, lanes, cols), 'req', split_axis=0, con...]
    ppermute x4, waiting for transfers between devices: 13.6 us -> 2.12 us  [the longest x2 2.11 us: around(): far_top = lax.ppermute(left[:half], axis, ring(axis, 1))]
    unnamed x28 -> x16, local copies, waits for them, and re-layouts: 5.93 us -> 0.05 us
    pallas_call x1 -> x3, Pallas kernels: 12.9 us -> 8.85 us  [the longest x2 5.13 us: gather_call(): pl.pallas_call(functools.partial(gather_kernel, parts), in_specs=[vmem] *...]
    ppermute x1, waiting for transfers between devices: 3.49 us -> 0.79 us  [on_device(): before = lax.ppermute(kv, 'req', up)]
    pallas_call x1, Pallas kernels: 7.21 us -> 4.55 us  [halo_call(): pl.pallas_call(halo_kernel, in_specs=[smem, smem, vmem, vmem, vmem, vmem,...]
    concatenate x2 -> x0, other arithmetic: 1.97 us -> none  [around(): jnp.concatenate([lax.ppermute(left[:half], axis, ring(axis, 1)), lax.pper...]
  transfers between devices with their start and end apart: 10 -> 10, of which waited for: 7 -> 5; matrix products, arithmetic and copies ran while one was open for 1% -> 0% of each run, Pallas kernels for 10% -> 16%
where the time goes in v2:
time: 112 us; the launch traced here: 111 us
  blocking collectives  34.8 us (31%)
  waiting for transfers between devices  29 us (26%)
  Pallas kernels  28.5 us (25%)
  starting transfers between devices  18.9 us (17%)
    all_to_all x1, blocking collectives, on_device(): lax.all_to_all(send.reshape(peers, lanes, cols), 'req', split_axis=0, con...  34.8 us
    ppermute x2, waiting for transfers between devices, around(): left = lax.ppermute(block, axis, ring(axis, 1))  21.4 us
    pallas_call x1, Pallas kernels, qkv_call(): pl.pallas_call(qkv_kernel, grid=(count // TILE,), in_specs=[pl.BlockSpec(...  8.45 us
    pallas_call x2, Pallas kernels, gather_call(): pl.pallas_call(functools.partial(gather_kernel, parts), in_specs=[vmem] *...  5.13 us
    ppermute x1, waiting for transfers between devices, on_device(): after = lax.ppermute(kv, 'req', down)  4.69 us
    ppermute x2, starting transfers between devices, around(): far_end = lax.ppermute(right[half:], axis, ring(axis, -1))  4.64 us
    pallas_call x1, Pallas kernels, halo_call(): pl.pallas_call(halo_kernel, in_specs=[smem, smem, vmem, vmem, vmem, vmem,...  4.55 us
    pallas_call x1, Pallas kernels, own_call(): pl.pallas_call(own_kernel, in_specs=[pl.BlockSpec(memory_space=pltpu.SMEM...  4.51 us
  transfers between devices with their start and end apart: 10, of which 5 were waited for; matrix products, arithmetic and copies ran while one was open for 0% of the time, Pallas kernels for 16%

profile of v2, /device:TPU:1, one launch (start us, length us, event | category | flops | bytes accessed | tf_op | source)
XLA Modules:
  0.0 111.5 jit_solution(16887563808784869033)
XLA Ops:
  0.0 2.1 %collective-permute-start.2 = (bf16[352,1408]{1,0:T(8,128)(2,1)}, bf16[352,1408]{1,0:T(8,128)(2,1)S(1)}, u32[]{:S(2)}, u32[]{:S(2)}) collective-permute-start(bf16[352,1408]{1,0:T(8,128)(2,1)} %refs_1_.1), channel_id=1, source_target_pairs={{0,1},{1,2},{2,3},{3,0},{4,5},{5,6},{6,7},{7,4},{8,9},{9,10},{10,1... | collective-permute-start | bytes 2973704 | tf_op jit(solution)/shard_map/ppermute | solution.py:370
  2.1 1.4 %collective-permute-start.3 = (bf16[352,1408]{1,0:T(8,128)(2,1)}, bf16[352,1408]{1,0:T(8,128)(2,1)S(1)}, u32[]{:S(2)}, u32[]{:S(2)}) collective-permute-start(bf16[352,1408]{1,0:T(8,128)(2,1)} %refs_1_.1), channel_id=1, source_target_pairs={{0,3},{1,0},{2,1},{3,2},{4,7},{5,4},{6,5},{7,6},{8,11},{9,8},{10,9... | collective-permute-start | bytes 2973704 | tf_op jit(solution)/shard_map/ppermute | solution.py:371
  3.6 8.4 %qkv.1 = (bf16[4,128,1024]{2,1,0:T(8,128)(2,1)S(1)}, bf16[2,4,88,1024]{3,2,1,0:T(8,128)(2,1)S(1)}) custom-call(s32[1,2]{1,0:T(1,128)} %plan_ref.3, bf16[176,192]{1,0:T(8,128)(2,1)} %constant.19.clone.table_ref, s32[1,1024]{1,0:T(1,128)} %bitcast.11, s32[1,1024]{1,0:T(1,128)} %bitcast.12, s32[1,1024]{1,0:T(1,128)} %bitcast.17, bf16[1024,1408]{1,0:T(8,128)(2,1)} %base_ref.1, ...), custom_call_target="tpu_custom_call" | custom-call | flops 3045064704 | bytes 10485760 | tf_op jit(solution)/shard_map/qkv/pallas_call | solution.py:107
  12.0 4.2 %collective-permute-start = (bf16[2,4,88,1024]{3,2,1,0:T(8,128)(2,1)S(1)}, bf16[2,4,88,1024]{3,2,1,0:T(8,128)(2,1)S(1)}, u32[]{:S(2)}, u32[]{:S(2)}) collective-permute-start(bf16[2,4,88,1024]{3,2,1,0:T(8,128)(2,1)S(1)} %get-tuple-element.16.kv_ref), channel_id=1, source_target_pairs={{0,4},{4,8},{8,12},{12,16},{16,20},{20,24},{24,28},{28,32},{32,36}... | collective-permute-start | bytes 4325384 | tf_op jit(solution)/shard_map/ppermute | solution.py:390
  16.2 2.0 %collective-permute-start.1 = (bf16[2,4,88,1024]{3,2,1,0:T(8,128)(2,1)S(1)}, bf16[2,4,88,1024]{3,2,1,0:T(8,128)(2,1)S(1)}, u32[]{:S(2)}, u32[]{:S(2)}) collective-permute-start(bf16[2,4,88,1024]{3,2,1,0:T(8,128)(2,1)S(1)} %get-tuple-element.16.kv_ref), channel_id=1, source_target_pairs={{4,0},{8,4},{12,8},{16,12},{20,16},{24,20},{28,24},{32,28},{36,32}... | collective-permute-start | bytes 4325384 | tf_op jit(solution)/shard_map/ppermute | solution.py:391
  18.2 5.1 %collective-permute-done.2.refs_2_ = bf16[352,1408]{1,0:T(8,128)(2,1)S(1)} collective-permute-done((bf16[352,1408]{1,0:T(8,128)(2,1)}, bf16[352,1408]{1,0:T(8,128)(2,1)S(1)}, u32[]{:S(2)}, u32[]{:S(2)}) %collective-permute-start.2) | collective-permute-done | bytes 991264 | tf_op jit(solution)/shard_map/ppermute | solution.py:370
  23.4 1.6 %collective-permute-start.4 = (bf16[176,1408]{1,0:T(8,128)(2,1)S(1)}, bf16[176,1408]{1,0:T(8,128)(2,1)S(1)}, u32[]{:S(2)}, u32[]{:S(2)}) collective-permute-start(bf16[176,1408]{1,0:T(8,128)(2,1)S(1)} %slice.16), channel_id=1, source_target_pairs={{0,1},{1,2},{2,3},{3,0},{4,5},{5,6},{6,7},{7,4},{8,9},{9,10},{10,1... | collective-permute-start | bytes 1486856 | tf_op jit(solution)/shard_map/ppermute | solution.py:372
  25.1 1.7 %collective-permute-start.5 = (bf16[176,1408]{1,0:T(8,128)(2,1)S(1)}, bf16[176,1408]{1,0:T(8,128)(2,1)S(1)}, u32[]{:S(2)}, u32[]{:S(2)}) collective-permute-start(bf16[176,1408]{1,0:T(8,128)(2,1)S(1)} %slice.17), channel_id=1, source_target_pairs={{0,3},{1,0},{2,1},{3,2},{4,7},{5,4},{6,5},{7,6},{8,11},{9,8},{10,9... | collective-permute-start | bytes 1486856 | tf_op jit(solution)/shard_map/ppermute | solution.py:373
  26.8 4.5 %own_keys.1 = (f32[4,96,1024]{2,1,0:T(8,128)S(1)}, f32[8,1024]{1,0:T(8,128)S(1)}) custom-call(s32[1,1024]{1,0:T(1,128)S(1)} %bitcast.13, s32[1,1024]{1,0:T(1,128)S(1)} %bitcast.14, bf16[4,128,1024]{2,1,0:T(8,128)(2,1)S(1)} %get-tuple-element.15.q_ref, bf16[2,4,88,1024]{3,2,1,0:T(8,128)(2,1)S(1)} %get-tuple-element.16.kv_ref), custom_call_target="tpu_custom_call" | custom-call | flops 8589934592 | bytes 8388608 | tf_op jit(solution)/shard_map/own_keys/pallas_call | solution.py:192
  31.4 0.8 collective-permute-done.before_ref
  32.1 4.7 %collective-permute-done.1.after_ref = bf16[2,4,88,1024]{3,2,1,0:T(8,128)(2,1)S(1)} collective-permute-done((bf16[2,4,88,1024]{3,2,1,0:T(8,128)(2,1)S(1)}, bf16[2,4,88,1024]{3,2,1,0:T(8,128)(2,1)S(1)}, u32[]{:S(2)}, u32[]{:S(2)}) %collective-permute-start.1) | collective-permute-done | bytes 1441824 | tf_op jit(solution)/shard_map/ppermute | solution.py:391
  36.9 4.5 %halo_keys.1.refs_0_ = bf16[352,1024]{1,0:T(8,128)(2,1)S(1)} custom-call(s32[1,2]{1,0:T(1,128)S(1)} %copy-done.4, s32[1,1024]{1,0:T(1,128)S(1)} %bitcast.15, bf16[4,128,1024]{2,1,0:T(8,128)(2,1)S(1)} %get-tuple-element.15.q_ref, f32[4,96,1024]{2,1,0:T(8,128)S(1)} %get-tuple-element.17.acc_in, f32[8,1024]{1,0:T(8,128)S(1)} %get-tuple-element.18.top_in, ...), custom_call_target="tpu_custom_call" | custom-call | flops 8589934592 | bytes 8388608 | tf_op jit(solution)/shard_map/halo_keys/pallas_call | solution.py:258
  41.4 0.9 collective-permute-start.6
  42.3 1.9 %collective-permute-start.7 = (bf16[352,1024]{1,0:T(8,128)(2,1)S(1)}, bf16[352,1024]{1,0:T(8,128)(2,1)S(1)}, u32[]{:S(2)}, u32[]{:S(2)}) collective-permute-start(bf16[352,1024]{1,0:T(8,128)(2,1)S(1)} %halo_keys.1.refs_0_), channel_id=1, source_target_pairs={{0,3},{1,0},{2,1},{3,2},{4,7},{5,4},{6,5},{7,6},{8,11},{9,8},{10,9... | collective-permute-start | bytes 2162696 | tf_op jit(solution)/shard_map/ppermute | solution.py:371
  44.2 16.2 %collective-permute-done.6.refs_0_ = bf16[352,1024]{1,0:T(8,128)(2,1)S(1)} collective-permute-done((bf16[352,1024]{1,0:T(8,128)(2,1)S(1)}, bf16[352,1024]{1,0:T(8,128)(2,1)S(1)}, u32[]{:S(2)}, u32[]{:S(2)}) %collective-permute-start.6) | collective-permute-done | bytes 720928 | tf_op jit(solution)/shard_map/ppermute | solution.py:370
  60.4 0.1 collective-permute-start.8
  60.6 2.9 %collective-permute-start.9 = (bf16[176,1024]{1,0:T(8,128)(2,1)S(1)}, bf16[176,1024]{1,0:T(8,128)(2,1)S(1)}, u32[]{:S(2)}, u32[]{:S(2)}) collective-permute-start(bf16[176,1024]{1,0:T(8,128)(2,1)S(1)} %slice.19), channel_id=1, source_target_pairs={{0,3},{1,0},{2,1},{3,2},{4,7},{5,4},{6,5},{7,6},{8,11},{9,8},{10,9... | collective-permute-start | bytes 1081352 | tf_op jit(solution)/shard_map/ppermute | solution.py:373
  63.5 1.8 %output.2.base_ref = f32[1024,1408]{1,0:T(8,128)S(1)} custom-call(bf16[1024,1408]{1,0:T(8,128)(2,1)S(1)} %copy-done, bf16[352,1024]{1,0:T(8,128)(2,1)S(1)} %halo_keys.1.refs_0_, bf16[352,1408]{1,0:T(8,128)(2,1)S(1)} %copy-done.1), custom_call_target="tpu_custom_call" | custom-call | flops 1015021568 | bytes 4194304 | tf_op jit(solution)/shard_map/output/pallas_call | solution.py:289
  65.3 0.0 slice-start.1
  65.3 3.4 %output.3.base_ref = f32[1024,1408]{1,0:T(8,128)S(1)} custom-call(f32[1024,1408]{1,0:T(8,128)S(1)} %output.2.base_ref, bf16[352,1024]{1,0:T(8,128)(2,1)S(1)} %collective-permute-done.6.refs_0_, bf16[352,1024]{1,0:T(8,128)(2,1)S(1)} %collective-permute-done.7.refs_1_, bf16[352,1408]{1,0:T(8,128)(2,1)S(1)} %collective-permute-done.2.refs_2_, ...), custom_call_target="tpu_custom_call" | custom-call | flops 2030043136 | bytes 4194304 | tf_op jit(solution)/shard_map/output/pallas_call | solution.py:289
  68.7 2.1 %collective-permute-done.8.refs_0_ = bf16[176,1024]{1,0:T(8,128)(2,1)S(1)} collective-permute-done((bf16[176,1024]{1,0:T(8,128)(2,1)S(1)}, bf16[176,1024]{1,0:T(8,128)(2,1)S(1)}, u32[]{:S(2)}, u32[]{:S(2)}) %collective-permute-start.8) | collective-permute-done | bytes 360480 | tf_op jit(solution)/shard_map/ppermute | solution.py:372
  70.8 3.7 %project.1 = bf16[512,640]{1,0:T(8,128)(2,1)S(1)} custom-call(s32[1,256]{1,0:T(1,128)S(1)} %bitcast.9, s32[1,256]{1,0:T(1,128)S(1)} %bitcast.10, f32[1024,1408]{1,0:T(8,128)S(1)} %output.3.base_ref, bf16[176,1024]{1,0:T(8,128)(2,1)S(1)} %collective-permute-done.8.refs_0_, bf16[176,1024]{1,0:T(8,128)(2,1)S(1)} %collective-permute-done.9.refs_1_, ...), custom_call_target="tpu_custom_call" | custom-call | flops 3221225472 | bytes 8388608 | tf_op jit(solution)/shard_map/project/pallas_call | solution.py:331
  74.6 34.8 %all_to_all.5 = bf16[64,8,640]{2,1,0:T(8,128)(2,1)} all-to-all(bf16[64,8,640]{2,1,0:T(8,128)(2,1)S(1)} %bitcast.8), channel_id=1, replica_groups=mesh['req'=64,'tp'=4] {'req'}, dimensions={0} | all-to-all | bytes 1310720 | tf_op jit(solution)/shard_map/all_to_all | solution.py:406
  109.4 2.1 %place.1 = bf16[256,512]{1,0:T(8,128)(2,1)} custom-call(bf16[512,640]{1,0:T(8,128)(2,1)} %bitcast.16), custom_call_target="tpu_custom_call" | custom-call | tf_op jit(solution)/shard_map/place/pallas_call | solution.py:354
  (26 shorter events, 0.2 us)
Async XLA Ops:
  0.0 23.4 %collective-permute-start.2 = (bf16[352,1408]{1,0:T(8,128)(2,1)}, bf16[352,1408]{1,0:T(8,128)(2,1)S(1)}, u32[]{:S(2)}, u32[]{:S(2)}) collective-permute-start(bf16[352,1408]{1,0:T(8,128)(2,1)} %refs_1_.1), channel_id=1, source_target_pairs={{0,1},{1,2},{2,3},{3,0},{4,5},{5,6},{6,7},{7,4},{8,9},{9,10},{10,1... | collective-permute-start | bytes 2973704 | tf_op jit(solution)/shard_map/ppermute | solution.py:370
  2.1 22.9 %collective-permute-start.3 = (bf16[352,1408]{1,0:T(8,128)(2,1)}, bf16[352,1408]{1,0:T(8,128)(2,1)S(1)}, u32[]{:S(2)}, u32[]{:S(2)}) collective-permute-start(bf16[352,1408]{1,0:T(8,128)(2,1)} %refs_1_.1), channel_id=1, source_target_pairs={{0,3},{1,0},{2,1},{3,2},{4,7},{5,4},{6,5},{7,6},{8,11},{9,8},{10,9... | collective-permute-start | bytes 2973704 | tf_op jit(solution)/shard_map/ppermute | solution.py:371
  3.6 23.3 %copy-start.3 = (s32[1024]{0:T(1024)S(1)}, s32[1024]{0:T(1024)}, u32[]{:S(2)}) copy-start(s32[1024]{0:T(1024)} %param.13) | copy-start | bytes 12292
  12.0 20.1 %collective-permute-start = (bf16[2,4,88,1024]{3,2,1,0:T(8,128)(2,1)S(1)}, bf16[2,4,88,1024]{3,2,1,0:T(8,128)(2,1)S(1)}, u32[]{:S(2)}, u32[]{:S(2)}) collective-permute-start(bf16[2,4,88,1024]{3,2,1,0:T(8,128)(2,1)S(1)} %get-tuple-element.16.kv_ref), channel_id=1, source_target_pairs={{0,4},{4,8},{8,12},{12,16},{16,20},{20,24},{24,28},{28,32},{32,36}... | collective-permute-start | bytes 4325384 | tf_op jit(solution)/shard_map/ppermute | solution.py:390
  16.2 20.6 %collective-permute-start.1 = (bf16[2,4,88,1024]{3,2,1,0:T(8,128)(2,1)S(1)}, bf16[2,4,88,1024]{3,2,1,0:T(8,128)(2,1)S(1)}, u32[]{:S(2)}, u32[]{:S(2)}) collective-permute-start(bf16[2,4,88,1024]{3,2,1,0:T(8,128)(2,1)S(1)} %get-tuple-element.16.kv_ref), channel_id=1, source_target_pairs={{4,0},{8,4},{12,8},{16,12},{20,16},{24,20},{28,24},{32,28},{36,32}... | collective-permute-start | bytes 4325384 | tf_op jit(solution)/shard_map/ppermute | solution.py:391
  23.4 13.4 %collective-permute-start.4 = (bf16[176,1408]{1,0:T(8,128)(2,1)S(1)}, bf16[176,1408]{1,0:T(8,128)(2,1)S(1)}, u32[]{:S(2)}, u32[]{:S(2)}) collective-permute-start(bf16[176,1408]{1,0:T(8,128)(2,1)S(1)} %slice.16), channel_id=1, source_target_pairs={{0,1},{1,2},{2,3},{3,0},{4,5},{5,6},{6,7},{7,4},{8,9},{9,10},{10,1... | collective-permute-start | bytes 1486856 | tf_op jit(solution)/shard_map/ppermute | solution.py:372
  25.1 11.7 %collective-permute-start.5 = (bf16[176,1408]{1,0:T(8,128)(2,1)S(1)}, bf16[176,1408]{1,0:T(8,128)(2,1)S(1)}, u32[]{:S(2)}, u32[]{:S(2)}) collective-permute-start(bf16[176,1408]{1,0:T(8,128)(2,1)S(1)} %slice.17), channel_id=1, source_target_pairs={{0,3},{1,0},{2,1},{3,2},{4,7},{5,4},{6,5},{7,6},{8,11},{9,8},{10,9... | collective-permute-start | bytes 1486856 | tf_op jit(solution)/shard_map/ppermute | solution.py:373
  26.8 10.0 %copy-start.4 = (s32[1,2]{1,0:T(1,128)S(1)}, s32[1,2]{1,0:T(1,128)}, u32[]{:S(2)}) copy-start(s32[1,2]{1,0:T(1,128)} %plan_ref.3) | copy-start | bytes 28
  36.8 26.6 %copy-start.5 = (s32[256]{0:T(256)S(1)}, s32[256]{0:T(256)}, u32[]{:S(2)}) copy-start(s32[256]{0:T(256)} %param.16) | copy-start | bytes 3076
  36.9 26.6 %copy-start = (bf16[1024,1408]{1,0:T(8,128)(2,1)S(1)}, bf16[1024,1408]{1,0:T(8,128)(2,1)}, u32[]{:S(2)}) copy-start(bf16[1024,1408]{1,0:T(8,128)(2,1)} %base_ref.1) | copy-start | bytes 8650756
  36.9 26.6 %copy-start.1 = (bf16[352,1408]{1,0:T(8,128)(2,1)S(1)}, bf16[352,1408]{1,0:T(8,128)(2,1)}, u32[]{:S(2)}) copy-start(bf16[352,1408]{1,0:T(8,128)(2,1)} %refs_1_.1) | copy-start | bytes 2973700
  41.4 19.0 %collective-permute-start.6 = (bf16[352,1024]{1,0:T(8,128)(2,1)S(1)}, bf16[352,1024]{1,0:T(8,128)(2,1)S(1)}, u32[]{:S(2)}, u32[]{:S(2)}) collective-permute-start(bf16[352,1024]{1,0:T(8,128)(2,1)S(1)} %halo_keys.1.refs_0_), channel_id=1, source_target_pairs={{0,1},{1,2},{2,3},{3,0},{4,5},{5,6},{6,7},{7,4},{8,9},{9,10},{10,1... | collective-permute-start | bytes 2162696 | tf_op jit(solution)/shard_map/ppermute | solution.py:370
  42.3 18.2 %collective-permute-start.7 = (bf16[352,1024]{1,0:T(8,128)(2,1)S(1)}, bf16[352,1024]{1,0:T(8,128)(2,1)S(1)}, u32[]{:S(2)}, u32[]{:S(2)}) collective-permute-start(bf16[352,1024]{1,0:T(8,128)(2,1)S(1)} %halo_keys.1.refs_0_), channel_id=1, source_target_pairs={{0,3},{1,0},{2,1},{3,2},{4,7},{5,4},{6,5},{7,6},{8,11},{9,8},{10,9... | collective-permute-start | bytes 2162696 | tf_op jit(solution)/shard_map/ppermute | solution.py:371
  60.4 10.4 %collective-permute-start.8 = (bf16[176,1024]{1,0:T(8,128)(2,1)S(1)}, bf16[176,1024]{1,0:T(8,128)(2,1)S(1)}, u32[]{:S(2)}, u32[]{:S(2)}) collective-permute-start(bf16[176,1024]{1,0:T(8,128)(2,1)S(1)} %slice.18), channel_id=1, source_target_pairs={{0,1},{1,2},{2,3},{3,0},{4,5},{5,6},{6,7},{7,4},{8,9},{9,10},{10,1... | collective-permute-start | bytes 1081352 | tf_op jit(solution)/shard_map/ppermute | solution.py:372
  60.6 10.2 %collective-permute-start.9 = (bf16[176,1024]{1,0:T(8,128)(2,1)S(1)}, bf16[176,1024]{1,0:T(8,128)(2,1)S(1)}, u32[]{:S(2)}, u32[]{:S(2)}) collective-permute-start(bf16[176,1024]{1,0:T(8,128)(2,1)S(1)} %slice.19), channel_id=1, source_target_pairs={{0,3},{1,0},{2,1},{3,2},{4,7},{5,4},{6,5},{7,6},{8,11},{9,8},{10,9... | collective-permute-start | bytes 1081352 | tf_op jit(solution)/shard_map/ppermute | solution.py:373
  63.5 7.3 %slice-start = ((s8[5767168]{0:T(1024)(128)(4,1)}), s8[4194304]{0:T(1024)(128)(4,1)S(1)}, s32[]{:S(2)}) async-start(s8[5767168]{0:T(1024)(128)(4,1)} %bitcast.6), calls=%async_computation.1 | async-start | bytes 8388608
  65.3 5.5 %slice-start.1 = ((s8[5767168]{0:T(1024)(128)(4,1)}), s8[1572864]{0:T(1024)(128)(4,1)S(1)}, s32[]{:S(2)}) async-start(s8[5767168]{0:T(1024)(128)(4,1)} %bitcast.6), calls=%async_computation.2 | async-start | bytes 3145728
  65.3 5.5 %copy-start.2 = (s32[256]{0:T(256)S(1)}, s32[256]{0:T(256)}, u32[]{:S(2)}) copy-start(s32[256]{0:T(256)} %param.17) | copy-start | bytes 3076

commit v3 on v2

--- a/solution.py
+++ b/solution.py
@@ -17,6 +17,7 @@
 TILE = 256
 QB = 512
 KB = 256
+PACK = 2
 F32 = jnp.float32
 BF16 = jnp.bfloat16
 NT = (((1,), (1,)), ((), ()))
@@ -55,19 +56,20 @@
     return (ids == jnp.where(label < 0, 16, label)).astype(F32)
 
 
-def qkv_kernel(plan_ref, table_ref, seg_ref, segt_ref, side_ref, x_ref, gain_ref, bias_ref, w_ref, q_ref, kv_ref):
-    heads = q_ref.shape[0]
-    step = pl.program_id(0)
+def normalised(x_ref, gain_ref, bias_ref):
     x = x_ref[...].astype(F32)
     centred = x - jnp.mean(x, axis=1, keepdims=True)
     variance = jnp.mean(centred * centred, axis=1, keepdims=True)
-    normed = (centred * lax.rsqrt(variance + 1e-6) * gain_ref[...].reshape(1, -1) + bias_ref[...].reshape(1, -1)).astype(BF16)
-
+    scaled = centred * lax.rsqrt(variance + 1e-6) * gain_ref[...].reshape(1, -1) + bias_ref[...].reshape(1, -1)
+    return scaled.astype(BF16)
+
+
+def rotations(plan_ref, table_ref, seg_ref, segt_ref, side_ref):
     below = seg_counts(seg_ref[...])
     seg = segt_ref[...]
     ids = lax.broadcasted_iota(jnp.int32, (16, TILE), 0)
     start = jnp.sum(jnp.where(ids == seg, below, 0.0), axis=0, keepdims=True).astype(jnp.int32)
-    token = lax.broadcasted_iota(jnp.int32, (1, TILE), 1) + step * TILE
+    token = lax.broadcasted_iota(jnp.int32, (1, TILE), 1) + pl.program_id(0) * TILE
     offset = token - start + jnp.where(seg == 0, plan_ref[0, 0], 0)
     window = lax.shift_right_logical(offset, 2)
     corner = offset & 3
@@ -86,26 +88,40 @@
         partner = jnp.where(first, pltpu.roll(value, HD - QUARTER, 0), pltpu.roll(value, QUARTER, 0))
         return value * cosine + partner * sine
 
+    return rotated
+
+
+def kv_kernel(plan_ref, table_ref, seg_ref, segt_ref, side_ref, x_ref, gain_ref, bias_ref, wk_ref, wv_ref, *kv_refs):
+    normed = normalised(x_ref, gain_ref, bias_ref)
+    rotated = rotations(plan_ref, table_ref, seg_ref, segt_ref, side_ref)
+    keys = lax.dot_general(wk_ref[0], normed, NT, preferred_element_type=F32)
+    values = lax.dot_general(wv_ref[0], normed, NT, preferred_element_type=F32)
+    pack = kv_refs[0].shape[1]
+    for h in range(pack * len(kv_refs)):
+        span = slice(h * HD, (h + 1) * HD)
+        kv_refs[h // pack][0, h % pack] = rotated(keys[span]).astype(BF16)
+        kv_refs[h // pack][1, h % pack] = values[span].astype(BF16)
+
+
+def q_kernel(plan_ref, table_ref, seg_ref, segt_ref, side_ref, x_ref, gain_ref, bias_ref, w_ref, q_ref):
+    normed = normalised(x_ref, gain_ref, bias_ref)
+    rotated = rotations(plan_ref, table_ref, seg_ref, segt_ref, side_ref)
+    queries = lax.dot_general(w_ref[0], normed, NT, preferred_element_type=F32)
     aug = lax.broadcasted_iota(jnp.int32, (AUG - HD, TILE), 0)
-    barred = jnp.where(aug == jnp.broadcast_to(seg, aug.shape), 0.0, jnp.where(aug <= 16, -BIG, 0.0))
-    queries = lax.dot_general(w_ref[0], normed, NT, preferred_element_type=F32)
-    keys = lax.dot_general(w_ref[1], normed, NT, preferred_element_type=F32)
-    values = lax.dot_general(w_ref[2], normed, NT, preferred_element_type=F32)
-    for h in range(heads):
-        span = slice(h * HD, (h + 1) * HD)
-        query = rotated(queries[span]) * (HD**-0.5 * LOG2E)
+    barred = jnp.where(aug == jnp.broadcast_to(segt_ref[...], aug.shape), 0.0, jnp.where(aug <= 16, -BIG, 0.0))
+    for h in range(q_ref.shape[0]):
+        query = rotated(queries[h * HD : (h + 1) * HD]) * (HD**-0.5 * LOG2E)
         q_ref[h] = jnp.concatenate([query, barred], axis=0).astype(BF16)
-        kv_ref[0, h] = rotated(keys[span]).astype(BF16)
-        kv_ref[1, h] = values[span].astype(BF16)
-
-
-def qkv_call(patches, seg, sides, plan, gain, bias, w_qkv, table):
+
+
+def qkv_call(kernel, name, rows, outs, patches, seg, sides, plan, gain, bias, w_qkv, table):
     count, width = patches.shape
-    local = w_qkv.shape[1]
-    heads = local // HD
     whole = lambda *shape: pl.BlockSpec(shape, lambda i: (0,) * len(shape))
-    return pl.pallas_call(
-        qkv_kernel,
+    pick = lambda k, part, size: pl.BlockSpec((1, size, width), lambda i: (k, part, 0))
+    flops = 2 * count * width * sum(size for _, _, size in rows)
+    args = (plan, table, seg, seg, sides, patches, gain, bias) + (w_qkv,) * len(rows)
+    return pl.pallas_call(
+        kernel,
         grid=(count // TILE,),
         in_specs=[
             pl.BlockSpec(memory_space=pltpu.SMEM),
@@ -116,40 +132,38 @@
             pl.BlockSpec((TILE, width), lambda i: (i, 0)),
             whole(width),
             whole(width),
-            whole(3, local, width),
+        ]
+        + [pick(*row) for row in rows],
+        out_specs=[
+            pl.BlockSpec(shape[:-1] + (TILE,), lambda i, n=len(shape): (0,) * (n - 1) + (i,)) for shape in outs
         ],
-        out_specs=[
-            pl.BlockSpec((heads, AUG, TILE), lambda i: (0, 0, i)),
-            pl.BlockSpec((2, heads, HD, TILE), lambda i: (0, 0, 0, i)),
-        ],
-        out_shape=[
-            jax.ShapeDtypeStruct((heads, AUG, count), BF16),
-            jax.ShapeDtypeStruct((2, heads, HD, count), BF16),
-        ],
-        compiler_params=pltpu.CompilerParams(vmem_limit_bytes=30 << 20),
-        cost_estimate=pl.CostEstimate(flops=6 * count * width * local, bytes_accessed=10 << 20, transcendentals=0),
-        name="qkv",
-    )(*[pltpu.with_memory_space_constraint(v, pltpu.HBM) for v in (plan, table, seg, seg, sides, patches, gain, bias, w_qkv)])
-
-
-def prepare_block(kv_ref, label, keys, values, base):
-    heads = keys.shape[0]
+        out_shape=[jax.ShapeDtypeStruct(shape, BF16) for shape in outs],
+        compiler_params=pltpu.CompilerParams(vmem_limit_bytes=28 << 20),
+        cost_estimate=pl.CostEstimate(flops=flops, bytes_accessed=6 << 20, transcendentals=0),
+        name=name,
+    )(*[pltpu.with_memory_space_constraint(v, pltpu.HBM) for v in args])
+
+
+def prepare_block(kv_refs, first, label, keys, values, base):
+    pack = kv_refs[0].shape[1]
     rows = label_rows(label)
     extra = VAUG - HD
     ones = (lax.broadcasted_iota(jnp.int32, (extra, KB), 0) == 0).astype(F32)
-    for h in range(heads):
-        block = jnp.concatenate([kv_ref[0, h, :, pl.ds(base, KB)].astype(F32), rows], axis=0)
+    for h in range(keys.shape[0]):
+        kv_ref = kv_refs[(first + h) // pack]
+        place = (first + h) % pack
+        block = jnp.concatenate([kv_ref[0, place, :, pl.ds(base, KB)].astype(F32), rows], axis=0)
         keys[h, pl.ds(base, KB), :] = block.astype(BF16).T
-        block = jnp.concatenate([kv_ref[1, h, :, pl.ds(base, KB)].astype(F32), ones], axis=0)
+        block = jnp.concatenate([kv_ref[1, place, :, pl.ds(base, KB)].astype(F32), ones], axis=0)
         values[h, :, pl.ds(base, KB)] = block.astype(BF16)
 
 
-def attend(q_ref, keys, values, acc, top, q_base, k_base):
+def attend(first, q_ref, keys, values, acc, top, q_base, k_base):
     heads = keys.shape[0]
     span = pl.ds(q_base, QB)
-    old = [top[h : h + 1, span] for h in range(heads)]
+    old = [top[first + h : first + h + 1, span] for h in range(heads)]
     scores = [
-        lax.dot_general(keys[h, pl.ds(k_base, KB), :], q_ref[h, :, span], NN, preferred_element_type=F32)
+        lax.dot_general(keys[h, pl.ds(k_base, KB), :], q_ref[first + h, :, span], NN, preferred_element_type=F32)
         for h in range(heads)
     ]
     new = [jnp.maximum(old[h], jnp.max(scores[h], axis=0, keepdims=True)) for h in range(heads)]
@@ -161,14 +175,15 @@
     sums = [acc[h, :, span] * jnp.exp2(old[h] - new[h]) + parts[h] for h in range(heads)]
     for h in range(heads):
         acc[h, :, span] = sums[h]
-        top[h : h + 1, span] = new[h]
-
-
-def own_kernel(sseg_ref, seg_ref, q_ref, kv_ref, acc_ref, top_ref, keys, values):
+        top[first + h : first + h + 1, span] = new[h]
+
+
+def own_kernel(sseg_ref, seg_ref, q_ref, *refs):
+    *kv_refs, acc_ref, top_ref, keys, values = refs
     count = seg_ref.shape[1]
     seg = seg_ref[...]
     for b in range(count // KB):
-        prepare_block(kv_ref, seg[:, b * KB : (b + 1) * KB], keys, values, b * KB)
+        prepare_block(kv_refs, 0, seg[:, b * KB : (b + 1) * KB], keys, values, b * KB)
     acc_ref[...] = jnp.zeros_like(acc_ref)
     top_ref[...] = jnp.full_like(top_ref, -BIG)
 
@@ -178,7 +193,7 @@
         high = jnp.sum((seg <= sseg_ref[0, q_base + QB - 1]).astype(jnp.int32))
 
         def inner(k, c):
-            attend(q_ref, keys, values, acc_ref, top_ref, q_base, pl.multiple_of(k * KB, KB))
+            attend(0, q_ref, keys, values, acc_ref, top_ref, q_base, pl.multiple_of(k * KB, KB))
             return c
 
         return lax.fori_loop(low // KB, (high + KB - 1) // KB, inner, carry)
@@ -191,7 +206,7 @@
     vmem = pl.BlockSpec(memory_space=pltpu.VMEM)
     return pl.pallas_call(
         own_kernel,
-        in_specs=[pl.BlockSpec(memory_space=pltpu.SMEM), vmem, vmem, vmem],
+        in_specs=[pl.BlockSpec(memory_space=pltpu.SMEM)] + [vmem] * (2 + len(kv)),
         out_specs=[vmem, vmem],
         out_shape=[
             jax.ShapeDtypeStruct((heads, VAUG, count), F32),
@@ -201,12 +216,13 @@
         compiler_params=pltpu.CompilerParams(vmem_limit_bytes=20 << 20),
         cost_estimate=pl.CostEstimate(flops=8 << 30, bytes_accessed=8 << 20, transcendentals=4 << 20),
         name="own_keys",
-    )(seg, seg, q, kv)
-
-
-def halo_kernel(plan_ref, sseg_ref, q_ref, acc_in, top_in, before_ref, after_ref, out_ref, acc, top, keys, values):
-    heads, _, count = q_ref.shape
-    acc[...] = acc_in[...]
+    )(seg, seg, q, *kv)
+
+
+def halo_kernel(first, plan_ref, sseg_ref, q_ref, acc_in, top_in, before_ref, after_ref, out_ref, acc, top, keys, values):
+    count = q_ref.shape[2]
+    heads = keys.shape[0]
+    acc[...] = acc_in[first : first + heads]
     top[...] = top_in[...]
     lead, trail = plan_ref[0, 0], plan_ref[0, 1]
     last = sseg_ref[0, count - 1]
@@ -215,14 +231,14 @@
     def before_block(k, carry):
         base = pl.multiple_of(k * KB, KB)
         label = jnp.where(token + base >= count - lead, 0, -1)
-        prepare_block(before_ref, label, keys, values, base)
+        prepare_block([before_ref], first, label, keys, values, base)
 
         def inner(b, c):
             q_base = pl.multiple_of(b * QB, QB)
 
             @pl.when(sseg_ref[0, q_base] == 0)
             def _():
-                attend(q_ref, keys, values, acc, top, q_base, base)
+                attend(first, q_ref, keys, values, acc, top, q_base, base)
 
             return c
 
@@ -233,14 +249,14 @@
     def after_block(k, carry):
         base = pl.multiple_of(k * KB, KB)
         label = jnp.where(token + base < trail, last, -1)
-        prepare_block(after_ref, label, keys, values, base)
+        prepare_block([after_ref], first, label, keys, values, base)
 
         def inner(b, c):
             q_base = pl.multiple_of(b * QB, QB)
 
             @pl.when(sseg_ref[0, q_base + QB - 1] == last)
             def _():
-                attend(q_ref, keys, values, acc, top, q_base, base)
+                attend(first, q_ref, keys, values, acc, top, q_base, base)
 
             return c
 
@@ -251,43 +267,45 @@
         out_ref[pl.ds(h * HD, HD), :] = (acc[h, :HD, :] / acc[h, HD : HD + 1, :]).astype(BF16)
 
 
-def halo_call(plan, seg, q, acc, top, before, after):
-    heads, _, count = q.shape
+def halo_call(first, plan, seg, q, acc, top, before, after):
+    count = q.shape[2]
+    heads = PACK
     vmem = pl.BlockSpec(memory_space=pltpu.VMEM)
     smem = pl.BlockSpec(memory_space=pltpu.SMEM)
     return pl.pallas_call(
-        halo_kernel,
+        functools.partial(halo_kernel, first),
         in_specs=[smem, smem, vmem, vmem, vmem, vmem, vmem],
         out_specs=vmem,
         out_shape=jax.ShapeDtypeStruct((heads * HD, count), BF16),
         scratch_shapes=[
-            pltpu.VMEM(acc.shape, F32),
+            pltpu.VMEM((heads, VAUG, count), F32),
             pltpu.VMEM(top.shape, F32),
             pltpu.VMEM((heads, count, AUG), BF16),
             pltpu.VMEM((heads, VAUG, count), BF16),
         ],
         compiler_params=pltpu.CompilerParams(vmem_limit_bytes=20 << 20),
-        cost_estimate=pl.CostEstimate(flops=8 << 30, bytes_accessed=8 << 20, transcendentals=4 << 20),
+        cost_estimate=pl.CostEstimate(flops=3 << 30, bytes_accessed=8 << 20, transcendentals=4 << 20),
         name="halo_keys",
     )(plan, seg, q, acc, top, before, after)
 
 
-def gather_kernel(parts, base_ref, *refs):
+def gather_kernel(parts, rows, base_ref, *refs):
     out_ref = refs[-1]
     for start in range(0, out_ref.shape[0], TILE):
         span = slice(start, start + TILE)
         total = base_ref[span].astype(F32)
-        for h_ref, w_ref in zip(refs[:parts], refs[parts : 2 * parts]):
-            total += lax.dot_general(h_ref[:, span], w_ref[...], TN, preferred_element_type=F32)
+        for h_ref, w_ref, row in zip(refs[:parts], refs[parts : 2 * parts], rows):
+            w = w_ref[row : row + h_ref.shape[0]]
+            total += lax.dot_general(h_ref[:, span], w, TN, preferred_element_type=F32)
         out_ref[span] = total
 
 
-def gather_call(base, heads_parts, w_parts):
+def gather_call(base, heads_parts, w_parts, rows):
     vmem = pl.BlockSpec(memory_space=pltpu.VMEM)
     parts = len(heads_parts)
     flops = 2 * base.shape[0] * base.shape[1] * sum(h.shape[0] for h in heads_parts)
     return pl.pallas_call(
-        functools.partial(gather_kernel, parts),
+        functools.partial(gather_kernel, parts, rows),
         in_specs=[vmem] * (1 + 2 * parts),
         out_specs=vmem,
         out_shape=jax.ShapeDtypeStruct(base.shape, F32),
@@ -297,15 +315,16 @@
     )(base, *heads_parts, *w_parts)
 
 
-def project_kernel(parts, slot_ref, dest_ref, base_ref, *refs):
+def project_kernel(parts, starts, slot_ref, dest_ref, base_ref, *refs):
     proj, send_ref, mixed = refs[2 * parts :]
     count, width = base_ref.shape
     chunks = width // 128
     for start in range(0, count, TILE):
         span = slice(start, start + TILE)
         total = base_ref[span]
-        for h_ref, w_ref in zip(refs[:parts], refs[parts : 2 * parts]):
-            total += lax.dot_general(h_ref[:, span], w_ref[...], TN, preferred_element_type=F32)
+        for h_ref, w_ref, row in zip(refs[:parts], refs[parts : 2 * parts], starts):
+            w = w_ref[row : row + h_ref.shape[0]]
+            total += lax.dot_general(h_ref[:, span], w, TN, preferred_element_type=F32)
         for c in range(chunks):
             mixed[c, span, :] = total[:, c * 128 : (c + 1) * 128]
     rows = count // 4
@@ -323,13 +342,13 @@
     send_ref[:, cols:] = jnp.broadcast_to(dest, (send_ref.shape[0], 128)).astype(BF16)
 
 
-def project_call(slot, dest, base, heads_parts, w_parts, w_proj, slots):
+def project_call(slot, dest, base, heads_parts, w_parts, starts, w_proj, slots):
     vmem = pl.BlockSpec(memory_space=pltpu.VMEM)
     parts = len(heads_parts)
     count, width = base.shape
     cols = w_proj.shape[1]
     return pl.pallas_call(
-        functools.partial(project_kernel, parts),
+        functools.partial(project_kernel, parts, starts),
         in_specs=[vmem] * (4 + 2 * parts),
         out_specs=vmem,
         out_shape=jax.ShapeDtypeStruct((slots, cols + 128), BF16),
@@ -366,7 +385,7 @@
 
 
 def around(block, axis):
-    half = block.shape[0] // 2
+    half = -(-block.shape[0] // 32) * 16
     left = lax.ppermute(block, axis, ring(axis, 1))
     right = lax.ppermute(block, axis, ring(axis, -1))
     far_top = lax.ppermute(left[:half], axis, ring(axis, 1))
@@ -376,31 +395,44 @@
 
 def on_device(patches, segment_ids, grid_sides, split_plan, owner_dev, dest_row, ln_gain, ln_bias, w_qkv, w_out, w_proj):
     count, width = patches.shape
+    local = w_qkv.shape[1]
+    heads = local // HD
     rows_out = owner_dev.shape[0]
     peers = lax.axis_size("req")
     lanes = 2 * rows_out // peers
     seg = segment_ids.reshape(1, count)
     table = jnp.asarray(rope_table())
     w_left, w_right, w_top, w_end = around(w_out, "tp")
-    q, kv = qkv_call(
-        patches, seg, grid_sides.reshape(1, count), split_plan, ln_gain, ln_bias, w_qkv, table
-    )
+    inputs = (patches, seg, grid_sides.reshape(1, count), split_plan, ln_gain, ln_bias, w_qkv, table)
+    (kv,) = qkv_call(kv_kernel, "keys_values", [(1, 0, local), (2, 0, local)], [(2, heads, HD, count)], *inputs)
     up = [(i, i + 1) for i in range(peers - 1)]
     down = [(j, i) for i, j in up]
     before = lax.ppermute(kv, "req", up)
     after = lax.ppermute(kv, "req", down)
-    acc, top = own_call(seg, q, kv)
+    (q,) = qkv_call(q_kernel, "queries", [(0, 0, local)], [(heads, AUG, count)], *inputs)
+    acc, top = own_call(seg, q, [kv])
     before, after, w_left, w_right, w_top, w_end = lax.optimization_barrier(
         (before, after, w_left, w_right, w_top, w_end)
     )
-    heads_out = halo_call(split_plan, seg, q, acc, top, before, after)
-    left, right, far_top, far_end = around(heads_out, "tp")
+    pack = PACK * HD
+    w_far = [w_top, w_end]
+    lows = list(range(0, local, pack))
+    outs, sides = [], []
+    for index in range(len(lows)):
+        if outs:
+            acc, outs[-1] = lax.optimization_barrier((acc, outs[-1]))
+        outs.append(halo_call(index * PACK, split_plan, seg, q, acc, top, before, after))
+        sides.append(around(outs[-1], "tp"))
+    terms = [(part, w_out, low) for part, low in zip(outs, lows)]
+    base = patches
+    for index, (left, right, far_top, far_end) in enumerate(sides):
+        terms += [(left, w_left, lows[index]), (right, w_right, lows[index])]
+        base = gather_call(base, *zip(*terms))
+        terms = [(far_top, w_far[index], 0), (far_end, w_far[index], far_top.shape[0])]
     within = jnp.arange(rows_out, dtype=jnp.int32) % lanes
     slot = (owner_dev * lanes + within).reshape(1, rows_out)
-    base = gather_call(patches, [heads_out], [w_out])
-    base = gather_call(base, [left, right], [w_left, w_right])
     send = project_call(
-        slot, dest_row.reshape(1, rows_out), base, [far_top, far_end], [w_top, w_end], w_proj, peers * lanes
+        slot, dest_row.reshape(1, rows_out), base, *zip(*terms), w_proj, peers * lanes
     )
     cols = send.shape[1]
     got = lax.all_to_all(send.reshape(peers, lanes, cols), "req", split_axis=0, concat_axis=0, tiled=True)

time: 112 us -> 113 us (level)
  waiting for transfers between devices: 29 us -> 11.5 us
  Pallas kernels: 28.5 us -> 36.6 us
  starting transfers between devices: 18.9 us -> 24.5 us
  blocking collectives: 34.8 us -> 38.8 us
    ppermute x2 -> x3, waiting for transfers between devices: 21.4 us -> 6.86 us  [around(): left = lax.ppermute(block, axis, ring(axis, 1))]
    pallas_call x5 -> x7, Pallas kernels: 21.8 us -> 30 us  [the longest x2 12.7 us: qkv_call(): pl.pallas_call(kernel, grid=(count // TILE,), in_specs=[pl.BlockSpec(memo...]
    all_to_all x1, blocking collectives: 34.8 us -> 38.8 us  [on_device(): lax.all_to_all(send.reshape(peers, lanes, cols), 'req', split_axis=0, con...]
    ppermute x2 -> x3, waiting for transfers between devices: 2.11 us -> 0.01 us  [around(): far_top = lax.ppermute(left[:half], axis, ring(axis, 1))]
    ppermute x2 -> x3, starting transfers between devices: 4.64 us -> 6.56 us  [around(): far_end = lax.ppermute(right[half:], axis, ring(axis, -1))]
    ppermute x2 -> x3, starting transfers between devices: 3.33 us -> 4.75 us  [around(): right = lax.ppermute(block, axis, ring(axis, -1))]
    ppermute x2 -> x3, starting transfers between devices: 2.99 us -> 4.33 us  [around(): left = lax.ppermute(block, axis, ring(axis, 1))]
    ppermute x2 -> x3, starting transfers between devices: 1.73 us -> 2.66 us  [around(): far_top = lax.ppermute(left[:half], axis, ring(axis, 1))]
  transfers between devices with their start and end apart: 10 -> 14, of which waited for: 5 -> 5; matrix products, arithmetic and copies ran while one was open for 0% -> 0% of each run, Pallas kernels for 16% -> 25%
where the time goes in v3:
time: 113 us; the launch traced here: 112 us
  blocking collectives  38.8 us (34%)
  Pallas kernels  36.6 us (32%)
  starting transfers between devices  24.5 us (22%)
  waiting for transfers between devices  11.5 us (10%)
    all_to_all x1, blocking collectives, on_device(): lax.all_to_all(send.reshape(peers, lanes, cols), 'req', split_axis=0, con...  38.8 us
    pallas_call x2, Pallas kernels, qkv_call(): pl.pallas_call(kernel, grid=(count // TILE,), in_specs=[pl.BlockSpec(memo...  12.7 us
    pallas_call x2, Pallas kernels, halo_call(): pl.pallas_call(functools.partial(halo_kernel, first), in_specs=[smem, sme...  6.87 us
    ppermute x3, waiting for transfers between devices, around(): left = lax.ppermute(block, axis, ring(axis, 1))  6.86 us
    pallas_call x2, Pallas kernels, gather_call(): pl.pallas_call(functools.partial(gather_kernel, parts, rows), in_specs=[v...  6.8 us
    ppermute x3, starting transfers between devices, around(): far_end = lax.ppermute(right[half:], axis, ring(axis, -1))  6.56 us
    ppermute x3, starting transfers between devices, around(): right = lax.ppermute(block, axis, ring(axis, -1))  4.75 us
    pallas_call x1, Pallas kernels, own_call(): pl.pallas_call(own_kernel, in_specs=[pl.BlockSpec(memory_space=pltpu.SMEM...  4.51 us
  transfers between devices with their start and end apart: 14, of which 5 were waited for; matrix products, arithmetic and copies ran while one was open for 0% of the time, Pallas kernels for 25%

profile of v3, /device:TPU:1, one launch (start us, length us, event | category | flops | bytes accessed | tf_op | source)
XLA Modules:
  0.0 111.8 jit_solution(10727316530938301024)
XLA Ops:
  0.0 2.1 %collective-permute-start.2 = (bf16[352,1408]{1,0:T(8,128)(2,1)}, bf16[352,1408]{1,0:T(8,128)(2,1)S(1)}, u32[]{:S(2)}, u32[]{:S(2)}) collective-permute-start(bf16[352,1408]{1,0:T(8,128)(2,1)} %refs_5_.1), channel_id=1, source_target_pairs={{0,1},{1,2},{2,3},{3,0},{4,5},{5,6},{6,7},{7,4},{8,9},{9,10},{10,1... | collective-permute-start | bytes 2973704 | tf_op jit(solution)/shard_map/ppermute | solution.py:389
  2.1 1.4 %collective-permute-start.3 = (bf16[352,1408]{1,0:T(8,128)(2,1)}, bf16[352,1408]{1,0:T(8,128)(2,1)S(1)}, u32[]{:S(2)}, u32[]{:S(2)}) collective-permute-start(bf16[352,1408]{1,0:T(8,128)(2,1)} %refs_5_.1), channel_id=1, source_target_pairs={{0,3},{1,0},{2,1},{3,2},{4,7},{5,4},{6,5},{7,6},{8,11},{9,8},{10,9... | collective-permute-start | bytes 2973704 | tf_op jit(solution)/shard_map/ppermute | solution.py:390
  3.6 6.9 %keys_values.1.refs_0_ = bf16[2,4,88,1024]{3,2,1,0:T(8,128)(2,1)S(1)} custom-call(s32[1,2]{1,0:T(1,128)} %plan_ref.7, bf16[176,192]{1,0:T(8,128)(2,1)} %constant.19.clone.table_ref, s32[1,1024]{1,0:T(1,128)} %bitcast.9, s32[1,1024]{1,0:T(1,128)} %bitcast.10, s32[1,1024]{1,0:T(1,128)} %bitcast.20, bf16[1024,1408]{1,0:T(8,128)(2,1)} %base_ref.1, ...), custom_call_target="tpu_custom_call" | custom-call | flops 2030043136 | bytes 6291456 | tf_op jit(solution)/shard_map/keys_values/pallas_call | solution.py:123
  10.5 4.2 %collective-permute-start = (bf16[2,4,88,1024]{3,2,1,0:T(8,128)(2,1)S(1)}, bf16[2,4,88,1024]{3,2,1,0:T(8,128)(2,1)S(1)}, u32[]{:S(2)}, u32[]{:S(2)}) collective-permute-start(bf16[2,4,88,1024]{3,2,1,0:T(8,128)(2,1)S(1)} %keys_values.1.refs_0_), channel_id=1, source_target_pairs={{0,4},{4,8},{8,12},{12,16},{16,20},{20,24},{24,28},{28,32},{32,36}... | collective-permute-start | bytes 4325384 | tf_op jit(solution)/shard_map/ppermute | solution.py:410
  14.7 2.0 %collective-permute-start.1 = (bf16[2,4,88,1024]{3,2,1,0:T(8,128)(2,1)S(1)}, bf16[2,4,88,1024]{3,2,1,0:T(8,128)(2,1)S(1)}, u32[]{:S(2)}, u32[]{:S(2)}) collective-permute-start(bf16[2,4,88,1024]{3,2,1,0:T(8,128)(2,1)S(1)} %keys_values.1.refs_0_), channel_id=1, source_target_pairs={{4,0},{8,4},{12,8},{16,12},{20,16},{24,20},{28,24},{32,28},{36,32}... | collective-permute-start | bytes 4325384 | tf_op jit(solution)/shard_map/ppermute | solution.py:411
  16.7 5.8 %queries.1.q_ref = bf16[4,128,1024]{2,1,0:T(8,128)(2,1)S(1)} custom-call(s32[1,2]{1,0:T(1,128)} %plan_ref.7, bf16[176,192]{1,0:T(8,128)(2,1)} %constant.19.clone.table_ref, s32[1,1024]{1,0:T(1,128)} %bitcast.11, s32[1,1024]{1,0:T(1,128)} %bitcast.12, s32[1,1024]{1,0:T(1,128)} %bitcast.21, bf16[1024,1408]{1,0:T(8,128)(2,1)} %base_ref.1, f32[1408]{0:T(1024)} %gain_ref.3, ...), custom_call_target="tpu_custom_call" | custom-call | flops 1015021568 | bytes 6291456 | tf_op jit(solution)/shard_map/queries/pallas_call | solution.py:123
  22.5 0.9 collective-permute-done.2.refs_6_
  23.4 1.6 %collective-permute-start.4 = (bf16[176,1408]{1,0:T(8,128)(2,1)S(1)}, bf16[176,1408]{1,0:T(8,128)(2,1)S(1)}, u32[]{:S(2)}, u32[]{:S(2)}) collective-permute-start(bf16[176,1408]{1,0:T(8,128)(2,1)S(1)} %slice.24), channel_id=1, source_target_pairs={{0,1},{1,2},{2,3},{3,0},{4,5},{5,6},{6,7},{7,4},{8,9},{9,10},{10,1... | collective-permute-start | bytes 1486856 | tf_op jit(solution)/shard_map/ppermute | solution.py:391
  25.1 1.7 %collective-permute-start.5 = (bf16[176,1408]{1,0:T(8,128)(2,1)S(1)}, bf16[176,1408]{1,0:T(8,128)(2,1)S(1)}, u32[]{:S(2)}, u32[]{:S(2)}) collective-permute-start(bf16[176,1408]{1,0:T(8,128)(2,1)S(1)} %slice.25), channel_id=1, source_target_pairs={{0,3},{1,0},{2,1},{3,2},{4,7},{5,4},{6,5},{7,6},{8,11},{9,8},{10,9... | collective-permute-start | bytes 1486856 | tf_op jit(solution)/shard_map/ppermute | solution.py:392
  26.9 4.5 %own_keys.1 = (f32[4,96,1024]{2,1,0:T(8,128)S(1)}, f32[8,1024]{1,0:T(8,128)S(1)}) custom-call(s32[1,1024]{1,0:T(1,128)S(1)} %bitcast.13, s32[1,1024]{1,0:T(1,128)S(1)} %bitcast.14, bf16[4,128,1024]{2,1,0:T(8,128)(2,1)S(1)} %queries.1.q_ref, bf16[2,4,88,1024]{3,2,1,0:T(8,128)(2,1)S(1)} %keys_values.1.refs_0_), custom_call_target="tpu_custom_call" | custom-call | flops 8589934592 | bytes 8388608 | tf_op jit(solution)/shard_map/own_keys/pallas_call | solution.py:207
  31.4 3.9 %collective-permute-done.1.after_ref = bf16[2,4,88,1024]{3,2,1,0:T(8,128)(2,1)S(1)} collective-permute-done((bf16[2,4,88,1024]{3,2,1,0:T(8,128)(2,1)S(1)}, bf16[2,4,88,1024]{3,2,1,0:T(8,128)(2,1)S(1)}, u32[]{:S(2)}, u32[]{:S(2)}) %collective-permute-start.1) | collective-permute-done | bytes 1441824 | tf_op jit(solution)/shard_map/ppermute | solution.py:411
  36.0 3.4 %halo_keys.2.refs_0_ = bf16[176,1024]{1,0:T(8,128)(2,1)S(1)} custom-call(s32[1,2]{1,0:T(1,128)S(1)} %copy-done.3, s32[1,1024]{1,0:T(1,128)S(1)} %bitcast.15, bf16[4,128,1024]{2,1,0:T(8,128)(2,1)S(1)} %queries.1.q_ref, f32[4,96,1024]{2,1,0:T(8,128)S(1)} %get-tuple-element.20.acc_in, f32[8,1024]{1,0:T(8,128)S(1)} %get-tuple-element.16.top_in, ...), custom_call_target="tpu_custom_call" | custom-call | flops 3221225472 | bytes 8388608 | tf_op jit(solution)/shard_map/halo_keys/pallas_call | solution.py:275
  39.5 1.7 %collective-permute-start.6 = (bf16[176,1024]{1,0:T(8,128)(2,1)S(1)}, bf16[176,1024]{1,0:T(8,128)(2,1)S(1)}, u32[]{:S(2)}, u32[]{:S(2)}) collective-permute-start(bf16[176,1024]{1,0:T(8,128)(2,1)S(1)} %halo_keys.2.refs_0_), channel_id=1, source_target_pairs={{0,1},{1,2},{2,3},{3,0},{4,5},{5,6},{6,7},{7,4},{8,9},{9,10},{10,1... | collective-permute-start | bytes 1081352 | tf_op jit(solution)/shard_map/ppermute | solution.py:389
  41.2 1.1 collective-permute-start.7
  42.3 3.4 %halo_keys.3.refs_1_ = bf16[176,1024]{1,0:T(8,128)(2,1)S(1)} custom-call(s32[1,2]{1,0:T(1,128)S(1)} %copy-done.3, s32[1,1024]{1,0:T(1,128)S(1)} %bitcast.16, bf16[4,128,1024]{2,1,0:T(8,128)(2,1)S(1)} %queries.1.q_ref, f32[4,96,1024]{2,1,0:T(8,128)S(1)} %get-tuple-element.20.acc_in, f32[8,1024]{1,0:T(8,128)S(1)} %get-tuple-element.16.top_in, ...), custom_call_target="tpu_custom_call" | custom-call | flops 3221225472 | bytes 8388608 | tf_op jit(solution)/shard_map/halo_keys/pallas_call | solution.py:275
  46.2 2.3 %collective-permute-start.11 = (bf16[176,1024]{1,0:T(8,128)(2,1)S(1)}, bf16[176,1024]{1,0:T(8,128)(2,1)S(1)}, u32[]{:S(2)}, u32[]{:S(2)}) collective-permute-start(bf16[176,1024]{1,0:T(8,128)(2,1)S(1)} %halo_keys.3.refs_1_), channel_id=1, source_target_pairs={{0,3},{1,0},{2,1},{3,2},{4,7},{5,4},{6,5},{7,6},{8,11},{9,8},{10,9... | collective-permute-start | bytes 1081352 | tf_op jit(solution)/shard_map/ppermute | solution.py:390
  50.2 2.2 %collective-permute-start.9 = (bf16[80,1024]{1,0:T(8,128)(2,1)S(1)}, bf16[80,1024]{1,0:T(8,128)(2,1)S(1)}, u32[]{:S(2)}, u32[]{:S(2)}) collective-permute-start(bf16[80,1024]{1,0:T(8,128)(2,1)S(1)} %slice.27), channel_id=1, source_target_pairs={{0,3},{1,0},{2,1},{3,2},{4,7},{5,4},{6,5},{7,6},{8,11},{9,8},{10,9... | collective-permute-start | bytes 491528 | tf_op jit(solution)/shard_map/ppermute | solution.py:392
  52.3 5.2 %collective-permute-done.10.refs_2_ = bf16[176,1024]{1,0:T(8,128)(2,1)S(1)} collective-permute-done((bf16[176,1024]{1,0:T(8,128)(2,1)S(1)}, bf16[176,1024]{1,0:T(8,128)(2,1)S(1)}, u32[]{:S(2)}, u32[]{:S(2)}) %collective-permute-start.10) | collective-permute-done | bytes 360480 | tf_op jit(solution)/shard_map/ppermute | solution.py:389
  57.7 2.7 %collective-permute-start.13 = (bf16[80,1024]{1,0:T(8,128)(2,1)S(1)}, bf16[80,1024]{1,0:T(8,128)(2,1)S(1)}, u32[]{:S(2)}, u32[]{:S(2)}) collective-permute-start(bf16[80,1024]{1,0:T(8,128)(2,1)S(1)} %slice.29), channel_id=1, source_target_pairs={{0,3},{1,0},{2,1},{3,2},{4,7},{5,4},{6,5},{7,6},{8,11},{9,8},{10,9... | collective-permute-start | bytes 491528 | tf_op jit(solution)/shard_map/ppermute | solution.py:392
  60.4 3.5 %output.2.base_ref = f32[1024,1408]{1,0:T(8,128)S(1)} custom-call(bf16[1024,1408]{1,0:T(8,128)(2,1)S(1)} %copy-done, bf16[176,1024]{1,0:T(8,128)(2,1)S(1)} %halo_keys.2.refs_0_, bf16[176,1024]{1,0:T(8,128)(2,1)S(1)} %halo_keys.3.refs_1_, bf16[176,1024]{1,0:T(8,128)(2,1)S(1)} %collective-permute-done.6.refs_2_, ...), custom_call_target="tpu_custom_call" | custom-call | flops 2030043136 | bytes 4194304 | tf_op jit(solution)/shard_map/output/pallas_call | solution.py:307
  63.9 3.3 %output.3.base_ref = f32[1024,1408]{1,0:T(8,128)S(1)} custom-call(f32[1024,1408]{1,0:T(8,128)S(1)} %output.2.base_ref, bf16[96,1024]{1,0:T(8,128)(2,1)S(1)} %collective-permute-done.8.refs_0_, bf16[80,1024]{1,0:T(8,128)(2,1)S(1)} %collective-permute-done.9.refs_1_, bf16[176,1024]{1,0:T(8,128)(2,1)S(1)} %collective-permute-done.10.refs_2_, ...), custom_call_target="tpu_custom_call" | custom-call | flops 1522532352 | bytes 4194304 | tf_op jit(solution)/shard_map/output/pallas_call | solution.py:307
  67.3 3.6 %project.1 = bf16[512,640]{1,0:T(8,128)(2,1)S(1)} custom-call(s32[1,256]{1,0:T(1,128)S(1)} %bitcast.17, s32[1,256]{1,0:T(1,128)S(1)} %bitcast.18, f32[1024,1408]{1,0:T(8,128)S(1)} %output.3.base_ref, bf16[96,1024]{1,0:T(8,128)(2,1)S(1)} %collective-permute-done.12.refs_0_, bf16[80,1024]{1,0:T(8,128)(2,1)S(1)} %collective-permute-done.13.refs_1_, ...), custom_call_target="tpu_custom_call" | custom-call | flops 3221225472 | bytes 8388608 | tf_op jit(solution)/shard_map/project/pallas_call | solution.py:350
  70.9 38.8 %all_to_all.5 = bf16[64,8,640]{2,1,0:T(8,128)(2,1)} all-to-all(bf16[64,8,640]{2,1,0:T(8,128)(2,1)S(1)} %bitcast.8), channel_id=1, replica_groups=mesh['req'=64,'tp'=4] {'req'}, dimensions={0} | all-to-all | bytes 1310720 | tf_op jit(solution)/shard_map/all_to_all | solution.py:438
  109.7 2.1 %place.1 = bf16[256,512]{1,0:T(8,128)(2,1)} custom-call(bf16[512,640]{1,0:T(8,128)(2,1)} %bitcast.19), custom_call_target="tpu_custom_call" | custom-call | tf_op jit(solution)/shard_map/place/pallas_call | solution.py:373
  (38 shorter events, 3.2 us)
Async XLA Ops:
  0.0 23.4 %collective-permute-start.2 = (bf16[352,1408]{1,0:T(8,128)(2,1)}, bf16[352,1408]{1,0:T(8,128)(2,1)S(1)}, u32[]{:S(2)}, u32[]{:S(2)}) collective-permute-start(bf16[352,1408]{1,0:T(8,128)(2,1)} %refs_5_.1), channel_id=1, source_target_pairs={{0,1},{1,2},{2,3},{3,0},{4,5},{5,6},{6,7},{7,4},{8,9},{9,10},{10,1... | collective-permute-start | bytes 2973704 | tf_op jit(solution)/shard_map/ppermute | solution.py:389
  2.1 22.9 %collective-permute-start.3 = (bf16[352,1408]{1,0:T(8,128)(2,1)}, bf16[352,1408]{1,0:T(8,128)(2,1)S(1)}, u32[]{:S(2)}, u32[]{:S(2)}) collective-permute-start(bf16[352,1408]{1,0:T(8,128)(2,1)} %refs_5_.1), channel_id=1, source_target_pairs={{0,3},{1,0},{2,1},{3,2},{4,7},{5,4},{6,5},{7,6},{8,11},{9,8},{10,9... | collective-permute-start | bytes 2973704 | tf_op jit(solution)/shard_map/ppermute | solution.py:390
  10.5 16.4 %copy-start.2 = (s32[1024]{0:T(1024)S(1)}, s32[1024]{0:T(1024)}, u32[]{:S(2)}) copy-start(s32[1024]{0:T(1024)} %param.13) | copy-start | bytes 12292
  10.5 20.9 %collective-permute-start = (bf16[2,4,88,1024]{3,2,1,0:T(8,128)(2,1)S(1)}, bf16[2,4,88,1024]{3,2,1,0:T(8,128)(2,1)S(1)}, u32[]{:S(2)}, u32[]{:S(2)}) collective-permute-start(bf16[2,4,88,1024]{3,2,1,0:T(8,128)(2,1)S(1)} %keys_values.1.refs_0_), channel_id=1, source_target_pairs={{0,4},{4,8},{8,12},{12,16},{16,20},{20,24},{24,28},{28,32},{32,36}... | collective-permute-start | bytes 4325384 | tf_op jit(solution)/shard_map/ppermute | solution.py:410
  14.7 20.6 %collective-permute-start.1 = (bf16[2,4,88,1024]{3,2,1,0:T(8,128)(2,1)S(1)}, bf16[2,4,88,1024]{3,2,1,0:T(8,128)(2,1)S(1)}, u32[]{:S(2)}, u32[]{:S(2)}) collective-permute-start(bf16[2,4,88,1024]{3,2,1,0:T(8,128)(2,1)S(1)} %keys_values.1.refs_0_), channel_id=1, source_target_pairs={{4,0},{8,4},{12,8},{16,12},{20,16},{24,20},{28,24},{32,28},{36,32}... | collective-permute-start | bytes 4325384 | tf_op jit(solution)/shard_map/ppermute | solution.py:411
  23.4 11.9 %collective-permute-start.4 = (bf16[176,1408]{1,0:T(8,128)(2,1)S(1)}, bf16[176,1408]{1,0:T(8,128)(2,1)S(1)}, u32[]{:S(2)}, u32[]{:S(2)}) collective-permute-start(bf16[176,1408]{1,0:T(8,128)(2,1)S(1)} %slice.24), channel_id=1, source_target_pairs={{0,1},{1,2},{2,3},{3,0},{4,5},{5,6},{6,7},{7,4},{8,9},{9,10},{10,1... | collective-permute-start | bytes 1486856 | tf_op jit(solution)/shard_map/ppermute | solution.py:391
  25.1 10.9 %copy-start.3 = (s32[1,2]{1,0:T(1,128)S(1)}, s32[1,2]{1,0:T(1,128)}, u32[]{:S(2)}) copy-start(s32[1,2]{1,0:T(1,128)} %plan_ref.7) | copy-start | bytes 28
  25.1 10.9 %collective-permute-start.5 = (bf16[176,1408]{1,0:T(8,128)(2,1)S(1)}, bf16[176,1408]{1,0:T(8,128)(2,1)S(1)}, u32[]{:S(2)}, u32[]{:S(2)}) collective-permute-start(bf16[176,1408]{1,0:T(8,128)(2,1)S(1)} %slice.25), channel_id=1, source_target_pairs={{0,3},{1,0},{2,1},{3,2},{4,7},{5,4},{6,5},{7,6},{8,11},{9,8},{10,9... | collective-permute-start | bytes 1486856 | tf_op jit(solution)/shard_map/ppermute | solution.py:392
  39.5 10.6 %copy-start.5 = (s32[256]{0:T(256)S(1)}, s32[256]{0:T(256)}, u32[]{:S(2)}) copy-start(s32[256]{0:T(256)} %param.16) | copy-start | bytes 3076
  39.5 20.9 %copy-start.1 = (bf16[352,1408]{1,0:T(8,128)(2,1)S(1)}, bf16[352,1408]{1,0:T(8,128)(2,1)}, u32[]{:S(2)}) copy-start(bf16[352,1408]{1,0:T(8,128)(2,1)} %refs_5_.1) | copy-start | bytes 2973700
  39.5 9.8 %collective-permute-start.6 = (bf16[176,1024]{1,0:T(8,128)(2,1)S(1)}, bf16[176,1024]{1,0:T(8,128)(2,1)S(1)}, u32[]{:S(2)}, u32[]{:S(2)}) collective-permute-start(bf16[176,1024]{1,0:T(8,128)(2,1)S(1)} %halo_keys.2.refs_0_), channel_id=1, source_target_pairs={{0,1},{1,2},{2,3},{3,0},{4,5},{5,6},{6,7},{7,4},{8,9},{9,10},{10,1... | collective-permute-start | bytes 1081352 | tf_op jit(solution)/shard_map/ppermute | solution.py:389
  41.2 8.9 %collective-permute-start.7 = (bf16[176,1024]{1,0:T(8,128)(2,1)S(1)}, bf16[176,1024]{1,0:T(8,128)(2,1)S(1)}, u32[]{:S(2)}, u32[]{:S(2)}) collective-permute-start(bf16[176,1024]{1,0:T(8,128)(2,1)S(1)} %halo_keys.2.refs_0_), channel_id=1, source_target_pairs={{0,3},{1,0},{2,1},{3,2},{4,7},{5,4},{6,5},{7,6},{8,11},{9,8},{10,9... | collective-permute-start | bytes 1081352 | tf_op jit(solution)/shard_map/ppermute | solution.py:390
  42.3 18.1 %copy-start = (bf16[1024,1408]{1,0:T(8,128)(2,1)S(1)}, bf16[1024,1408]{1,0:T(8,128)(2,1)}, u32[]{:S(2)}) copy-start(bf16[1024,1408]{1,0:T(8,128)(2,1)} %base_ref.1) | copy-start | bytes 8650756
  45.7 11.8 %collective-permute-start.10 = (bf16[176,1024]{1,0:T(8,128)(2,1)S(1)}, bf16[176,1024]{1,0:T(8,128)(2,1)S(1)}, u32[]{:S(2)}, u32[]{:S(2)}) collective-permute-start(bf16[176,1024]{1,0:T(8,128)(2,1)S(1)} %halo_keys.3.refs_1_), channel_id=1, source_target_pairs={{0,1},{1,2},{2,3},{3,0},{4,5},{5,6},{6,7},{7,4},{8,9},{9,10},{10,1... | collective-permute-start | bytes 1081352 | tf_op jit(solution)/shard_map/ppermute | solution.py:389
  46.2 11.5 %collective-permute-start.11 = (bf16[176,1024]{1,0:T(8,128)(2,1)S(1)}, bf16[176,1024]{1,0:T(8,128)(2,1)S(1)}, u32[]{:S(2)}, u32[]{:S(2)}) collective-permute-start(bf16[176,1024]{1,0:T(8,128)(2,1)S(1)} %halo_keys.3.refs_1_), channel_id=1, source_target_pairs={{0,3},{1,0},{2,1},{3,2},{4,7},{5,4},{6,5},{7,6},{8,11},{9,8},{10,9... | collective-permute-start | bytes 1081352 | tf_op jit(solution)/shard_map/ppermute | solution.py:390
  49.3 14.6 %collective-permute-start.8 = (bf16[96,1024]{1,0:T(8,128)(2,1)S(1)}, bf16[96,1024]{1,0:T(8,128)(2,1)S(1)}, u32[]{:S(2)}, u32[]{:S(2)}) collective-permute-start(bf16[96,1024]{1,0:T(8,128)(2,1)S(1)} %slice.26), channel_id=1, source_target_pairs={{0,1},{1,2},{2,3},{3,0},{4,5},{5,6},{6,7},{7,4},{8,9},{9,10},{10,1... | collective-permute-start | bytes 589832 | tf_op jit(solution)/shard_map/ppermute | solution.py:391
  50.2 13.7 %collective-permute-start.9 = (bf16[80,1024]{1,0:T(8,128)(2,1)S(1)}, bf16[80,1024]{1,0:T(8,128)(2,1)S(1)}, u32[]{:S(2)}, u32[]{:S(2)}) collective-permute-start(bf16[80,1024]{1,0:T(8,128)(2,1)S(1)} %slice.27), channel_id=1, source_target_pairs={{0,3},{1,0},{2,1},{3,2},{4,7},{5,4},{6,5},{7,6},{8,11},{9,8},{10,9... | collective-permute-start | bytes 491528 | tf_op jit(solution)/shard_map/ppermute | solution.py:392
  57.5 9.7 %collective-permute-start.12 = (bf16[96,1024]{1,0:T(8,128)(2,1)S(1)}, bf16[96,1024]{1,0:T(8,128)(2,1)S(1)}, u32[]{:S(2)}, u32[]{:S(2)}) collective-permute-start(bf16[96,1024]{1,0:T(8,128)(2,1)S(1)} %slice.28), channel_id=1, source_target_pairs={{0,1},{1,2},{2,3},{3,0},{4,5},{5,6},{6,7},{7,4},{8,9},{9,10},{10,1... | collective-permute-start | bytes 589832 | tf_op jit(solution)/shard_map/ppermute | solution.py:391
  57.7 9.5 %collective-permute-start.13 = (bf16[80,1024]{1,0:T(8,128)(2,1)S(1)}, bf16[80,1024]{1,0:T(8,128)(2,1)S(1)}, u32[]{:S(2)}, u32[]{:S(2)}) collective-permute-start(bf16[80,1024]{1,0:T(8,128)(2,1)S(1)} %slice.29), channel_id=1, source_target_pairs={{0,3},{1,0},{2,1},{3,2},{4,7},{5,4},{6,5},{7,6},{8,11},{9,8},{10,9... | collective-permute-start | bytes 491528 | tf_op jit(solution)/shard_map/ppermute | solution.py:392
  60.4 6.9 %slice-start = ((s8[5767168]{0:T(1024)(128)(4,1)}), s8[4194304]{0:T(1024)(128)(4,1)S(1)}, s32[]{:S(2)}) async-start(s8[5767168]{0:T(1024)(128)(4,1)} %bitcast.6), calls=%async_computation.1 | async-start | bytes 8388608
  63.8 3.4 %slice-start.1 = ((s8[5767168]{0:T(1024)(128)(4,1)}), s8[1572864]{0:T(1024)(128)(4,1)S(1)}, s32[]{:S(2)}) async-start(s8[5767168]{0:T(1024)(128)(4,1)} %bitcast.6), calls=%async_computation.2 | async-start | bytes 3145728
  63.8 3.4 %copy-start.4 = (s32[256]{0:T(256)S(1)}, s32[256]{0:T(256)}, u32[]{:S(2)}) copy-start(s32[256]{0:T(256)} %param.17) | copy-start | bytes 3076

commit v4 on v3

--- a/solution.py
+++ b/solution.py
@@ -139,22 +139,19 @@
         ],
         out_shape=[jax.ShapeDtypeStruct(shape, BF16) for shape in outs],
         compiler_params=pltpu.CompilerParams(vmem_limit_bytes=28 << 20),
-        cost_estimate=pl.CostEstimate(flops=flops, bytes_accessed=6 << 20, transcendentals=0),
+        cost_estimate=pl.CostEstimate(flops=flops // 1, bytes_accessed=1 << 20, transcendentals=0),
         name=name,
     )(*[pltpu.with_memory_space_constraint(v, pltpu.HBM) for v in args])
 
 
-def prepare_block(kv_refs, first, label, keys, values, base):
-    pack = kv_refs[0].shape[1]
+def prepare_block(kv_ref, first, label, keys, values, base):
     rows = label_rows(label)
     extra = VAUG - HD
     ones = (lax.broadcasted_iota(jnp.int32, (extra, KB), 0) == 0).astype(F32)
     for h in range(keys.shape[0]):
-        kv_ref = kv_refs[(first + h) // pack]
-        place = (first + h) % pack
-        block = jnp.concatenate([kv_ref[0, place, :, pl.ds(base, KB)].astype(F32), rows], axis=0)
+        block = jnp.concatenate([kv_ref[0, first + h, :, pl.ds(base, KB)].astype(F32), rows], axis=0)
         keys[h, pl.ds(base, KB), :] = block.astype(BF16).T
-        block = jnp.concatenate([kv_ref[1, place, :, pl.ds(base, KB)].astype(F32), ones], axis=0)
+        block = jnp.concatenate([kv_ref[1, first + h, :, pl.ds(base, KB)].astype(F32), ones], axis=0)
         values[h, :, pl.ds(base, KB)] = block.astype(BF16)
 
 
@@ -178,12 +175,11 @@
         top[first + h : first + h + 1, span] = new[h]
 
 
-def own_kernel(sseg_ref, seg_ref, q_ref, *refs):
-    *kv_refs, acc_ref, top_ref, keys, values = refs
+def own_kernel(sseg_ref, seg_ref, q_ref, kv_ref, acc_ref, top_ref, keys, values):
     count = seg_ref.shape[1]
     seg = seg_ref[...]
     for b in range(count // KB):
-        prepare_block(kv_refs, 0, seg[:, b * KB : (b + 1) * KB], keys, values, b * KB)
+        prepare_block(kv_ref, 0, seg[:, b * KB : (b + 1) * KB], keys, values, b * KB)
     acc_ref[...] = jnp.zeros_like(acc_ref)
     top_ref[...] = jnp.full_like(top_ref, -BIG)
 
@@ -201,12 +197,40 @@
     lax.fori_loop(0, count // QB, block, 0)
 
 
+def neighbour(first, follows, plan_ref, sseg_ref, kv_ref, q_ref, keys, values, acc, top):
+    count = q_ref.shape[2]
+    last = sseg_ref[0, count - 1]
+    begin = jnp.where(follows == 1, 0, count - plan_ref[0, 0])
+    end = jnp.where(follows == 1, plan_ref[0, 1], count)
+    image = jnp.where(follows == 1, last, 0)
+    token = lax.broadcasted_iota(jnp.int32, (1, KB), 1)
+
+    def block(k, carry):
+        base = pl.multiple_of(k * KB, KB)
+        label = jnp.where((token + base >= begin) & (token + base < end), image, -1)
+        prepare_block(kv_ref, first, label, keys, values, base)
+
+        def inner(b, c):
+            q_base = pl.multiple_of(b * QB, QB)
+
+            @pl.when(sseg_ref[0, q_base + follows * (QB - 1)] == image)
+            def _():
+                attend(first, q_ref, keys, values, acc, top, q_base, base)
+
+            return c
+
+        return lax.fori_loop(0, count // QB, inner, carry)
+
+    lax.fori_loop(begin // KB, (end + KB - 1) // KB, block, 0)
+
+
 def own_call(seg, q, kv):
     heads, _, count = q.shape
     vmem = pl.BlockSpec(memory_space=pltpu.VMEM)
+    smem = pl.BlockSpec(memory_space=pltpu.SMEM)
     return pl.pallas_call(
         own_kernel,
-        in_specs=[pl.BlockSpec(memory_space=pltpu.SMEM)] + [vmem] * (2 + len(kv)),
+        in_specs=[smem] + [vmem] * 3,
         out_specs=[vmem, vmem],
         out_shape=[
             jax.ShapeDtypeStruct((heads, VAUG, count), F32),
@@ -214,79 +238,61 @@
         ],
         scratch_shapes=[pltpu.VMEM((heads, count, AUG), BF16), pltpu.VMEM((heads, VAUG, count), BF16)],
         compiler_params=pltpu.CompilerParams(vmem_limit_bytes=20 << 20),
-        cost_estimate=pl.CostEstimate(flops=8 << 30, bytes_accessed=8 << 20, transcendentals=4 << 20),
+        cost_estimate=pl.CostEstimate(flops=32 << 28, bytes_accessed=1 << 20, transcendentals=0),
         name="own_keys",
-    )(seg, seg, q, *kv)
-
-
-def halo_kernel(first, plan_ref, sseg_ref, q_ref, acc_in, top_in, before_ref, after_ref, out_ref, acc, top, keys, values):
-    count = q_ref.shape[2]
+    )(seg, seg, q, kv)
+
+
+def near_kernel(plan_ref, sseg_ref, q_ref, acc_in, top_in, kv_ref, acc_ref, top_ref, keys, values):
+    acc_ref[...] = acc_in[...]
+    top_ref[...] = top_in[...]
+    neighbour(0, 1 - plan_ref[0, 2], plan_ref, sseg_ref, kv_ref, q_ref, keys, values, acc_ref, top_ref)
+
+
+def near_call(plan, seg, q, acc, top, kv):
+    heads, _, count = q.shape
+    vmem = pl.BlockSpec(memory_space=pltpu.VMEM)
+    smem = pl.BlockSpec(memory_space=pltpu.SMEM)
+    return pl.pallas_call(
+        near_kernel,
+        in_specs=[smem, smem, vmem, vmem, vmem, vmem],
+        out_specs=[vmem, vmem],
+        out_shape=[jax.ShapeDtypeStruct(acc.shape, F32), jax.ShapeDtypeStruct(top.shape, F32)],
+        scratch_shapes=[pltpu.VMEM((heads, count, AUG), BF16), pltpu.VMEM((heads, VAUG, count), BF16)],
+        compiler_params=pltpu.CompilerParams(vmem_limit_bytes=20 << 20),
+        cost_estimate=pl.CostEstimate(flops=1 << 28, bytes_accessed=1 << 20, transcendentals=0),
+        name="near_keys",
+    )(plan, seg, q, acc, top, kv)
+
+
+def far_kernel(first, plan_ref, sseg_ref, q_ref, acc_in, top_in, kv_ref, out_ref, acc, top, keys, values):
     heads = keys.shape[0]
     acc[...] = acc_in[first : first + heads]
     top[...] = top_in[...]
-    lead, trail = plan_ref[0, 0], plan_ref[0, 1]
-    last = sseg_ref[0, count - 1]
-    token = lax.broadcasted_iota(jnp.int32, (1, KB), 1)
-
-    def before_block(k, carry):
-        base = pl.multiple_of(k * KB, KB)
-        label = jnp.where(token + base >= count - lead, 0, -1)
-        prepare_block([before_ref], first, label, keys, values, base)
-
-        def inner(b, c):
-            q_base = pl.multiple_of(b * QB, QB)
-
-            @pl.when(sseg_ref[0, q_base] == 0)
-            def _():
-                attend(first, q_ref, keys, values, acc, top, q_base, base)
-
-            return c
-
-        return lax.fori_loop(0, count // QB, inner, carry)
-
-    lax.fori_loop((count - lead) // KB, count // KB, before_block, 0)
-
-    def after_block(k, carry):
-        base = pl.multiple_of(k * KB, KB)
-        label = jnp.where(token + base < trail, last, -1)
-        prepare_block([after_ref], first, label, keys, values, base)
-
-        def inner(b, c):
-            q_base = pl.multiple_of(b * QB, QB)
-
-            @pl.when(sseg_ref[0, q_base + QB - 1] == last)
-            def _():
-                attend(first, q_ref, keys, values, acc, top, q_base, base)
-
-            return c
-
-        return lax.fori_loop(0, count // QB, inner, carry)
-
-    lax.fori_loop(0, (trail + KB - 1) // KB, after_block, 0)
+    neighbour(first, plan_ref[0, 2], plan_ref, sseg_ref, kv_ref, q_ref, keys, values, acc, top)
     for h in range(heads):
         out_ref[pl.ds(h * HD, HD), :] = (acc[h, :HD, :] / acc[h, HD : HD + 1, :]).astype(BF16)
 
 
-def halo_call(first, plan, seg, q, acc, top, before, after):
+def far_call(first, plan, seg, q, acc, top, kv):
     count = q.shape[2]
-    heads = PACK
     vmem = pl.BlockSpec(memory_space=pltpu.VMEM)
     smem = pl.BlockSpec(memory_space=pltpu.SMEM)
     return pl.pallas_call(
-        functools.partial(halo_kernel, first),
-        in_specs=[smem, smem, vmem, vmem, vmem, vmem, vmem],
+        functools.partial(far_kernel, first),
+        in_specs=[smem, smem, vmem, vmem, vmem, vmem],
         out_specs=vmem,
-        out_shape=jax.ShapeDtypeStruct((heads * HD, count), BF16),
+        out_shape=jax.ShapeDtypeStruct((PACK * HD, count), BF16),
         scratch_shapes=[
-            pltpu.VMEM((heads, VAUG, count), F32),
+            pltpu.VMEM((PACK, VAUG, count), F32),
             pltpu.VMEM(top.shape, F32),
-            pltpu.VMEM((heads, count, AUG), BF16),
-            pltpu.VMEM((heads, VAUG, count), BF16),
+            pltpu.VMEM((PACK, count, AUG), BF16),
+            pltpu.VMEM((PACK, VAUG, count), BF16),
         ],
         compiler_params=pltpu.CompilerParams(vmem_limit_bytes=20 << 20),
-        cost_estimate=pl.CostEstimate(flops=3 << 30, bytes_accessed=8 << 20, transcendentals=4 << 20),
-        name="halo_keys",
-    )(plan, seg, q, acc, top, before, after)
+        cost_estimate=pl.CostEstimate(flops=12 << 28, bytes_accessed=1 << 20, transcendentals=0),
+        name="far_keys",
+    )(plan, seg, q, acc, top, kv)
 
 
 def gather_kernel(parts, rows, base_ref, *refs):
@@ -310,7 +316,7 @@
         out_specs=vmem,
         out_shape=jax.ShapeDtypeStruct(base.shape, F32),
         compiler_params=pltpu.CompilerParams(vmem_limit_bytes=16 << 20),
-        cost_estimate=pl.CostEstimate(flops=flops, bytes_accessed=4 << 20, transcendentals=0),
+        cost_estimate=pl.CostEstimate(flops=flops // 32, bytes_accessed=1 << 16, transcendentals=0),
         name="output",
     )(base, *heads_parts, *w_parts)
 
@@ -384,13 +390,17 @@
     return [(i, (i + shift) % size) for i in range(size)]
 
 
-def around(block, axis):
-    half = -(-block.shape[0] // 32) * 16
-    left = lax.ppermute(block, axis, ring(axis, 1))
-    right = lax.ppermute(block, axis, ring(axis, -1))
-    far_top = lax.ppermute(left[:half], axis, ring(axis, 1))
-    far_end = lax.ppermute(right[half:], axis, ring(axis, -1))
-    return left, right, far_top, far_end
+def swaps(firsts):
+    return [pair for i in firsts for pair in ((i, i + 1), (i + 1, i))]
+
+
+def beside(block, axis):
+    return lax.ppermute(block, axis, ring(axis, 1)), lax.ppermute(block, axis, ring(axis, -1))
+
+
+def beyond(left, right, axis):
+    half = -(-left.shape[0] // 32) * 16
+    return lax.ppermute(left[:half], axis, ring(axis, 1)), lax.ppermute(right[half:], axis, ring(axis, -1))
 
 
 def on_device(patches, segment_ids, grid_sides, split_plan, owner_dev, dest_row, ln_gain, ln_bias, w_qkv, w_out, w_proj):
@@ -402,33 +412,34 @@
     lanes = 2 * rows_out // peers
     seg = segment_ids.reshape(1, count)
     table = jnp.asarray(rope_table())
-    w_left, w_right, w_top, w_end = around(w_out, "tp")
+    w_left, w_right = beside(w_out, "tp")
+    w_top, w_end = beyond(w_left, w_right, "tp")
     inputs = (patches, seg, grid_sides.reshape(1, count), split_plan, ln_gain, ln_bias, w_qkv, table)
     (kv,) = qkv_call(kv_kernel, "keys_values", [(1, 0, local), (2, 0, local)], [(2, heads, HD, count)], *inputs)
-    up = [(i, i + 1) for i in range(peers - 1)]
-    down = [(j, i) for i, j in up]
-    before = lax.ppermute(kv, "req", up)
-    after = lax.ppermute(kv, "req", down)
+    far = lax.ppermute(kv, "req", swaps(range(1, peers - 1, 2)))
+    near = lax.ppermute(kv, "req", swaps(range(0, peers - 1, 2)))
+    parity = (lax.axis_index("req") % 2).astype(jnp.int32).reshape(1, 1)
+    plan = jnp.concatenate([split_plan, parity], axis=1)
     (q,) = qkv_call(q_kernel, "queries", [(0, 0, local)], [(heads, AUG, count)], *inputs)
-    acc, top = own_call(seg, q, [kv])
-    before, after, w_left, w_right, w_top, w_end = lax.optimization_barrier(
-        (before, after, w_left, w_right, w_top, w_end)
-    )
+    acc, top = own_call(seg, q, kv)
+    acc, top = near_call(plan, seg, q, acc, top, near)
+    far, w_left, w_right, w_top, w_end = lax.optimization_barrier((far, w_left, w_right, w_top, w_end))
     pack = PACK * HD
-    w_far = [w_top, w_end]
     lows = list(range(0, local, pack))
     outs, sides = [], []
     for index in range(len(lows)):
         if outs:
             acc, outs[-1] = lax.optimization_barrier((acc, outs[-1]))
-        outs.append(halo_call(index * PACK, split_plan, seg, q, acc, top, before, after))
-        sides.append(around(outs[-1], "tp"))
+        outs.append(far_call(index * PACK, plan, seg, q, acc, top, far))
+        sides.append(beside(outs[-1], "tp"))
+    w_far = [w_top, w_end]
     terms = [(part, w_out, low) for part, low in zip(outs, lows)]
     base = patches
-    for index, (left, right, far_top, far_end) in enumerate(sides):
+    for index, (left, right) in enumerate(sides):
+        opposite = beyond(left, right, "tp")
         terms += [(left, w_left, lows[index]), (right, w_right, lows[index])]
         base = gather_call(base, *zip(*terms))
-        terms = [(far_top, w_far[index], 0), (far_end, w_far[index], far_top.shape[0])]
+        terms = [(opposite[0], w_far[index], 0), (opposite[1], w_far[index], opposite[0].shape[0])]
     within = jnp.arange(rows_out, dtype=jnp.int32) % lanes
     slot = (owner_dev * lanes + within).reshape(1, rows_out)
     send = project_call(

time: 113 us -> 113 us (level)
  blocking collectives: 38.8 us -> 43.2 us
  waiting for transfers between devices: 11.5 us -> 7.64 us
  Pallas kernels: 36.6 us -> 38.1 us
  starting transfers between devices: 24.5 us -> 23.2 us
    all_to_all x1, blocking collectives: 38.8 us -> 43.2 us  [on_device(): lax.all_to_all(send.reshape(peers, lanes, cols), 'req', split_axis=0, con...]
    ppermute x14, waiting for transfers between devices: 11.5 us -> 7.64 us  [the longest x3 7.61 us: beside(): lax.ppermute(block, axis, ring(axis, 1))]
    pallas_call x3 -> x4, Pallas kernels: 11.4 us -> 12.9 us  [the longest x1 5.26 us: near_call(): pl.pallas_call(near_kernel, in_specs=[smem, smem, vmem, vmem, vmem, vmem]...]
    ppermute x14, starting transfers between devices: 24.5 us -> 23.2 us  [the longest x3 6.98 us: beyond(): lax.ppermute(right[half:], axis, ring(axis, -1))]
  transfers between devices with their start and end apart: 14 -> 14, of which waited for: 5 -> 3; matrix products, arithmetic and copies ran while one was open for 0% -> 0% of each run, Pallas kernels for 25% -> 27%
where the time goes in v4:
time: 113 us
  blocking collectives  43.2 us (38%)
  Pallas kernels  38.1 us (34%)
  starting transfers between devices  23.2 us (21%)
  waiting for transfers between devices  7.64 us (7%)
    all_to_all x1, blocking collectives, on_device(): lax.all_to_all(send.reshape(peers, lanes, cols), 'req', split_axis=0, con...  43.2 us
    pallas_call x2, Pallas kernels, qkv_call(): pl.pallas_call(kernel, grid=(count // TILE,), in_specs=[pl.BlockSpec(memo...  12.7 us
    ppermute x3, waiting for transfers between devices, beside(): lax.ppermute(block, axis, ring(axis, 1))  7.61 us
    ppermute x3, starting transfers between devices, beyond(): lax.ppermute(right[half:], axis, ring(axis, -1))  6.98 us
    pallas_call x2, Pallas kernels, gather_call(): pl.pallas_call(functools.partial(gather_kernel, parts, rows), in_specs=[v...  6.79 us
    ppermute x3, starting transfers between devices, beside(): lax.ppermute(block, axis, ring(axis, -1))  5.81 us
    pallas_call x1, Pallas kernels, near_call(): pl.pallas_call(near_kernel, in_specs=[smem, smem, vmem, vmem, vmem, vmem]...  5.26 us
    pallas_call x1, Pallas kernels, own_call(): pl.pallas_call(own_kernel, in_specs=[smem] + [vmem] * 3, out_specs=[vmem,...  4.51 us
  transfers between devices with their start and end apart: 14, of which 3 were waited for; matrix products, arithmetic and copies ran while one was open for 0% of the time, Pallas kernels for 27%

profile of v4, /device:TPU:1, one launch (start us, length us, event | category | flops | bytes accessed | tf_op | source)
XLA Modules:
  0.0 112.7 jit_solution(2037426015748558247)
XLA Ops:
  0.0 2.1 %collective-permute-start.2 = (bf16[352,1408]{1,0:T(8,128)(2,1)}, bf16[352,1408]{1,0:T(8,128)(2,1)S(1)}, u32[]{:S(2)}, u32[]{:S(2)}) collective-permute-start(bf16[352,1408]{1,0:T(8,128)(2,1)} %refs_5_.1), channel_id=1, source_target_pairs={{0,1},{1,2},{2,3},{3,0},{4,5},{5,6},{6,7},{7,4},{8,9},{9,10},{10,1... | collective-permute-start | bytes 2973704 | tf_op jit(solution)/shard_map/ppermute | solution.py:398
  2.1 1.4 %collective-permute-start.3 = (bf16[352,1408]{1,0:T(8,128)(2,1)}, bf16[352,1408]{1,0:T(8,128)(2,1)S(1)}, u32[]{:S(2)}, u32[]{:S(2)}) collective-permute-start(bf16[352,1408]{1,0:T(8,128)(2,1)} %refs_5_.1), channel_id=1, source_target_pairs={{0,3},{1,0},{2,1},{3,2},{4,7},{5,4},{6,5},{7,6},{8,11},{9,8},{10,9... | collective-permute-start | bytes 2973704 | tf_op jit(solution)/shard_map/ppermute | solution.py:398
  3.6 6.9 %keys_values.1.kv_ref = bf16[2,4,88,1024]{3,2,1,0:T(8,128)(2,1)S(1)} custom-call(s32[1,2]{1,0:T(1,128)} %plan_ref.3, bf16[176,192]{1,0:T(8,128)(2,1)} %constant.37.clone.table_ref, s32[1,1024]{1,0:T(1,128)} %bitcast.10, s32[1,1024]{1,0:T(1,128)} %bitcast.11, s32[1,1024]{1,0:T(1,128)} %bitcast.22, bf16[1024,1408]{1,0:T(8,128)(2,1)} %base_ref.1, ...), custom_call_target="tpu_custom_call" | custom-call | flops 2030043136 | bytes 1048576 | tf_op jit(solution)/shard_map/keys_values/pallas_call | solution.py:123
  10.5 3.0 %collective-permute-start = (bf16[2,4,88,1024]{3,2,1,0:T(8,128)(2,1)S(1)}, bf16[2,4,88,1024]{3,2,1,0:T(8,128)(2,1)}, u32[]{:S(2)}, u32[]{:S(2)}) collective-permute-start(bf16[2,4,88,1024]{3,2,1,0:T(8,128)(2,1)S(1)} %keys_values.1.kv_ref), channel_id=1, source_target_pairs={{0,4},{4,0},{8,12},{12,8},{16,20},{20,16},{24,28},{28,24},{32,36},... | collective-permute-start | bytes 4325384 | tf_op jit(solution)/shard_map/ppermute | solution.py:420
  13.5 1.9 %collective-permute-start.1 = (bf16[2,4,88,1024]{3,2,1,0:T(8,128)(2,1)S(1)}, bf16[2,4,88,1024]{3,2,1,0:T(8,128)(2,1)}, u32[]{:S(2)}, u32[]{:S(2)}) collective-permute-start(bf16[2,4,88,1024]{3,2,1,0:T(8,128)(2,1)S(1)} %keys_values.1.kv_ref), channel_id=1, source_target_pairs={{4,8},{8,4},{12,16},{16,12},{20,24},{24,20},{28,32},{32,28},{36,40... | collective-permute-start | bytes 4325384 | tf_op jit(solution)/shard_map/ppermute | solution.py:419
  15.4 5.8 %queries.1.q_ref = bf16[4,128,1024]{2,1,0:T(8,128)(2,1)S(1)} custom-call(s32[1,2]{1,0:T(1,128)} %plan_ref.3, bf16[176,192]{1,0:T(8,128)(2,1)} %constant.37.clone.table_ref, s32[1,1024]{1,0:T(1,128)} %bitcast.12, s32[1,1024]{1,0:T(1,128)} %bitcast.13, s32[1,1024]{1,0:T(1,128)} %bitcast.23, bf16[1024,1408]{1,0:T(8,128)(2,1)} %base_ref.1, f32[1408]{0:T(1024)} %gain_ref.3, ...), custom_call_target="tpu_custom_call" | custom-call | flops 1015021568 | bytes 1048576 | tf_op jit(solution)/shard_map/queries/pallas_call | solution.py:123
  21.3 2.1 %collective-permute-done.2.refs_6_ = bf16[352,1408]{1,0:T(8,128)(2,1)S(1)} collective-permute-done((bf16[352,1408]{1,0:T(8,128)(2,1)}, bf16[352,1408]{1,0:T(8,128)(2,1)S(1)}, u32[]{:S(2)}, u32[]{:S(2)}) %collective-permute-start.2) | collective-permute-done | bytes 991264 | tf_op jit(solution)/shard_map/ppermute | solution.py:398
  23.4 1.6 %collective-permute-start.4 = (bf16[176,1408]{1,0:T(8,128)(2,1)S(1)}, bf16[176,1408]{1,0:T(8,128)(2,1)S(1)}, u32[]{:S(2)}, u32[]{:S(2)}) collective-permute-start(bf16[176,1408]{1,0:T(8,128)(2,1)S(1)} %slice.24), channel_id=1, source_target_pairs={{0,1},{1,2},{2,3},{3,0},{4,5},{5,6},{6,7},{7,4},{8,9},{9,10},{10,1... | collective-permute-start | bytes 1486856 | tf_op jit(solution)/shard_map/ppermute | solution.py:403
  25.1 1.7 %collective-permute-start.5 = (bf16[176,1408]{1,0:T(8,128)(2,1)S(1)}, bf16[176,1408]{1,0:T(8,128)(2,1)S(1)}, u32[]{:S(2)}, u32[]{:S(2)}) collective-permute-start(bf16[176,1408]{1,0:T(8,128)(2,1)S(1)} %slice.25), channel_id=1, source_target_pairs={{0,3},{1,0},{2,1},{3,2},{4,7},{5,4},{6,5},{7,6},{8,11},{9,8},{10,9... | collective-permute-start | bytes 1486856 | tf_op jit(solution)/shard_map/ppermute | solution.py:403
  26.8 4.5 %own_keys.1 = (f32[4,96,1024]{2,1,0:T(8,128)S(1)}, f32[8,1024]{1,0:T(8,128)S(1)}) custom-call(s32[1,1024]{1,0:T(1,128)S(1)} %bitcast.14, s32[1,1024]{1,0:T(1,128)S(1)} %bitcast.15, bf16[4,128,1024]{2,1,0:T(8,128)(2,1)S(1)} %queries.1.q_ref, bf16[2,4,88,1024]{3,2,1,0:T(8,128)(2,1)S(1)} %keys_values.1.kv_ref), custom_call_target="tpu_custom_call" | custom-call | flops 8589934592 | bytes 1048576 | tf_op jit(solution)/shard_map/own_keys/pallas_call | solution.py:231
  31.4 5.3 %near_keys.1 = (f32[4,96,1024]{2,1,0:T(8,128)S(1)}, f32[8,1024]{1,0:T(8,128)S(1)}) custom-call(s32[1,3]{1,0:T(1,128)S(1)} %pad_add_fusion.plan_ref, s32[1,1024]{1,0:T(1,128)S(1)} %bitcast.16, bf16[4,128,1024]{2,1,0:T(8,128)(2,1)S(1)} %queries.1.q_ref, f32[4,96,1024]{2,1,0:T(8,128)S(1)} %get-tuple-element.16.acc_in, f32[8,1024]{1,0:T(8,128)S(1)} %get-tuple-element.17.top_in, ...), custom_call_target="tpu_custom_call" | custom-call | flops 268435456 | bytes 1048576 | tf_op jit(solution)/shard_map/near_keys/pallas_call | solution.py:256
  36.7 1.5 %far_keys.2.refs_0_ = bf16[176,1024]{1,0:T(8,128)(2,1)S(1)} custom-call(s32[1,3]{1,0:T(1,128)S(1)} %pad_add_fusion.plan_ref, s32[1,1024]{1,0:T(1,128)S(1)} %bitcast.17, bf16[4,128,1024]{2,1,0:T(8,128)(2,1)S(1)} %queries.1.q_ref, f32[4,96,1024]{2,1,0:T(8,128)S(1)} %get-tuple-element.22.acc_in, f32[8,1024]{1,0:T(8,128)S(1)} %get-tuple-element.19.top_in, ...), custom_call_target="tpu_custom_call" | custom-call | flops 3221225472 | bytes 1048576 | tf_op jit(solution)/shard_map/far_keys/pallas_call | solution.py:281
  38.2 1.0 collective-permute-start.6
  39.2 1.7 %collective-permute-start.7 = (bf16[176,1024]{1,0:T(8,128)(2,1)S(1)}, bf16[176,1024]{1,0:T(8,128)(2,1)S(1)}, u32[]{:S(2)}, u32[]{:S(2)}) collective-permute-start(bf16[176,1024]{1,0:T(8,128)(2,1)S(1)} %far_keys.2.refs_0_), channel_id=1, source_target_pairs={{0,3},{1,0},{2,1},{3,2},{4,7},{5,4},{6,5},{7,6},{8,11},{9,8},{10,9... | collective-permute-start | bytes 1081352 | tf_op jit(solution)/shard_map/ppermute | solution.py:398
  40.9 1.6 %far_keys.3.refs_1_ = bf16[176,1024]{1,0:T(8,128)(2,1)S(1)} custom-call(s32[1,3]{1,0:T(1,128)S(1)} %pad_add_fusion.plan_ref, s32[1,1024]{1,0:T(1,128)S(1)} %bitcast.18, bf16[4,128,1024]{2,1,0:T(8,128)(2,1)S(1)} %queries.1.q_ref, f32[4,96,1024]{2,1,0:T(8,128)S(1)} %get-tuple-element.22.acc_in, f32[8,1024]{1,0:T(8,128)S(1)} %get-tuple-element.19.top_in, ...), custom_call_target="tpu_custom_call" | custom-call | flops 3221225472 | bytes 1048576 | tf_op jit(solution)/shard_map/far_keys/pallas_call | solution.py:281
  42.7 2.7 %collective-permute-start.11 = (bf16[176,1024]{1,0:T(8,128)(2,1)S(1)}, bf16[176,1024]{1,0:T(8,128)(2,1)S(1)}, u32[]{:S(2)}, u32[]{:S(2)}) collective-permute-start(bf16[176,1024]{1,0:T(8,128)(2,1)S(1)} %far_keys.3.refs_1_), channel_id=1, source_target_pairs={{0,3},{1,0},{2,1},{3,2},{4,7},{5,4},{6,5},{7,6},{8,11},{9,8},{10,9... | collective-permute-start | bytes 1081352 | tf_op jit(solution)/shard_map/ppermute | solution.py:398
  46.3 2.5 %collective-permute-start.9 = (bf16[80,1024]{1,0:T(8,128)(2,1)S(1)}, bf16[80,1024]{1,0:T(8,128)(2,1)S(1)}, u32[]{:S(2)}, u32[]{:S(2)}) collective-permute-start(bf16[80,1024]{1,0:T(8,128)(2,1)S(1)} %slice.27), channel_id=1, source_target_pairs={{0,3},{1,0},{2,1},{3,2},{4,7},{5,4},{6,5},{7,6},{8,11},{9,8},{10,9... | collective-permute-start | bytes 491528 | tf_op jit(solution)/shard_map/ppermute | solution.py:403
  48.8 5.1 %collective-permute-done.10.refs_2_ = bf16[176,1024]{1,0:T(8,128)(2,1)S(1)} collective-permute-done((bf16[176,1024]{1,0:T(8,128)(2,1)S(1)}, bf16[176,1024]{1,0:T(8,128)(2,1)S(1)}, u32[]{:S(2)}, u32[]{:S(2)}) %collective-permute-start.10) | collective-permute-done | bytes 360480 | tf_op jit(solution)/shard_map/ppermute | solution.py:398
  54.0 2.7 %collective-permute-start.13 = (bf16[80,1024]{1,0:T(8,128)(2,1)S(1)}, bf16[80,1024]{1,0:T(8,128)(2,1)S(1)}, u32[]{:S(2)}, u32[]{:S(2)}) collective-permute-start(bf16[80,1024]{1,0:T(8,128)(2,1)S(1)} %slice.29), channel_id=1, source_target_pairs={{0,3},{1,0},{2,1},{3,2},{4,7},{5,4},{6,5},{7,6},{8,11},{9,8},{10,9... | collective-permute-start | bytes 491528 | tf_op jit(solution)/shard_map/ppermute | solution.py:403
  56.8 3.5 %output.2.base_ref = f32[1024,1408]{1,0:T(8,128)S(1)} custom-call(bf16[1024,1408]{1,0:T(8,128)(2,1)S(1)} %copy-done, bf16[176,1024]{1,0:T(8,128)(2,1)S(1)} %far_keys.2.refs_0_, bf16[176,1024]{1,0:T(8,128)(2,1)S(1)} %far_keys.3.refs_1_, bf16[176,1024]{1,0:T(8,128)(2,1)S(1)} %collective-permute-done.6.refs_2_, ...), custom_call_target="tpu_custom_call" | custom-call | flops 63438848 | bytes 65536 | tf_op jit(solution)/shard_map/output/pallas_call | solution.py:313
  60.3 3.3 %output.3.base_ref = f32[1024,1408]{1,0:T(8,128)S(1)} custom-call(f32[1024,1408]{1,0:T(8,128)S(1)} %output.2.base_ref, bf16[96,1024]{1,0:T(8,128)(2,1)S(1)} %collective-permute-done.8.refs_0_, bf16[80,1024]{1,0:T(8,128)(2,1)S(1)} %collective-permute-done.9.refs_1_, bf16[176,1024]{1,0:T(8,128)(2,1)S(1)} %collective-permute-done.10.refs_2_, ...), custom_call_target="tpu_custom_call" | custom-call | flops 47579136 | bytes 65536 | tf_op jit(solution)/shard_map/output/pallas_call | solution.py:313
  63.7 3.6 %project.1 = bf16[512,640]{1,0:T(8,128)(2,1)S(1)} custom-call(s32[1,256]{1,0:T(1,128)S(1)} %bitcast.19, s32[1,256]{1,0:T(1,128)S(1)} %bitcast.20, f32[1024,1408]{1,0:T(8,128)S(1)} %output.3.base_ref, bf16[96,1024]{1,0:T(8,128)(2,1)S(1)} %collective-permute-done.12.refs_0_, bf16[80,1024]{1,0:T(8,128)(2,1)S(1)} %collective-permute-done.13.refs_1_, ...), custom_call_target="tpu_custom_call" | custom-call | flops 3221225472 | bytes 8388608 | tf_op jit(solution)/shard_map/project/pallas_call | solution.py:356
  67.3 43.2 %all_to_all.5 = bf16[64,8,640]{2,1,0:T(8,128)(2,1)} all-to-all(bf16[64,8,640]{2,1,0:T(8,128)(2,1)S(1)} %bitcast.9), channel_id=1, replica_groups=mesh['req'=64,'tp'=4] {'req'}, dimensions={0} | all-to-all | bytes 1310720 | tf_op jit(solution)/shard_map/all_to_all | solution.py:449
  110.6 2.1 %place.1 = bf16[256,512]{1,0:T(8,128)(2,1)} custom-call(bf16[512,640]{1,0:T(8,128)(2,1)} %bitcast.21), custom_call_target="tpu_custom_call" | custom-call | tf_op jit(solution)/shard_map/place/pallas_call | solution.py:379
  (40 shorter events, 1.4 us)
Async XLA Ops:
  0.0 23.4 %collective-permute-start.2 = (bf16[352,1408]{1,0:T(8,128)(2,1)}, bf16[352,1408]{1,0:T(8,128)(2,1)S(1)}, u32[]{:S(2)}, u32[]{:S(2)}) collective-permute-start(bf16[352,1408]{1,0:T(8,128)(2,1)} %refs_5_.1), channel_id=1, source_target_pairs={{0,1},{1,2},{2,3},{3,0},{4,5},{5,6},{6,7},{7,4},{8,9},{9,10},{10,1... | collective-permute-start | bytes 2973704 | tf_op jit(solution)/shard_map/ppermute | solution.py:398
  2.1 22.9 %collective-permute-start.3 = (bf16[352,1408]{1,0:T(8,128)(2,1)}, bf16[352,1408]{1,0:T(8,128)(2,1)S(1)}, u32[]{:S(2)}, u32[]{:S(2)}) collective-permute-start(bf16[352,1408]{1,0:T(8,128)(2,1)} %refs_5_.1), channel_id=1, source_target_pairs={{0,3},{1,0},{2,1},{3,2},{4,7},{5,4},{6,5},{7,6},{8,11},{9,8},{10,9... | collective-permute-start | bytes 2973704 | tf_op jit(solution)/shard_map/ppermute | solution.py:398
  10.5 20.9 %collective-permute-start = (bf16[2,4,88,1024]{3,2,1,0:T(8,128)(2,1)S(1)}, bf16[2,4,88,1024]{3,2,1,0:T(8,128)(2,1)}, u32[]{:S(2)}, u32[]{:S(2)}) collective-permute-start(bf16[2,4,88,1024]{3,2,1,0:T(8,128)(2,1)S(1)} %keys_values.1.kv_ref), channel_id=1, source_target_pairs={{0,4},{4,0},{8,12},{12,8},{16,20},{20,16},{24,28},{28,24},{32,36},... | collective-permute-start | bytes 4325384 | tf_op jit(solution)/shard_map/ppermute | solution.py:420
  13.5 23.2 %collective-permute-start.1 = (bf16[2,4,88,1024]{3,2,1,0:T(8,128)(2,1)S(1)}, bf16[2,4,88,1024]{3,2,1,0:T(8,128)(2,1)}, u32[]{:S(2)}, u32[]{:S(2)}) collective-permute-start(bf16[2,4,88,1024]{3,2,1,0:T(8,128)(2,1)S(1)} %keys_values.1.kv_ref), channel_id=1, source_target_pairs={{4,8},{8,4},{12,16},{16,12},{20,24},{24,20},{28,32},{32,28},{36,40... | collective-permute-start | bytes 4325384 | tf_op jit(solution)/shard_map/ppermute | solution.py:419
  15.4 5.8 %copy-start.4 = (s32[1,2]{1,0:T(1,128)S(1)}, s32[1,2]{1,0:T(1,128)}, u32[]{:S(2)}) copy-start(s32[1,2]{1,0:T(1,128)} %plan_ref.3) | copy-start | bytes 28
  15.4 11.4 %copy-start.2 = (s32[1024]{0:T(1024)S(1)}, s32[1024]{0:T(1024)}, u32[]{:S(2)}) copy-start(s32[1024]{0:T(1024)} %param.13) | copy-start | bytes 12292
  23.4 13.2 %collective-permute-start.4 = (bf16[176,1408]{1,0:T(8,128)(2,1)S(1)}, bf16[176,1408]{1,0:T(8,128)(2,1)S(1)}, u32[]{:S(2)}, u32[]{:S(2)}) collective-permute-start(bf16[176,1408]{1,0:T(8,128)(2,1)S(1)} %slice.24), channel_id=1, source_target_pairs={{0,1},{1,2},{2,3},{3,0},{4,5},{5,6},{6,7},{7,4},{8,9},{9,10},{10,1... | collective-permute-start | bytes 1486856 | tf_op jit(solution)/shard_map/ppermute | solution.py:403
  25.1 11.6 %collective-permute-start.5 = (bf16[176,1408]{1,0:T(8,128)(2,1)S(1)}, bf16[176,1408]{1,0:T(8,128)(2,1)S(1)}, u32[]{:S(2)}, u32[]{:S(2)}) collective-permute-start(bf16[176,1408]{1,0:T(8,128)(2,1)S(1)} %slice.25), channel_id=1, source_target_pairs={{0,3},{1,0},{2,1},{3,2},{4,7},{5,4},{6,5},{7,6},{8,11},{9,8},{10,9... | collective-permute-start | bytes 1486856 | tf_op jit(solution)/shard_map/ppermute | solution.py:403
  38.2 18.6 %copy-start.5 = (s32[256]{0:T(256)S(1)}, s32[256]{0:T(256)}, u32[]{:S(2)}) copy-start(s32[256]{0:T(256)} %param.16) | copy-start | bytes 3076
  38.2 18.6 %copy-start.1 = (bf16[352,1408]{1,0:T(8,128)(2,1)S(1)}, bf16[352,1408]{1,0:T(8,128)(2,1)}, u32[]{:S(2)}) copy-start(bf16[352,1408]{1,0:T(8,128)(2,1)} %refs_5_.1) | copy-start | bytes 2973700
  38.2 7.6 %collective-permute-start.6 = (bf16[176,1024]{1,0:T(8,128)(2,1)S(1)}, bf16[176,1024]{1,0:T(8,128)(2,1)S(1)}, u32[]{:S(2)}, u32[]{:S(2)}) collective-permute-start(bf16[176,1024]{1,0:T(8,128)(2,1)S(1)} %far_keys.2.refs_0_), channel_id=1, source_target_pairs={{0,1},{1,2},{2,3},{3,0},{4,5},{5,6},{6,7},{7,4},{8,9},{9,10},{10,1... | collective-permute-start | bytes 1081352 | tf_op jit(solution)/shard_map/ppermute | solution.py:398
  39.2 7.0 %collective-permute-start.7 = (bf16[176,1024]{1,0:T(8,128)(2,1)S(1)}, bf16[176,1024]{1,0:T(8,128)(2,1)S(1)}, u32[]{:S(2)}, u32[]{:S(2)}) collective-permute-start(bf16[176,1024]{1,0:T(8,128)(2,1)S(1)} %far_keys.2.refs_0_), channel_id=1, source_target_pairs={{0,3},{1,0},{2,1},{3,2},{4,7},{5,4},{6,5},{7,6},{8,11},{9,8},{10,9... | collective-permute-start | bytes 1081352 | tf_op jit(solution)/shard_map/ppermute | solution.py:398
  40.9 15.8 %copy-start = (bf16[1024,1408]{1,0:T(8,128)(2,1)S(1)}, bf16[1024,1408]{1,0:T(8,128)(2,1)}, u32[]{:S(2)}) copy-start(bf16[1024,1408]{1,0:T(8,128)(2,1)} %base_ref.1) | copy-start | bytes 8650756
  42.6 11.3 %collective-permute-start.10 = (bf16[176,1024]{1,0:T(8,128)(2,1)S(1)}, bf16[176,1024]{1,0:T(8,128)(2,1)S(1)}, u32[]{:S(2)}, u32[]{:S(2)}) collective-permute-start(bf16[176,1024]{1,0:T(8,128)(2,1)S(1)} %far_keys.3.refs_1_), channel_id=1, source_target_pairs={{0,1},{1,2},{2,3},{3,0},{4,5},{5,6},{6,7},{7,4},{8,9},{9,10},{10,1... | collective-permute-start | bytes 1081352 | tf_op jit(solution)/shard_map/ppermute | solution.py:398
  42.7 11.3 %collective-permute-start.11 = (bf16[176,1024]{1,0:T(8,128)(2,1)S(1)}, bf16[176,1024]{1,0:T(8,128)(2,1)S(1)}, u32[]{:S(2)}, u32[]{:S(2)}) collective-permute-start(bf16[176,1024]{1,0:T(8,128)(2,1)S(1)} %far_keys.3.refs_1_), channel_id=1, source_target_pairs={{0,3},{1,0},{2,1},{3,2},{4,7},{5,4},{6,5},{7,6},{8,11},{9,8},{10,9... | collective-permute-start | bytes 1081352 | tf_op jit(solution)/shard_map/ppermute | solution.py:398
  45.8 14.5 %collective-permute-start.8 = (bf16[96,1024]{1,0:T(8,128)(2,1)S(1)}, bf16[96,1024]{1,0:T(8,128)(2,1)S(1)}, u32[]{:S(2)}, u32[]{:S(2)}) collective-permute-start(bf16[96,1024]{1,0:T(8,128)(2,1)S(1)} %slice.26), channel_id=1, source_target_pairs={{0,1},{1,2},{2,3},{3,0},{4,5},{5,6},{6,7},{7,4},{8,9},{9,10},{10,1... | collective-permute-start | bytes 589832 | tf_op jit(solution)/shard_map/ppermute | solution.py:403
  46.3 14.0 %collective-permute-start.9 = (bf16[80,1024]{1,0:T(8,128)(2,1)S(1)}, bf16[80,1024]{1,0:T(8,128)(2,1)S(1)}, u32[]{:S(2)}, u32[]{:S(2)}) collective-permute-start(bf16[80,1024]{1,0:T(8,128)(2,1)S(1)} %slice.27), channel_id=1, source_target_pairs={{0,3},{1,0},{2,1},{3,2},{4,7},{5,4},{6,5},{7,6},{8,11},{9,8},{10,9... | collective-permute-start | bytes 491528 | tf_op jit(solution)/shard_map/ppermute | solution.py:403
  53.9 9.8 %collective-permute-start.12 = (bf16[96,1024]{1,0:T(8,128)(2,1)S(1)}, bf16[96,1024]{1,0:T(8,128)(2,1)S(1)}, u32[]{:S(2)}, u32[]{:S(2)}) collective-permute-start(bf16[96,1024]{1,0:T(8,128)(2,1)S(1)} %slice.28), channel_id=1, source_target_pairs={{0,1},{1,2},{2,3},{3,0},{4,5},{5,6},{6,7},{7,4},{8,9},{9,10},{10,1... | collective-permute-start | bytes 589832 | tf_op jit(solution)/shard_map/ppermute | solution.py:403
  54.0 9.6 %collective-permute-start.13 = (bf16[80,1024]{1,0:T(8,128)(2,1)S(1)}, bf16[80,1024]{1,0:T(8,128)(2,1)S(1)}, u32[]{:S(2)}, u32[]{:S(2)}) collective-permute-start(bf16[80,1024]{1,0:T(8,128)(2,1)S(1)} %slice.29), channel_id=1, source_target_pairs={{0,3},{1,0},{2,1},{3,2},{4,7},{5,4},{6,5},{7,6},{8,11},{9,8},{10,9... | collective-permute-start | bytes 491528 | tf_op jit(solution)/shard_map/ppermute | solution.py:403
  56.8 6.9 %slice-start = ((s8[5767168]{0:T(1024)(128)(4,1)}), s8[1572864]{0:T(1024)(128)(4,1)S(1)}, s32[]{:S(2)}) async-start(s8[5767168]{0:T(1024)(128)(4,1)} %bitcast.7), calls=%async_computation.1 | async-start | bytes 3145728
  60.3 3.4 %slice-start.1 = ((s8[5767168]{0:T(1024)(128)(4,1)}), s8[4194304]{0:T(1024)(128)(4,1)S(1)}, s32[]{:S(2)}) async-start(s8[5767168]{0:T(1024)(128)(4,1)} %bitcast.7), calls=%async_computation.2 | async-start | bytes 8388608
  60.3 3.4 %copy-start.3 = (s32[256]{0:T(256)S(1)}, s32[256]{0:T(256)}, u32[]{:S(2)}) copy-start(s32[256]{0:T(256)} %param.17) | copy-start | bytes 3076

commit v5 on v4

--- a/solution.py
+++ b/solution.py
@@ -238,7 +238,7 @@
         ],
         scratch_shapes=[pltpu.VMEM((heads, count, AUG), BF16), pltpu.VMEM((heads, VAUG, count), BF16)],
         compiler_params=pltpu.CompilerParams(vmem_limit_bytes=20 << 20),
-        cost_estimate=pl.CostEstimate(flops=32 << 28, bytes_accessed=1 << 20, transcendentals=0),
+        cost_estimate=pl.CostEstimate(flops=64 << 28, bytes_accessed=1 << 20, transcendentals=0),
         name="own_keys",
     )(seg, seg, q, kv)
 
@@ -316,7 +316,7 @@
         out_specs=vmem,
         out_shape=jax.ShapeDtypeStruct(base.shape, F32),
         compiler_params=pltpu.CompilerParams(vmem_limit_bytes=16 << 20),
-        cost_estimate=pl.CostEstimate(flops=flops // 32, bytes_accessed=1 << 16, transcendentals=0),
+        cost_estimate=pl.CostEstimate(flops=flops // 8, bytes_accessed=1 << 16, transcendentals=0),
         name="output",
     )(base, *heads_parts, *w_parts)
 
@@ -413,7 +413,6 @@
     seg = segment_ids.reshape(1, count)
     table = jnp.asarray(rope_table())
     w_left, w_right = beside(w_out, "tp")
-    w_top, w_end = beyond(w_left, w_right, "tp")
     inputs = (patches, seg, grid_sides.reshape(1, count), split_plan, ln_gain, ln_bias, w_qkv, table)
     (kv,) = qkv_call(kv_kernel, "keys_values", [(1, 0, local), (2, 0, local)], [(2, heads, HD, count)], *inputs)
     far = lax.ppermute(kv, "req", swaps(range(1, peers - 1, 2)))
@@ -422,20 +421,23 @@
     plan = jnp.concatenate([split_plan, parity], axis=1)
     (q,) = qkv_call(q_kernel, "queries", [(0, 0, local)], [(heads, AUG, count)], *inputs)
     acc, top = own_call(seg, q, kv)
+    acc, w_left, w_right = lax.optimization_barrier((acc, w_left, w_right))
+    w_top, w_end = beyond(w_left, w_right, "tp")
     acc, top = near_call(plan, seg, q, acc, top, near)
-    far, w_left, w_right, w_top, w_end = lax.optimization_barrier((far, w_left, w_right, w_top, w_end))
     pack = PACK * HD
     lows = list(range(0, local, pack))
     outs, sides = [], []
     for index in range(len(lows)):
         if outs:
-            acc, outs[-1] = lax.optimization_barrier((acc, outs[-1]))
+            acc, outs[-1], w_top, w_end = lax.optimization_barrier((acc, outs[-1], w_top, w_end))
         outs.append(far_call(index * PACK, plan, seg, q, acc, top, far))
         sides.append(beside(outs[-1], "tp"))
     w_far = [w_top, w_end]
     terms = [(part, w_out, low) for part, low in zip(outs, lows)]
     base = patches
     for index, (left, right) in enumerate(sides):
+        if index:
+            base, left, right = lax.optimization_barrier((base, left, right))
         opposite = beyond(left, right, "tp")
         terms += [(left, w_left, lows[index]), (right, w_right, lows[index])]
         base = gather_call(base, *zip(*terms))

time: 113 us -> 112 us (level)
  blocking collectives: 43.2 us -> 37.9 us
  local copies, waits for them, and re-layouts: 0.18 us -> 5.08 us
  Pallas kernels: 38.1 us -> 40.8 us
  waiting for transfers between devices: 7.64 us -> 5.17 us
    all_to_all x1, blocking collectives: 43.2 us -> 37.9 us  [on_device(): lax.all_to_all(send.reshape(peers, lanes, cols), 'req', split_axis=0, con...]
    ppermute x3, waiting for transfers between devices: 7.61 us -> 3.85 us  [beside(): lax.ppermute(block, axis, ring(axis, 1))]
    unnamed x16 -> x24, local copies, waits for them, and re-layouts: 0.05 us -> 3.4 us
    ppermute x3, starting transfers between devices: 2.22 us -> 0.35 us  [beyond(): lax.ppermute(left[:half], axis, ring(axis, 1))]
    pallas_call x2, Pallas kernels: 6.79 us -> 8.36 us  [gather_call(): pl.pallas_call(functools.partial(gather_kernel, parts, rows), in_specs=[v...]
    ppermute x3, waiting for transfers between devices: 0.01 us -> 1.3 us  [beyond(): lax.ppermute(left[:half], axis, ring(axis, 1))]
    ppermute x3, starting transfers between devices: 6.98 us -> 8.14 us  [beyond(): lax.ppermute(right[half:], axis, ring(axis, -1))]
  transfers between devices with their start and end apart: 14 -> 14, of which waited for: 3 -> 3; matrix products, arithmetic and copies ran while one was open for 0% -> 2% of each run, Pallas kernels for 27% -> 31%
where the time goes in v5:
time: 112 us
  Pallas kernels  40.8 us (36%)
  blocking collectives  37.9 us (34%)
  starting transfers between devices  22.4 us (20%)
  waiting for transfers between devices  5.17 us (5%)
  local copies, waits for them, and re-layouts  5.08 us (5%)
    all_to_all x1, blocking collectives, on_device(): lax.all_to_all(send.reshape(peers, lanes, cols), 'req', split_axis=0, con...  37.9 us
    pallas_call x2, Pallas kernels, qkv_call(): pl.pallas_call(kernel, grid=(count // TILE,), in_specs=[pl.BlockSpec(memo...  13.3 us
    pallas_call x2, Pallas kernels, gather_call(): pl.pallas_call(functools.partial(gather_kernel, parts, rows), in_specs=[v...  8.36 us
    ppermute x3, starting transfers between devices, beyond(): lax.ppermute(right[half:], axis, ring(axis, -1))  8.14 us
    ppermute x3, starting transfers between devices, beside(): lax.ppermute(block, axis, ring(axis, -1))  6.77 us
    pallas_call x1, Pallas kernels, own_call(): pl.pallas_call(own_kernel, in_specs=[smem] + [vmem] * 3, out_specs=[vmem,...  5.29 us
    pallas_call x1, Pallas kernels, near_call(): pl.pallas_call(near_kernel, in_specs=[smem, smem, vmem, vmem, vmem, vmem]...  5.21 us
    ppermute x3, waiting for transfers between devices, beside(): lax.ppermute(block, axis, ring(axis, 1))  3.85 us
  transfers between devices with their start and end apart: 14, of which 3 were waited for; matrix products, arithmetic and copies ran while one was open for 2% of the time, Pallas kernels for 31%

profile of v5, /device:TPU:1, one launch (start us, length us, event | category | flops | bytes accessed | tf_op | source)
XLA Modules:
  0.0 111.8 jit_solution(7503309855469016704)
XLA Ops:
  0.0 2.1 %collective-permute-start = (bf16[352,1408]{1,0:T(8,128)(2,1)}, bf16[352,1408]{1,0:T(8,128)(2,1)S(1)}, u32[]{:S(2)}, u32[]{:S(2)}) collective-permute-start(bf16[352,1408]{1,0:T(8,128)(2,1)} %refs_5_.1), channel_id=1, source_target_pairs={{0,1},{1,2},{2,3},{3,0},{4,5},{5,6},{6,7},{7,4},{8,9},{9,10},{10,1... | collective-permute-start | bytes 2973704 | tf_op jit(solution)/shard_map/ppermute | solution.py:398
  2.1 1.4 %collective-permute-start.1 = (bf16[352,1408]{1,0:T(8,128)(2,1)}, bf16[352,1408]{1,0:T(8,128)(2,1)S(1)}, u32[]{:S(2)}, u32[]{:S(2)}) collective-permute-start(bf16[352,1408]{1,0:T(8,128)(2,1)} %refs_5_.1), channel_id=1, source_target_pairs={{0,3},{1,0},{2,1},{3,2},{4,7},{5,4},{6,5},{7,6},{8,11},{9,8},{10,9... | collective-permute-start | bytes 2973704 | tf_op jit(solution)/shard_map/ppermute | solution.py:398
  3.6 7.5 %keys_values.1.kv_ref = bf16[2,4,88,1024]{3,2,1,0:T(8,128)(2,1)} custom-call(s32[1,2]{1,0:T(1,128)} %plan_ref.3, bf16[176,192]{1,0:T(8,128)(2,1)} %constant.37.clone.table_ref, s32[1,1024]{1,0:T(1,128)} %bitcast.10, s32[1,1024]{1,0:T(1,128)} %bitcast.11, s32[1,1024]{1,0:T(1,128)} %bitcast.22, bf16[1024,1408]{1,0:T(8,128)(2,1)} %base_ref.1, f32[1408]{0:T(1024)} %gain_ref.3, ...), custom_call_target="tpu_custom_call" | custom-call | flops 2030043136 | bytes 1048576 | tf_op jit(solution)/shard_map/keys_values/pallas_call | solution.py:123
  11.1 2.9 %collective-permute-start.2 = (bf16[2,4,88,1024]{3,2,1,0:T(8,128)(2,1)}, bf16[2,4,88,1024]{3,2,1,0:T(8,128)(2,1)}, u32[]{:S(2)}, u32[]{:S(2)}) collective-permute-start(bf16[2,4,88,1024]{3,2,1,0:T(8,128)(2,1)} %keys_values.1.kv_ref), channel_id=1, source_target_pairs={{0,4},{4,0},{8,12},{12,8},{16,20},{20,16},{24,28},{28,24},{32,36},... | collective-permute-start | bytes 4325384 | tf_op jit(solution)/shard_map/ppermute | solution.py:419
  14.0 1.9 %collective-permute-start.3 = (bf16[2,4,88,1024]{3,2,1,0:T(8,128)(2,1)}, bf16[2,4,88,1024]{3,2,1,0:T(8,128)(2,1)}, u32[]{:S(2)}, u32[]{:S(2)}) collective-permute-start(bf16[2,4,88,1024]{3,2,1,0:T(8,128)(2,1)} %keys_values.1.kv_ref), channel_id=1, source_target_pairs={{4,8},{8,4},{12,16},{16,12},{20,24},{24,20},{28,32},{32,28},{36,40... | collective-permute-start | bytes 4325384 | tf_op jit(solution)/shard_map/ppermute | solution.py:418
  15.9 5.8 %queries.1.q_ref = bf16[4,128,1024]{2,1,0:T(8,128)(2,1)S(1)} custom-call(s32[1,2]{1,0:T(1,128)} %plan_ref.3, bf16[176,192]{1,0:T(8,128)(2,1)} %constant.37.clone.table_ref, s32[1,1024]{1,0:T(1,128)} %bitcast.12, s32[1,1024]{1,0:T(1,128)} %bitcast.13, s32[1,1024]{1,0:T(1,128)} %bitcast.23, bf16[1024,1408]{1,0:T(8,128)(2,1)} %base_ref.1, f32[1408]{0:T(1024)} %gain_ref.3, ...), custom_call_target="tpu_custom_call" | custom-call | flops 1015021568 | bytes 1048576 | tf_op jit(solution)/shard_map/queries/pallas_call | solution.py:123
  21.7 5.3 %own_keys.1 = (f32[4,96,1024]{2,1,0:T(8,128)S(1)}, f32[8,1024]{1,0:T(8,128)S(1)}) custom-call(s32[1,1024]{1,0:T(1,128)S(1)} %bitcast.14, s32[1,1024]{1,0:T(1,128)S(1)} %bitcast.15, bf16[4,128,1024]{2,1,0:T(8,128)(2,1)S(1)} %queries.1.q_ref, bf16[2,4,88,1024]{3,2,1,0:T(8,128)(2,1)} %keys_values.1.kv_ref), custom_call_target="tpu_custom_call" | custom-call | flops 17179869184 | bytes 1048576 | tf_op jit(solution)/shard_map/own_keys/pallas_call | solution.py:231
  29.9 2.7 %collective-permute-start.5 = (bf16[176,1408]{1,0:T(8,128)(2,1)}, bf16[176,1408]{1,0:T(8,128)(2,1)S(1)}, u32[]{:S(2)}, u32[]{:S(2)}) collective-permute-start(bf16[176,1408]{1,0:T(8,128)(2,1)} %slice.19), channel_id=1, source_target_pairs={{0,3},{1,0},{2,1},{3,2},{4,7},{5,4},{6,5},{7,6},{8,11},{9,8},{10,9... | collective-permute-start | bytes 1486856 | tf_op jit(solution)/shard_map/ppermute | solution.py:403
  32.6 1.4 %copy-done.3 = f32[4,96,1024]{2,1,0:T(8,128)S(1)} copy-done((f32[4,96,1024]{2,1,0:T(8,128)S(1)}, f32[4,96,1024]{2,1,0:T(8,128)}, u32[]{:S(2)}) %copy-start.3) | copy-done | bytes 1572888
  34.8 5.2 %near_keys.1 = (f32[4,96,1024]{2,1,0:T(8,128)S(1)}, f32[8,1024]{1,0:T(8,128)S(1)}) custom-call(s32[1,3]{1,0:T(1,128)S(1)} %pad_add_fusion.plan_ref, s32[1,1024]{1,0:T(1,128)S(1)} %bitcast.16, bf16[4,128,1024]{2,1,0:T(8,128)(2,1)S(1)} %queries.1.q_ref, f32[4,96,1024]{2,1,0:T(8,128)S(1)} %copy-done.3, f32[8,1024]{1,0:T(8,128)S(1)} %copy-done.6, ...), custom_call_target="tpu_custom_call" | custom-call | flops 268435456 | bytes 1048576 | tf_op jit(solution)/shard_map/near_keys/pallas_call | solution.py:256
  40.0 1.5 %far_keys.2.refs_0_ = bf16[176,1024]{1,0:T(8,128)(2,1)S(1)} custom-call(s32[1,3]{1,0:T(1,128)S(1)} %pad_add_fusion.plan_ref, s32[1,1024]{1,0:T(1,128)S(1)} %bitcast.17, bf16[4,128,1024]{2,1,0:T(8,128)(2,1)S(1)} %queries.1.q_ref, f32[4,96,1024]{2,1,0:T(8,128)S(1)} %get-tuple-element.27.acc_in, f32[8,1024]{1,0:T(8,128)S(1)} %get-tuple-element.23.top_in, ...), custom_call_target="tpu_custom_call" | custom-call | flops 3221225472 | bytes 1048576 | tf_op jit(solution)/shard_map/far_keys/pallas_call | solution.py:281
  41.6 2.7 %collective-permute-start.7 = (bf16[176,1024]{1,0:T(8,128)(2,1)S(1)}, bf16[176,1024]{1,0:T(8,128)(2,1)S(1)}, u32[]{:S(2)}, u32[]{:S(2)}) collective-permute-start(bf16[176,1024]{1,0:T(8,128)(2,1)S(1)} %far_keys.2.refs_0_), channel_id=1, source_target_pairs={{0,3},{1,0},{2,1},{3,2},{4,7},{5,4},{6,5},{7,6},{8,11},{9,8},{10,9... | collective-permute-start | bytes 1081352 | tf_op jit(solution)/shard_map/ppermute | solution.py:398
  44.3 1.5 %far_keys.3.refs_1_ = bf16[176,1024]{1,0:T(8,128)(2,1)S(1)} custom-call(s32[1,3]{1,0:T(1,128)S(1)} %pad_add_fusion.plan_ref, s32[1,1024]{1,0:T(1,128)S(1)} %bitcast.18, bf16[4,128,1024]{2,1,0:T(8,128)(2,1)S(1)} %queries.1.q_ref, f32[4,96,1024]{2,1,0:T(8,128)S(1)} %get-tuple-element.27.acc_in, f32[8,1024]{1,0:T(8,128)S(1)} %get-tuple-element.23.top_in, ...), custom_call_target="tpu_custom_call" | custom-call | flops 3221225472 | bytes 1048576 | tf_op jit(solution)/shard_map/far_keys/pallas_call | solution.py:281
  45.9 2.7 %collective-permute-start.9 = (bf16[176,1024]{1,0:T(8,128)(2,1)S(1)}, bf16[176,1024]{1,0:T(8,128)(2,1)S(1)}, u32[]{:S(2)}, u32[]{:S(2)}) collective-permute-start(bf16[176,1024]{1,0:T(8,128)(2,1)S(1)} %far_keys.3.refs_1_), channel_id=1, source_target_pairs={{0,3},{1,0},{2,1},{3,2},{4,7},{5,4},{6,5},{7,6},{8,11},{9,8},{10,9... | collective-permute-start | bytes 1081352 | tf_op jit(solution)/shard_map/ppermute | solution.py:398
  48.5 2.7 %collective-permute-done.6.refs_2_ = bf16[176,1024]{1,0:T(8,128)(2,1)S(1)} collective-permute-done((bf16[176,1024]{1,0:T(8,128)(2,1)S(1)}, bf16[176,1024]{1,0:T(8,128)(2,1)S(1)}, u32[]{:S(2)}, u32[]{:S(2)}) %collective-permute-start.6) | collective-permute-done | bytes 360480 | tf_op jit(solution)/shard_map/ppermute | solution.py:398
  51.5 2.7 %collective-permute-start.11 = (bf16[80,1024]{1,0:T(8,128)(2,1)S(1)}, bf16[80,1024]{1,0:T(8,128)(2,1)S(1)}, u32[]{:S(2)}, u32[]{:S(2)}) collective-permute-start(bf16[80,1024]{1,0:T(8,128)(2,1)S(1)} %slice.25), channel_id=1, source_target_pairs={{0,3},{1,0},{2,1},{3,2},{4,7},{5,4},{6,5},{7,6},{8,11},{9,8},{10,9... | collective-permute-start | bytes 491528 | tf_op jit(solution)/shard_map/ppermute | solution.py:403
  54.3 3.5 %output.2.base_ref = f32[1024,1408]{1,0:T(8,128)S(1)} custom-call(bf16[1024,1408]{1,0:T(8,128)(2,1)S(1)} %copy-done, bf16[176,1024]{1,0:T(8,128)(2,1)S(1)} %far_keys.2.refs_0_, bf16[176,1024]{1,0:T(8,128)(2,1)S(1)} %far_keys.3.refs_1_, bf16[176,1024]{1,0:T(8,128)(2,1)S(1)} %collective-permute-done.6.refs_2_, ...), custom_call_target="tpu_custom_call" | custom-call | flops 253755392 | bytes 65536 | tf_op jit(solution)/shard_map/output/pallas_call | solution.py:313
  57.7 1.2 %collective-permute-done.8.refs_2_ = bf16[176,1024]{1,0:T(8,128)(2,1)S(1)} collective-permute-done((bf16[176,1024]{1,0:T(8,128)(2,1)S(1)}, bf16[176,1024]{1,0:T(8,128)(2,1)S(1)}, u32[]{:S(2)}, u32[]{:S(2)}) %collective-permute-start.8) | collective-permute-done | bytes 360480 | tf_op jit(solution)/shard_map/ppermute | solution.py:398
  59.0 2.7 %collective-permute-start.13 = (bf16[80,1024]{1,0:T(8,128)(2,1)S(1)}, bf16[80,1024]{1,0:T(8,128)(2,1)S(1)}, u32[]{:S(2)}, u32[]{:S(2)}) collective-permute-start(bf16[80,1024]{1,0:T(8,128)(2,1)S(1)} %slice.23), channel_id=1, source_target_pairs={{0,3},{1,0},{2,1},{3,2},{4,7},{5,4},{6,5},{7,6},{8,11},{9,8},{10,9... | collective-permute-start | bytes 491528 | tf_op jit(solution)/shard_map/ppermute | solution.py:403
  61.8 1.3 %collective-permute-done.10.refs_0_ = bf16[96,1024]{1,0:T(8,128)(2,1)S(1)} collective-permute-done((bf16[96,1024]{1,0:T(8,128)(2,1)S(1)}, bf16[96,1024]{1,0:T(8,128)(2,1)S(1)}, u32[]{:S(2)}, u32[]{:S(2)}) %collective-permute-start.10) | collective-permute-done | bytes 196640 | tf_op jit(solution)/shard_map/ppermute | solution.py:403
  63.1 4.9 %output.3.base_ref = f32[1024,1408]{1,0:T(8,128)S(1)} custom-call(f32[1024,1408]{1,0:T(8,128)S(1)} %output.2.base_ref, bf16[96,1024]{1,0:T(8,128)(2,1)S(1)} %collective-permute-done.10.refs_0_, bf16[80,1024]{1,0:T(8,128)(2,1)S(1)} %collective-permute-done.11.refs_1_, bf16[176,1024]{1,0:T(8,128)(2,1)S(1)} %collective-permute-done.8.refs_2_, ...), custom_call_target="tpu_custom_call" | custom-call | flops 190316544 | bytes 65536 | tf_op jit(solution)/shard_map/output/pallas_call | solution.py:313
  68.1 3.6 %project.1 = bf16[512,640]{1,0:T(8,128)(2,1)S(1)} custom-call(s32[1,256]{1,0:T(1,128)S(1)} %bitcast.19, s32[1,256]{1,0:T(1,128)S(1)} %bitcast.20, f32[1024,1408]{1,0:T(8,128)S(1)} %output.3.base_ref, bf16[96,1024]{1,0:T(8,128)(2,1)S(1)} %collective-permute-done.12.refs_0_, bf16[80,1024]{1,0:T(8,128)(2,1)S(1)} %collective-permute-done.13.refs_1_, ...), custom_call_target="tpu_custom_call" | custom-call | flops 3221225472 | bytes 8388608 | tf_op jit(solution)/shard_map/project/pallas_call | solution.py:356
  71.7 37.9 %all_to_all.5 = bf16[64,8,640]{2,1,0:T(8,128)(2,1)} all-to-all(bf16[64,8,640]{2,1,0:T(8,128)(2,1)S(1)} %bitcast.9), channel_id=1, replica_groups=mesh['req'=64,'tp'=4] {'req'}, dimensions={0} | all-to-all | bytes 1310720 | tf_op jit(solution)/shard_map/all_to_all | solution.py:451
  109.6 2.1 %place.1 = bf16[256,512]{1,0:T(8,128)(2,1)} custom-call(bf16[512,640]{1,0:T(8,128)(2,1)} %bitcast.21), custom_call_target="tpu_custom_call" | custom-call | tf_op jit(solution)/shard_map/place/pallas_call | solution.py:379
  (48 shorter events, 4.3 us)
Async XLA Ops:
  0.0 28.2 %collective-permute-start = (bf16[352,1408]{1,0:T(8,128)(2,1)}, bf16[352,1408]{1,0:T(8,128)(2,1)S(1)}, u32[]{:S(2)}, u32[]{:S(2)}) collective-permute-start(bf16[352,1408]{1,0:T(8,128)(2,1)} %refs_5_.1), channel_id=1, source_target_pairs={{0,1},{1,2},{2,3},{3,0},{4,5},{5,6},{6,7},{7,4},{8,9},{9,10},{10,1... | collective-permute-start | bytes 2973704 | tf_op jit(solution)/shard_map/ppermute | solution.py:398
  2.1 26.1 %collective-permute-start.1 = (bf16[352,1408]{1,0:T(8,128)(2,1)}, bf16[352,1408]{1,0:T(8,128)(2,1)S(1)}, u32[]{:S(2)}, u32[]{:S(2)}) collective-permute-start(bf16[352,1408]{1,0:T(8,128)(2,1)} %refs_5_.1), channel_id=1, source_target_pairs={{0,3},{1,0},{2,1},{3,2},{4,7},{5,4},{6,5},{7,6},{8,11},{9,8},{10,9... | collective-permute-start | bytes 2973704 | tf_op jit(solution)/shard_map/ppermute | solution.py:398
  11.1 10.6 %copy-start.4 = (s32[1024]{0:T(1024)S(1)}, s32[1024]{0:T(1024)}, u32[]{:S(2)}) copy-start(s32[1024]{0:T(1024)} %param.13) | copy-start | bytes 12292
  11.1 21.5 %collective-permute-start.2 = (bf16[2,4,88,1024]{3,2,1,0:T(8,128)(2,1)}, bf16[2,4,88,1024]{3,2,1,0:T(8,128)(2,1)}, u32[]{:S(2)}, u32[]{:S(2)}) collective-permute-start(bf16[2,4,88,1024]{3,2,1,0:T(8,128)(2,1)} %keys_values.1.kv_ref), channel_id=1, source_target_pairs={{0,4},{4,0},{8,12},{12,8},{16,20},{20,16},{24,28},{28,24},{32,36},... | collective-permute-start | bytes 4325384 | tf_op jit(solution)/shard_map/ppermute | solution.py:419
  14.0 26.0 %collective-permute-start.3 = (bf16[2,4,88,1024]{3,2,1,0:T(8,128)(2,1)}, bf16[2,4,88,1024]{3,2,1,0:T(8,128)(2,1)}, u32[]{:S(2)}, u32[]{:S(2)}) collective-permute-start(bf16[2,4,88,1024]{3,2,1,0:T(8,128)(2,1)} %keys_values.1.kv_ref), channel_id=1, source_target_pairs={{4,8},{8,4},{12,16},{16,12},{20,24},{24,20},{28,32},{32,28},{36,40... | collective-permute-start | bytes 4325384 | tf_op jit(solution)/shard_map/ppermute | solution.py:418
  21.7 10.8 %copy-start.8 = (s32[1,2]{1,0:T(1,128)S(1)}, s32[1,2]{1,0:T(1,128)}, u32[]{:S(2)}) copy-start(s32[1,2]{1,0:T(1,128)} %plan_ref.3) | copy-start | bytes 28
  27.0 1.2 %copy-start.2 = (f32[4,96,1024]{2,1,0:T(8,128)}, f32[4,96,1024]{2,1,0:T(8,128)S(1)}, u32[]{:S(2)}) copy-start(f32[4,96,1024]{2,1,0:T(8,128)S(1)} %get-tuple-element.20.acc_in) | copy-start | bytes 4718596
  29.1 15.2 %collective-permute-start.4 = (bf16[176,1408]{1,0:T(8,128)(2,1)}, bf16[176,1408]{1,0:T(8,128)(2,1)}, u32[]{:S(2)}, u32[]{:S(2)}) collective-permute-start(bf16[176,1408]{1,0:T(8,128)(2,1)} %slice.18), channel_id=1, source_target_pairs={{0,1},{1,2},{2,3},{3,0},{4,5},{5,6},{6,7},{7,4},{8,9},{9,10},{10,1... | collective-permute-start | bytes 1486856 | tf_op jit(solution)/shard_map/ppermute | solution.py:403
  29.9 14.4 %collective-permute-start.5 = (bf16[176,1408]{1,0:T(8,128)(2,1)}, bf16[176,1408]{1,0:T(8,128)(2,1)S(1)}, u32[]{:S(2)}, u32[]{:S(2)}) collective-permute-start(bf16[176,1408]{1,0:T(8,128)(2,1)} %slice.19), channel_id=1, source_target_pairs={{0,3},{1,0},{2,1},{3,2},{4,7},{5,4},{6,5},{7,6},{8,11},{9,8},{10,9... | collective-permute-start | bytes 1486856 | tf_op jit(solution)/shard_map/ppermute | solution.py:403
  32.6 1.4 %copy-start.3 = (f32[4,96,1024]{2,1,0:T(8,128)S(1)}, f32[4,96,1024]{2,1,0:T(8,128)}, u32[]{:S(2)}) copy-start(f32[4,96,1024]{2,1,0:T(8,128)} %copy-done.2) | copy-start | bytes 4718596
  41.5 12.7 %copy-start = (bf16[1024,1408]{1,0:T(8,128)(2,1)S(1)}, bf16[1024,1408]{1,0:T(8,128)(2,1)}, u32[]{:S(2)}) copy-start(bf16[1024,1408]{1,0:T(8,128)(2,1)} %base_ref.1) | copy-start | bytes 8650756
  41.5 12.7 %copy-start.1 = (bf16[352,1408]{1,0:T(8,128)(2,1)S(1)}, bf16[352,1408]{1,0:T(8,128)(2,1)}, u32[]{:S(2)}) copy-start(bf16[352,1408]{1,0:T(8,128)(2,1)} %refs_5_.1) | copy-start | bytes 2973700
  41.5 9.7 %collective-permute-start.6 = (bf16[176,1024]{1,0:T(8,128)(2,1)S(1)}, bf16[176,1024]{1,0:T(8,128)(2,1)S(1)}, u32[]{:S(2)}, u32[]{:S(2)}) collective-permute-start(bf16[176,1024]{1,0:T(8,128)(2,1)S(1)} %far_keys.2.refs_0_), channel_id=1, source_target_pairs={{0,1},{1,2},{2,3},{3,0},{4,5},{5,6},{6,7},{7,4},{8,9},{9,10},{10,1... | collective-permute-start | bytes 1081352 | tf_op jit(solution)/shard_map/ppermute | solution.py:398
  41.6 9.9 %collective-permute-start.7 = (bf16[176,1024]{1,0:T(8,128)(2,1)S(1)}, bf16[176,1024]{1,0:T(8,128)(2,1)S(1)}, u32[]{:S(2)}, u32[]{:S(2)}) collective-permute-start(bf16[176,1024]{1,0:T(8,128)(2,1)S(1)} %far_keys.2.refs_0_), channel_id=1, source_target_pairs={{0,3},{1,0},{2,1},{3,2},{4,7},{5,4},{6,5},{7,6},{8,11},{9,8},{10,9... | collective-permute-start | bytes 1081352 | tf_op jit(solution)/shard_map/ppermute | solution.py:398
  45.8 13.1 %collective-permute-start.8 = (bf16[176,1024]{1,0:T(8,128)(2,1)S(1)}, bf16[176,1024]{1,0:T(8,128)(2,1)S(1)}, u32[]{:S(2)}, u32[]{:S(2)}) collective-permute-start(bf16[176,1024]{1,0:T(8,128)(2,1)S(1)} %far_keys.3.refs_1_), channel_id=1, source_target_pairs={{0,1},{1,2},{2,3},{3,0},{4,5},{5,6},{6,7},{7,4},{8,9},{9,10},{10,1... | collective-permute-start | bytes 1081352 | tf_op jit(solution)/shard_map/ppermute | solution.py:398
  45.9 13.0 %collective-permute-start.9 = (bf16[176,1024]{1,0:T(8,128)(2,1)S(1)}, bf16[176,1024]{1,0:T(8,128)(2,1)S(1)}, u32[]{:S(2)}, u32[]{:S(2)}) collective-permute-start(bf16[176,1024]{1,0:T(8,128)(2,1)S(1)} %far_keys.3.refs_1_), channel_id=1, source_target_pairs={{0,3},{1,0},{2,1},{3,2},{4,7},{5,4},{6,5},{7,6},{8,11},{9,8},{10,9... | collective-permute-start | bytes 1081352 | tf_op jit(solution)/shard_map/ppermute | solution.py:398
  51.2 11.9 %collective-permute-start.10 = (bf16[96,1024]{1,0:T(8,128)(2,1)S(1)}, bf16[96,1024]{1,0:T(8,128)(2,1)S(1)}, u32[]{:S(2)}, u32[]{:S(2)}) collective-permute-start(bf16[96,1024]{1,0:T(8,128)(2,1)S(1)} %slice.24), channel_id=1, source_target_pairs={{0,1},{1,2},{2,3},{3,0},{4,5},{5,6},{6,7},{7,4},{8,9},{9,10},{10,1... | collective-permute-start | bytes 589832 | tf_op jit(solution)/shard_map/ppermute | solution.py:403
  51.5 10.3 %copy-start.9 = (s32[256]{0:T(256)S(1)}, s32[256]{0:T(256)}, u32[]{:S(2)}) copy-start(s32[256]{0:T(256)} %param.16) | copy-start | bytes 3076
  51.5 10.3 %collective-permute-start.11 = (bf16[80,1024]{1,0:T(8,128)(2,1)S(1)}, bf16[80,1024]{1,0:T(8,128)(2,1)S(1)}, u32[]{:S(2)}, u32[]{:S(2)}) collective-permute-start(bf16[80,1024]{1,0:T(8,128)(2,1)S(1)} %slice.25), channel_id=1, source_target_pairs={{0,3},{1,0},{2,1},{3,2},{4,7},{5,4},{6,5},{7,6},{8,11},{9,8},{10,9... | collective-permute-start | bytes 491528 | tf_op jit(solution)/shard_map/ppermute | solution.py:403
  58.9 9.1 %collective-permute-start.12 = (bf16[96,1024]{1,0:T(8,128)(2,1)S(1)}, bf16[96,1024]{1,0:T(8,128)(2,1)S(1)}, u32[]{:S(2)}, u32[]{:S(2)}) collective-permute-start(bf16[96,1024]{1,0:T(8,128)(2,1)S(1)} %slice.22), channel_id=1, source_target_pairs={{0,1},{1,2},{2,3},{3,0},{4,5},{5,6},{6,7},{7,4},{8,9},{9,10},{10,1... | collective-permute-start | bytes 589832 | tf_op jit(solution)/shard_map/ppermute | solution.py:403
  59.0 9.0 %collective-permute-start.13 = (bf16[80,1024]{1,0:T(8,128)(2,1)S(1)}, bf16[80,1024]{1,0:T(8,128)(2,1)S(1)}, u32[]{:S(2)}, u32[]{:S(2)}) collective-permute-start(bf16[80,1024]{1,0:T(8,128)(2,1)S(1)} %slice.23), channel_id=1, source_target_pairs={{0,3},{1,0},{2,1},{3,2},{4,7},{5,4},{6,5},{7,6},{8,11},{9,8},{10,9... | collective-permute-start | bytes 491528 | tf_op jit(solution)/shard_map/ppermute | solution.py:403
  61.8 6.3 %slice-start = ((s8[5767168]{0:T(1024)(128)(4,1)}), s8[4194304]{0:T(1024)(128)(4,1)S(1)}, s32[]{:S(2)}) async-start(s8[5767168]{0:T(1024)(128)(4,1)} %bitcast.7), calls=%async_computation.1 | async-start | bytes 8388608
  61.8 6.3 %slice-start.1 = ((s8[5767168]{0:T(1024)(128)(4,1)}), s8[1572864]{0:T(1024)(128)(4,1)S(1)}, s32[]{:S(2)}) async-start(s8[5767168]{0:T(1024)(128)(4,1)} %bitcast.7), calls=%async_computation.2 | async-start | bytes 3145728
  61.8 6.3 %copy-start.7 = (s32[256]{0:T(256)S(1)}, s32[256]{0:T(256)}, u32[]{:S(2)}) copy-start(s32[256]{0:T(256)} %param.17) | copy-start | bytes 3076
  (2 other events, 1.6 us)

commit v6 on v5

--- a/solution.py
+++ b/solution.py
@@ -138,7 +138,7 @@
             pl.BlockSpec(shape[:-1] + (TILE,), lambda i, n=len(shape): (0,) * (n - 1) + (i,)) for shape in outs
         ],
         out_shape=[jax.ShapeDtypeStruct(shape, BF16) for shape in outs],
-        compiler_params=pltpu.CompilerParams(vmem_limit_bytes=28 << 20),
+        compiler_params=pltpu.CompilerParams(vmem_limit_bytes=12 << 20),
         cost_estimate=pl.CostEstimate(flops=flops // 1, bytes_accessed=1 << 20, transcendentals=0),
         name=name,
     )(*[pltpu.with_memory_space_constraint(v, pltpu.HBM) for v in args])
@@ -237,7 +237,7 @@
             jax.ShapeDtypeStruct((8, count), F32),
         ],
         scratch_shapes=[pltpu.VMEM((heads, count, AUG), BF16), pltpu.VMEM((heads, VAUG, count), BF16)],
-        compiler_params=pltpu.CompilerParams(vmem_limit_bytes=20 << 20),
+        compiler_params=pltpu.CompilerParams(vmem_limit_bytes=10 << 20),
         cost_estimate=pl.CostEstimate(flops=64 << 28, bytes_accessed=1 << 20, transcendentals=0),
         name="own_keys",
     )(seg, seg, q, kv)
@@ -259,7 +259,7 @@
         out_specs=[vmem, vmem],
         out_shape=[jax.ShapeDtypeStruct(acc.shape, F32), jax.ShapeDtypeStruct(top.shape, F32)],
         scratch_shapes=[pltpu.VMEM((heads, count, AUG), BF16), pltpu.VMEM((heads, VAUG, count), BF16)],
-        compiler_params=pltpu.CompilerParams(vmem_limit_bytes=20 << 20),
+        compiler_params=pltpu.CompilerParams(vmem_limit_bytes=10 << 20),
         cost_estimate=pl.CostEstimate(flops=1 << 28, bytes_accessed=1 << 20, transcendentals=0),
         name="near_keys",
     )(plan, seg, q, acc, top, kv)
@@ -271,7 +271,7 @@
     top[...] = top_in[...]
     neighbour(first, plan_ref[0, 2], plan_ref, sseg_ref, kv_ref, q_ref, keys, values, acc, top)
     for h in range(heads):
-        out_ref[pl.ds(h * HD, HD), :] = (acc[h, :HD, :] / acc[h, HD : HD + 1, :]).astype(BF16)
+        out_ref[pl.ds(h * HD, HD), :] = (acc[h, :HD, :] * (1.0 / acc[h, HD : HD + 1, :])).astype(BF16)
 
 
 def far_call(first, plan, seg, q, acc, top, kv):
@@ -289,7 +289,7 @@
             pltpu.VMEM((PACK, count, AUG), BF16),
             pltpu.VMEM((PACK, VAUG, count), BF16),
         ],
-        compiler_params=pltpu.CompilerParams(vmem_limit_bytes=20 << 20),
+        compiler_params=pltpu.CompilerParams(vmem_limit_bytes=10 << 20),
         cost_estimate=pl.CostEstimate(flops=12 << 28, bytes_accessed=1 << 20, transcendentals=0),
         name="far_keys",
     )(plan, seg, q, acc, top, kv)
@@ -315,7 +315,7 @@
         in_specs=[vmem] * (1 + 2 * parts),
         out_specs=vmem,
         out_shape=jax.ShapeDtypeStruct(base.shape, F32),
-        compiler_params=pltpu.CompilerParams(vmem_limit_bytes=16 << 20),
+        compiler_params=pltpu.CompilerParams(vmem_limit_bytes=12 << 20),
         cost_estimate=pl.CostEstimate(flops=flops // 8, bytes_accessed=1 << 16, transcendentals=0),
         name="output",
     )(base, *heads_parts, *w_parts)
@@ -359,7 +359,7 @@
         out_specs=vmem,
         out_shape=jax.ShapeDtypeStruct((slots, cols + 128), BF16),
         scratch_shapes=[pltpu.VMEM((width // 128, count, 128), F32)],
-        compiler_params=pltpu.CompilerParams(vmem_limit_bytes=24 << 20),
+        compiler_params=pltpu.CompilerParams(vmem_limit_bytes=20 << 20),
         cost_estimate=pl.CostEstimate(flops=3 << 30, bytes_accessed=8 << 20, transcendentals=0),
         name="project",
     )(slot, dest, base, *heads_parts, *w_parts, w_proj)
@@ -421,16 +421,18 @@
     plan = jnp.concatenate([split_plan, parity], axis=1)
     (q,) = qkv_call(q_kernel, "queries", [(0, 0, local)], [(heads, AUG, count)], *inputs)
     acc, top = own_call(seg, q, kv)
-    acc, w_left, w_right = lax.optimization_barrier((acc, w_left, w_right))
+    acc, top = near_call(plan, seg, q, acc, top, near)
+    top, w_left, w_right = lax.optimization_barrier((top, w_left, w_right))
     w_top, w_end = beyond(w_left, w_right, "tp")
-    acc, top = near_call(plan, seg, q, acc, top, near)
     pack = PACK * HD
     lows = list(range(0, local, pack))
     outs, sides = [], []
     for index in range(len(lows)):
         if outs:
-            acc, outs[-1], w_top, w_end = lax.optimization_barrier((acc, outs[-1], w_top, w_end))
+            acc, outs[-1] = lax.optimization_barrier((acc, outs[-1]))
         outs.append(far_call(index * PACK, plan, seg, q, acc, top, far))
+        if index == 1:
+            outs[-1], w_top, w_end = lax.optimization_barrier((outs[-1], w_top, w_end))
         sides.append(beside(outs[-1], "tp"))
     w_far = [w_top, w_end]
     terms = [(part, w_out, low) for part, low in zip(outs, lows)]

time: 112 us -> 110 us (0.982)
  waiting for transfers between devices: 5.17 us -> 12 us
  local copies, waits for them, and re-layouts: 5.08 us -> 0.18 us
  blocking collectives: 37.9 us -> 35.3 us
  Pallas kernels: 40.8 us -> 39.3 us
    ppermute x3, waiting for transfers between devices: 1.3 us -> 5.79 us  [beyond(): lax.ppermute(left[:half], axis, ring(axis, 1))]
    unnamed x24 -> x16, local copies, waits for them, and re-layouts: 3.4 us -> 0.05 us
    all_to_all x1, blocking collectives: 37.9 us -> 35.3 us  [on_device(): lax.all_to_all(send.reshape(peers, lanes, cols), 'req', split_axis=0, con...]
    ppermute x3, waiting for transfers between devices: 3.85 us -> 6.24 us  [beside(): lax.ppermute(block, axis, ring(axis, 1))]
    pallas_call x2, Pallas kernels: 8.36 us -> 6.79 us  [gather_call(): pl.pallas_call(functools.partial(gather_kernel, parts, rows), in_specs=[v...]
  transfers between devices with their start and end apart: 14 -> 14, of which waited for: 3 -> 4; matrix products, arithmetic and copies ran while one was open for 2% -> 0% of each run, Pallas kernels for 31% -> 31%
where the time goes in v6:
time: 110 us
  Pallas kernels  39.3 us (36%)
  blocking collectives  35.3 us (32%)
  starting transfers between devices  22.5 us (20%)
  waiting for transfers between devices  12 us (11%)
    all_to_all x1, blocking collectives, on_device(): lax.all_to_all(send.reshape(peers, lanes, cols), 'req', split_axis=0, con...  35.3 us
    pallas_call x2, Pallas kernels, qkv_call(): pl.pallas_call(kernel, grid=(count // TILE,), in_specs=[pl.BlockSpec(memo...  13.3 us
    ppermute x3, starting transfers between devices, beyond(): lax.ppermute(right[half:], axis, ring(axis, -1))  7.63 us
    pallas_call x2, Pallas kernels, gather_call(): pl.pallas_call(functools.partial(gather_kernel, parts, rows), in_specs=[v...  6.79 us
    ppermute x3, waiting for transfers between devices, beside(): lax.ppermute(block, axis, ring(axis, 1))  6.24 us
    ppermute x3, starting transfers between devices, beside(): lax.ppermute(block, axis, ring(axis, -1))  6.19 us
    ppermute x3, waiting for transfers between devices, beyond(): lax.ppermute(left[:half], axis, ring(axis, 1))  5.79 us
    pallas_call x1, Pallas kernels, own_call(): pl.pallas_call(own_kernel, in_specs=[smem] + [vmem] * 3, out_specs=[vmem,...  5.28 us
  transfers between devices with their start and end apart: 14, of which 4 were waited for; matrix products, arithmetic and copies ran while one was open for 0% of the time, Pallas kernels for 31%

profile of v6, /device:TPU:1, one launch (start us, length us, event | category | flops | bytes accessed | tf_op | source)
XLA Modules:
  0.0 109.7 jit_solution(10803984429657641021)
XLA Ops:
  0.0 2.1 %collective-permute-start.1 = (bf16[352,1408]{1,0:T(8,128)(2,1)}, bf16[352,1408]{1,0:T(8,128)(2,1)S(1)}, u32[]{:S(2)}, u32[]{:S(2)}) collective-permute-start(bf16[352,1408]{1,0:T(8,128)(2,1)} %refs_5_.1), channel_id=1, source_target_pairs={{0,1},{1,2},{2,3},{3,0},{4,5},{5,6},{6,7},{7,4},{8,9},{9,10},{10,1... | collective-permute-start | bytes 2973704 | tf_op jit(solution)/shard_map/ppermute | solution.py:398
  2.1 1.4 %collective-permute-start.2 = (bf16[352,1408]{1,0:T(8,128)(2,1)}, bf16[352,1408]{1,0:T(8,128)(2,1)S(1)}, u32[]{:S(2)}, u32[]{:S(2)}) collective-permute-start(bf16[352,1408]{1,0:T(8,128)(2,1)} %refs_5_.1), channel_id=1, source_target_pairs={{0,3},{1,0},{2,1},{3,2},{4,7},{5,4},{6,5},{7,6},{8,11},{9,8},{10,9... | collective-permute-start | bytes 2973704 | tf_op jit(solution)/shard_map/ppermute | solution.py:398
  3.6 7.5 %keys_values.1.kv_ref = bf16[2,4,88,1024]{3,2,1,0:T(8,128)(2,1)} custom-call(s32[1,2]{1,0:T(1,128)} %plan_ref.3, bf16[176,192]{1,0:T(8,128)(2,1)} %constant.37.clone.table_ref, s32[1,1024]{1,0:T(1,128)} %bitcast.10, s32[1,1024]{1,0:T(1,128)} %bitcast.11, s32[1,1024]{1,0:T(1,128)} %bitcast.22, bf16[1024,1408]{1,0:T(8,128)(2,1)} %base_ref.1, f32[1408]{0:T(1024)} %gain_ref.3, ...), custom_call_target="tpu_custom_call" | custom-call | flops 2030043136 | bytes 1048576 | tf_op jit(solution)/shard_map/keys_values/pallas_call | solution.py:123
  11.1 2.9 %collective-permute-start = (bf16[2,4,88,1024]{3,2,1,0:T(8,128)(2,1)}, bf16[2,4,88,1024]{3,2,1,0:T(8,128)(2,1)}, u32[]{:S(2)}, u32[]{:S(2)}) collective-permute-start(bf16[2,4,88,1024]{3,2,1,0:T(8,128)(2,1)} %keys_values.1.kv_ref), channel_id=1, source_target_pairs={{0,4},{4,0},{8,12},{12,8},{16,20},{20,16},{24,28},{28,24},{32,36},... | collective-permute-start | bytes 4325384 | tf_op jit(solution)/shard_map/ppermute | solution.py:419
  14.0 1.9 %collective-permute-start.3 = (bf16[2,4,88,1024]{3,2,1,0:T(8,128)(2,1)}, bf16[2,4,88,1024]{3,2,1,0:T(8,128)(2,1)}, u32[]{:S(2)}, u32[]{:S(2)}) collective-permute-start(bf16[2,4,88,1024]{3,2,1,0:T(8,128)(2,1)} %keys_values.1.kv_ref), channel_id=1, source_target_pairs={{4,8},{8,4},{12,16},{16,12},{20,24},{24,20},{28,32},{32,28},{36,40... | collective-permute-start | bytes 4325384 | tf_op jit(solution)/shard_map/ppermute | solution.py:418
  16.0 5.8 %queries.1.q_ref = bf16[4,128,1024]{2,1,0:T(8,128)(2,1)S(1)} custom-call(s32[1,2]{1,0:T(1,128)} %plan_ref.3, bf16[176,192]{1,0:T(8,128)(2,1)} %constant.37.clone.table_ref, s32[1,1024]{1,0:T(1,128)} %bitcast.12, s32[1,1024]{1,0:T(1,128)} %bitcast.13, s32[1,1024]{1,0:T(1,128)} %bitcast.23, bf16[1024,1408]{1,0:T(8,128)(2,1)} %base_ref.1, f32[1408]{0:T(1024)} %gain_ref.3, ...), custom_call_target="tpu_custom_call" | custom-call | flops 1015021568 | bytes 1048576 | tf_op jit(solution)/shard_map/queries/pallas_call | solution.py:123
  21.8 5.3 %own_keys.1 = (f32[4,96,1024]{2,1,0:T(8,128)S(1)}, f32[8,1024]{1,0:T(8,128)S(1)}) custom-call(s32[1,1024]{1,0:T(1,128)S(1)} %bitcast.14, s32[1,1024]{1,0:T(1,128)S(1)} %bitcast.15, bf16[4,128,1024]{2,1,0:T(8,128)(2,1)S(1)} %queries.1.q_ref, bf16[2,4,88,1024]{3,2,1,0:T(8,128)(2,1)} %keys_values.1.kv_ref), custom_call_target="tpu_custom_call" | custom-call | flops 17179869184 | bytes 1048576 | tf_op jit(solution)/shard_map/own_keys/pallas_call | solution.py:231
  27.1 5.2 %near_keys.1 = (f32[4,96,1024]{2,1,0:T(8,128)S(1)}, f32[8,1024]{1,0:T(8,128)S(1)}) custom-call(s32[1,3]{1,0:T(1,128)S(1)} %pad_add_fusion.plan_ref, s32[1,1024]{1,0:T(1,128)S(1)} %bitcast.16, bf16[4,128,1024]{2,1,0:T(8,128)(2,1)S(1)} %queries.1.q_ref, f32[4,96,1024]{2,1,0:T(8,128)S(1)} %get-tuple-element.20.acc_in, f32[8,1024]{1,0:T(8,128)S(1)} %get-tuple-element.21.top_in, ...), custom_call_target="tpu_custom_call" | custom-call | flops 268435456 | bytes 1048576 | tf_op jit(solution)/shard_map/near_keys/pallas_call | solution.py:256
  32.6 2.7 %collective-permute-start.5 = (bf16[176,1408]{1,0:T(8,128)(2,1)S(1)}, bf16[176,1408]{1,0:T(8,128)(2,1)S(1)}, u32[]{:S(2)}, u32[]{:S(2)}) collective-permute-start(bf16[176,1408]{1,0:T(8,128)(2,1)S(1)} %slice.19), channel_id=1, source_target_pairs={{0,3},{1,0},{2,1},{3,2},{4,7},{5,4},{6,5},{7,6},{8,11},{9,8},{10,9... | collective-permute-start | bytes 1486856 | tf_op jit(solution)/shard_map/ppermute | solution.py:403
  35.3 1.5 %far_keys.2.refs_0_ = bf16[176,1024]{1,0:T(8,128)(2,1)S(1)} custom-call(s32[1,3]{1,0:T(1,128)S(1)} %pad_add_fusion.plan_ref, s32[1,1024]{1,0:T(1,128)S(1)} %bitcast.17, bf16[4,128,1024]{2,1,0:T(8,128)(2,1)S(1)} %queries.1.q_ref, f32[4,96,1024]{2,1,0:T(8,128)S(1)} %get-tuple-element.26.acc_in, f32[8,1024]{1,0:T(8,128)S(1)} %get-tuple-element.24.top_in, ...), custom_call_target="tpu_custom_call" | custom-call | flops 3221225472 | bytes 1048576 | tf_op jit(solution)/shard_map/far_keys/pallas_call | solution.py:281
  36.9 2.7 %collective-permute-start.7 = (bf16[176,1024]{1,0:T(8,128)(2,1)S(1)}, bf16[176,1024]{1,0:T(8,128)(2,1)S(1)}, u32[]{:S(2)}, u32[]{:S(2)}) collective-permute-start(bf16[176,1024]{1,0:T(8,128)(2,1)S(1)} %far_keys.2.refs_0_), channel_id=1, source_target_pairs={{0,3},{1,0},{2,1},{3,2},{4,7},{5,4},{6,5},{7,6},{8,11},{9,8},{10,9... | collective-permute-start | bytes 1081352 | tf_op jit(solution)/shard_map/ppermute | solution.py:398
  39.6 1.5 %far_keys.3.refs_1_ = bf16[176,1024]{1,0:T(8,128)(2,1)S(1)} custom-call(s32[1,3]{1,0:T(1,128)S(1)} %pad_add_fusion.plan_ref, s32[1,1024]{1,0:T(1,128)S(1)} %bitcast.18, bf16[4,128,1024]{2,1,0:T(8,128)(2,1)S(1)} %queries.1.q_ref, f32[4,96,1024]{2,1,0:T(8,128)S(1)} %get-tuple-element.26.acc_in, f32[8,1024]{1,0:T(8,128)S(1)} %get-tuple-element.24.top_in, ...), custom_call_target="tpu_custom_call" | custom-call | flops 3221225472 | bytes 1048576 | tf_op jit(solution)/shard_map/far_keys/pallas_call | solution.py:281
  41.0 4.5 %collective-permute-done.4.refs_4_.refs_5_ = bf16[176,1408]{1,0:T(8,128)(2,1)S(1)} collective-permute-done((bf16[176,1408]{1,0:T(8,128)(2,1)S(1)}, bf16[176,1408]{1,0:T(8,128)(2,1)S(1)}, u32[]{:S(2)}, u32[]{:S(2)}) %collective-permute-start.4) | collective-permute-done | bytes 495648 | tf_op jit(solution)/shard_map/ppermute | solution.py:403
  46.1 2.1 %collective-permute-start.9 = (bf16[176,1024]{1,0:T(8,128)(2,1)S(1)}, bf16[176,1024]{1,0:T(8,128)(2,1)S(1)}, u32[]{:S(2)}, u32[]{:S(2)}) collective-permute-start(bf16[176,1024]{1,0:T(8,128)(2,1)S(1)} %far_keys.3.refs_1_), channel_id=1, source_target_pairs={{0,3},{1,0},{2,1},{3,2},{4,7},{5,4},{6,5},{7,6},{8,11},{9,8},{10,9... | collective-permute-start | bytes 1081352 | tf_op jit(solution)/shard_map/ppermute | solution.py:398
  48.2 5.0 %collective-permute-done.6.refs_2_ = bf16[176,1024]{1,0:T(8,128)(2,1)S(1)} collective-permute-done((bf16[176,1024]{1,0:T(8,128)(2,1)S(1)}, bf16[176,1024]{1,0:T(8,128)(2,1)S(1)}, u32[]{:S(2)}, u32[]{:S(2)}) %collective-permute-start.6) | collective-permute-done | bytes 360480 | tf_op jit(solution)/shard_map/ppermute | solution.py:398
  53.6 2.7 %collective-permute-start.11 = (bf16[80,1024]{1,0:T(8,128)(2,1)S(1)}, bf16[80,1024]{1,0:T(8,128)(2,1)S(1)}, u32[]{:S(2)}, u32[]{:S(2)}) collective-permute-start(bf16[80,1024]{1,0:T(8,128)(2,1)S(1)} %slice.25), channel_id=1, source_target_pairs={{0,3},{1,0},{2,1},{3,2},{4,7},{5,4},{6,5},{7,6},{8,11},{9,8},{10,9... | collective-permute-start | bytes 491528 | tf_op jit(solution)/shard_map/ppermute | solution.py:403
  56.3 3.5 %output.2.base_ref = f32[1024,1408]{1,0:T(8,128)S(1)} custom-call(bf16[1024,1408]{1,0:T(8,128)(2,1)S(1)} %copy-done, bf16[176,1024]{1,0:T(8,128)(2,1)S(1)} %far_keys.2.refs_0_, bf16[176,1024]{1,0:T(8,128)(2,1)S(1)} %far_keys.3.refs_1_, bf16[176,1024]{1,0:T(8,128)(2,1)S(1)} %collective-permute-done.6.refs_2_, ...), custom_call_target="tpu_custom_call" | custom-call | flops 253755392 | bytes 65536 | tf_op jit(solution)/shard_map/output/pallas_call | solution.py:313
  59.8 1.2 %collective-permute-done.8.refs_2_ = bf16[176,1024]{1,0:T(8,128)(2,1)S(1)} collective-permute-done((bf16[176,1024]{1,0:T(8,128)(2,1)S(1)}, bf16[176,1024]{1,0:T(8,128)(2,1)S(1)}, u32[]{:S(2)}, u32[]{:S(2)}) %collective-permute-start.8) | collective-permute-done | bytes 360480 | tf_op jit(solution)/shard_map/ppermute | solution.py:398
  61.7 2.2 %collective-permute-start.13 = (bf16[80,1024]{1,0:T(8,128)(2,1)S(1)}, bf16[80,1024]{1,0:T(8,128)(2,1)S(1)}, u32[]{:S(2)}, u32[]{:S(2)}) collective-permute-start(bf16[80,1024]{1,0:T(8,128)(2,1)S(1)} %slice.23), channel_id=1, source_target_pairs={{0,3},{1,0},{2,1},{3,2},{4,7},{5,4},{6,5},{7,6},{8,11},{9,8},{10,9... | collective-permute-start | bytes 491528 | tf_op jit(solution)/shard_map/ppermute | solution.py:403
  63.9 1.3 %collective-permute-done.10.refs_0_ = bf16[96,1024]{1,0:T(8,128)(2,1)S(1)} collective-permute-done((bf16[96,1024]{1,0:T(8,128)(2,1)S(1)}, bf16[96,1024]{1,0:T(8,128)(2,1)S(1)}, u32[]{:S(2)}, u32[]{:S(2)}) %collective-permute-start.10) | collective-permute-done | bytes 196640 | tf_op jit(solution)/shard_map/ppermute | solution.py:403
  65.2 3.3 %output.3.base_ref = f32[1024,1408]{1,0:T(8,128)S(1)} custom-call(f32[1024,1408]{1,0:T(8,128)S(1)} %output.2.base_ref, bf16[96,1024]{1,0:T(8,128)(2,1)S(1)} %collective-permute-done.10.refs_0_, bf16[80,1024]{1,0:T(8,128)(2,1)S(1)} %collective-permute-done.11.refs_1_, bf16[176,1024]{1,0:T(8,128)(2,1)S(1)} %collective-permute-done.8.refs_2_, ...), custom_call_target="tpu_custom_call" | custom-call | flops 190316544 | bytes 65536 | tf_op jit(solution)/shard_map/output/pallas_call | solution.py:313
  68.6 3.6 %project.1 = bf16[512,640]{1,0:T(8,128)(2,1)S(1)} custom-call(s32[1,256]{1,0:T(1,128)S(1)} %bitcast.19, s32[1,256]{1,0:T(1,128)S(1)} %bitcast.20, f32[1024,1408]{1,0:T(8,128)S(1)} %output.3.base_ref, bf16[96,1024]{1,0:T(8,128)(2,1)S(1)} %collective-permute-done.12.refs_0_, bf16[80,1024]{1,0:T(8,128)(2,1)S(1)} %collective-permute-done.13.refs_1_, ...), custom_call_target="tpu_custom_call" | custom-call | flops 3221225472 | bytes 8388608 | tf_op jit(solution)/shard_map/project/pallas_call | solution.py:356
  72.2 35.3 %all_to_all.5 = bf16[64,8,640]{2,1,0:T(8,128)(2,1)} all-to-all(bf16[64,8,640]{2,1,0:T(8,128)(2,1)S(1)} %bitcast.9), channel_id=1, replica_groups=mesh['req'=64,'tp'=4] {'req'}, dimensions={0} | all-to-all | bytes 1310720 | tf_op jit(solution)/shard_map/all_to_all | solution.py:453
  107.5 2.1 %place.1 = bf16[256,512]{1,0:T(8,128)(2,1)} custom-call(bf16[512,640]{1,0:T(8,128)(2,1)} %bitcast.21), custom_call_target="tpu_custom_call" | custom-call | tf_op jit(solution)/shard_map/place/pallas_call | solution.py:379
  (40 shorter events, 2.0 us)
Async XLA Ops:
  0.0 32.4 %collective-permute-start.1 = (bf16[352,1408]{1,0:T(8,128)(2,1)}, bf16[352,1408]{1,0:T(8,128)(2,1)S(1)}, u32[]{:S(2)}, u32[]{:S(2)}) collective-permute-start(bf16[352,1408]{1,0:T(8,128)(2,1)} %refs_5_.1), channel_id=1, source_target_pairs={{0,1},{1,2},{2,3},{3,0},{4,5},{5,6},{6,7},{7,4},{8,9},{9,10},{10,1... | collective-permute-start | bytes 2973704 | tf_op jit(solution)/shard_map/ppermute | solution.py:398
  2.1 30.2 %collective-permute-start.2 = (bf16[352,1408]{1,0:T(8,128)(2,1)}, bf16[352,1408]{1,0:T(8,128)(2,1)S(1)}, u32[]{:S(2)}, u32[]{:S(2)}) collective-permute-start(bf16[352,1408]{1,0:T(8,128)(2,1)} %refs_5_.1), channel_id=1, source_target_pairs={{0,3},{1,0},{2,1},{3,2},{4,7},{5,4},{6,5},{7,6},{8,11},{9,8},{10,9... | collective-permute-start | bytes 2973704 | tf_op jit(solution)/shard_map/ppermute | solution.py:398
  11.1 16.0 %collective-permute-start = (bf16[2,4,88,1024]{3,2,1,0:T(8,128)(2,1)}, bf16[2,4,88,1024]{3,2,1,0:T(8,128)(2,1)}, u32[]{:S(2)}, u32[]{:S(2)}) collective-permute-start(bf16[2,4,88,1024]{3,2,1,0:T(8,128)(2,1)} %keys_values.1.kv_ref), channel_id=1, source_target_pairs={{0,4},{4,0},{8,12},{12,8},{16,20},{20,16},{24,28},{28,24},{32,36},... | collective-permute-start | bytes 4325384 | tf_op jit(solution)/shard_map/ppermute | solution.py:419
  14.0 21.3 %collective-permute-start.3 = (bf16[2,4,88,1024]{3,2,1,0:T(8,128)(2,1)}, bf16[2,4,88,1024]{3,2,1,0:T(8,128)(2,1)}, u32[]{:S(2)}, u32[]{:S(2)}) collective-permute-start(bf16[2,4,88,1024]{3,2,1,0:T(8,128)(2,1)} %keys_values.1.kv_ref), channel_id=1, source_target_pairs={{4,8},{8,4},{12,16},{16,12},{20,24},{24,20},{28,32},{32,28},{36,40... | collective-permute-start | bytes 4325384 | tf_op jit(solution)/shard_map/ppermute | solution.py:418
  15.9 5.8 %copy-start.4 = (s32[1,2]{1,0:T(1,128)S(1)}, s32[1,2]{1,0:T(1,128)}, u32[]{:S(2)}) copy-start(s32[1,2]{1,0:T(1,128)} %plan_ref.3) | copy-start | bytes 28
  15.9 5.9 %copy-start.2 = (s32[1024]{0:T(1024)S(1)}, s32[1024]{0:T(1024)}, u32[]{:S(2)}) copy-start(s32[1024]{0:T(1024)} %param.13) | copy-start | bytes 12292
  32.4 13.1 %collective-permute-start.4 = (bf16[176,1408]{1,0:T(8,128)(2,1)S(1)}, bf16[176,1408]{1,0:T(8,128)(2,1)S(1)}, u32[]{:S(2)}, u32[]{:S(2)}) collective-permute-start(bf16[176,1408]{1,0:T(8,128)(2,1)S(1)} %slice.18), channel_id=1, source_target_pairs={{0,1},{1,2},{2,3},{3,0},{4,5},{5,6},{6,7},{7,4},{8,9},{9,10},{10,1... | collective-permute-start | bytes 1486856 | tf_op jit(solution)/shard_map/ppermute | solution.py:403
  32.6 13.0 %collective-permute-start.5 = (bf16[176,1408]{1,0:T(8,128)(2,1)S(1)}, bf16[176,1408]{1,0:T(8,128)(2,1)S(1)}, u32[]{:S(2)}, u32[]{:S(2)}) collective-permute-start(bf16[176,1408]{1,0:T(8,128)(2,1)S(1)} %slice.19), channel_id=1, source_target_pairs={{0,3},{1,0},{2,1},{3,2},{4,7},{5,4},{6,5},{7,6},{8,11},{9,8},{10,9... | collective-permute-start | bytes 1486856 | tf_op jit(solution)/shard_map/ppermute | solution.py:403
  36.8 19.5 %copy-start = (bf16[1024,1408]{1,0:T(8,128)(2,1)S(1)}, bf16[1024,1408]{1,0:T(8,128)(2,1)}, u32[]{:S(2)}) copy-start(bf16[1024,1408]{1,0:T(8,128)(2,1)} %base_ref.1) | copy-start | bytes 8650756
  36.8 19.5 %copy-start.1 = (bf16[352,1408]{1,0:T(8,128)(2,1)S(1)}, bf16[352,1408]{1,0:T(8,128)(2,1)}, u32[]{:S(2)}) copy-start(bf16[352,1408]{1,0:T(8,128)(2,1)} %refs_5_.1) | copy-start | bytes 2973700
  36.8 16.5 %collective-permute-start.6 = (bf16[176,1024]{1,0:T(8,128)(2,1)S(1)}, bf16[176,1024]{1,0:T(8,128)(2,1)S(1)}, u32[]{:S(2)}, u32[]{:S(2)}) collective-permute-start(bf16[176,1024]{1,0:T(8,128)(2,1)S(1)} %far_keys.2.refs_0_), channel_id=1, source_target_pairs={{0,1},{1,2},{2,3},{3,0},{4,5},{5,6},{6,7},{7,4},{8,9},{9,10},{10,1... | collective-permute-start | bytes 1081352 | tf_op jit(solution)/shard_map/ppermute | solution.py:398
  36.9 16.7 %collective-permute-start.7 = (bf16[176,1024]{1,0:T(8,128)(2,1)S(1)}, bf16[176,1024]{1,0:T(8,128)(2,1)S(1)}, u32[]{:S(2)}, u32[]{:S(2)}) collective-permute-start(bf16[176,1024]{1,0:T(8,128)(2,1)S(1)} %far_keys.2.refs_0_), channel_id=1, source_target_pairs={{0,3},{1,0},{2,1},{3,2},{4,7},{5,4},{6,5},{7,6},{8,11},{9,8},{10,9... | collective-permute-start | bytes 1081352 | tf_op jit(solution)/shard_map/ppermute | solution.py:398
  45.5 15.4 %collective-permute-start.8 = (bf16[176,1024]{1,0:T(8,128)(2,1)S(1)}, bf16[176,1024]{1,0:T(8,128)(2,1)S(1)}, u32[]{:S(2)}, u32[]{:S(2)}) collective-permute-start(bf16[176,1024]{1,0:T(8,128)(2,1)S(1)} %far_keys.3.refs_1_), channel_id=1, source_target_pairs={{0,1},{1,2},{2,3},{3,0},{4,5},{5,6},{6,7},{7,4},{8,9},{9,10},{10,1... | collective-permute-start | bytes 1081352 | tf_op jit(solution)/shard_map/ppermute | solution.py:398
  46.1 14.9 %collective-permute-start.9 = (bf16[176,1024]{1,0:T(8,128)(2,1)S(1)}, bf16[176,1024]{1,0:T(8,128)(2,1)S(1)}, u32[]{:S(2)}, u32[]{:S(2)}) collective-permute-start(bf16[176,1024]{1,0:T(8,128)(2,1)S(1)} %far_keys.3.refs_1_), channel_id=1, source_target_pairs={{0,3},{1,0},{2,1},{3,2},{4,7},{5,4},{6,5},{7,6},{8,11},{9,8},{10,9... | collective-permute-start | bytes 1081352 | tf_op jit(solution)/shard_map/ppermute | solution.py:398
  53.3 11.9 %collective-permute-start.10 = (bf16[96,1024]{1,0:T(8,128)(2,1)S(1)}, bf16[96,1024]{1,0:T(8,128)(2,1)S(1)}, u32[]{:S(2)}, u32[]{:S(2)}) collective-permute-start(bf16[96,1024]{1,0:T(8,128)(2,1)S(1)} %slice.24), channel_id=1, source_target_pairs={{0,1},{1,2},{2,3},{3,0},{4,5},{5,6},{6,7},{7,4},{8,9},{9,10},{10,1... | collective-permute-start | bytes 589832 | tf_op jit(solution)/shard_map/ppermute | solution.py:403
  53.6 10.3 %copy-start.5 = (s32[256]{0:T(256)S(1)}, s32[256]{0:T(256)}, u32[]{:S(2)}) copy-start(s32[256]{0:T(256)} %param.16) | copy-start | bytes 3076
  53.6 10.3 %collective-permute-start.11 = (bf16[80,1024]{1,0:T(8,128)(2,1)S(1)}, bf16[80,1024]{1,0:T(8,128)(2,1)S(1)}, u32[]{:S(2)}, u32[]{:S(2)}) collective-permute-start(bf16[80,1024]{1,0:T(8,128)(2,1)S(1)} %slice.25), channel_id=1, source_target_pairs={{0,3},{1,0},{2,1},{3,2},{4,7},{5,4},{6,5},{7,6},{8,11},{9,8},{10,9... | collective-permute-start | bytes 491528 | tf_op jit(solution)/shard_map/ppermute | solution.py:403
  61.0 7.5 %collective-permute-start.12 = (bf16[96,1024]{1,0:T(8,128)(2,1)S(1)}, bf16[96,1024]{1,0:T(8,128)(2,1)S(1)}, u32[]{:S(2)}, u32[]{:S(2)}) collective-permute-start(bf16[96,1024]{1,0:T(8,128)(2,1)S(1)} %slice.22), channel_id=1, source_target_pairs={{0,1},{1,2},{2,3},{3,0},{4,5},{5,6},{6,7},{7,4},{8,9},{9,10},{10,1... | collective-permute-start | bytes 589832 | tf_op jit(solution)/shard_map/ppermute | solution.py:403
  61.7 6.8 %collective-permute-start.13 = (bf16[80,1024]{1,0:T(8,128)(2,1)S(1)}, bf16[80,1024]{1,0:T(8,128)(2,1)S(1)}, u32[]{:S(2)}, u32[]{:S(2)}) collective-permute-start(bf16[80,1024]{1,0:T(8,128)(2,1)S(1)} %slice.23), channel_id=1, source_target_pairs={{0,3},{1,0},{2,1},{3,2},{4,7},{5,4},{6,5},{7,6},{8,11},{9,8},{10,9... | collective-permute-start | bytes 491528 | tf_op jit(solution)/shard_map/ppermute | solution.py:403
  63.9 4.7 %slice-start = ((s8[5767168]{0:T(1024)(128)(4,1)}), s8[4194304]{0:T(1024)(128)(4,1)S(1)}, s32[]{:S(2)}) async-start(s8[5767168]{0:T(1024)(128)(4,1)} %bitcast.7), calls=%async_computation.1 | async-start | bytes 8388608
  63.9 4.7 %slice-start.1 = ((s8[5767168]{0:T(1024)(128)(4,1)}), s8[1572864]{0:T(1024)(128)(4,1)S(1)}, s32[]{:S(2)}) async-start(s8[5767168]{0:T(1024)(128)(4,1)} %bitcast.7), calls=%async_computation.2 | async-start | bytes 3145728
  63.9 4.7 %copy-start.3 = (s32[256]{0:T(256)S(1)}, s32[256]{0:T(256)}, u32[]{:S(2)}) copy-start(s32[256]{0:T(256)} %param.17) | copy-start | bytes 3076

commit v7 on v6

--- a/solution.py
+++ b/solution.py
@@ -91,26 +91,19 @@
     return rotated
 
 
-def kv_kernel(plan_ref, table_ref, seg_ref, segt_ref, side_ref, x_ref, gain_ref, bias_ref, wk_ref, wv_ref, *kv_refs):
+def qkv_kernel(plan_ref, table_ref, seg_ref, segt_ref, side_ref, x_ref, gain_ref, bias_ref, wk_ref, wv_ref, wq_ref, kv_ref, q_ref):
     normed = normalised(x_ref, gain_ref, bias_ref)
     rotated = rotations(plan_ref, table_ref, seg_ref, segt_ref, side_ref)
     keys = lax.dot_general(wk_ref[0], normed, NT, preferred_element_type=F32)
     values = lax.dot_general(wv_ref[0], normed, NT, preferred_element_type=F32)
-    pack = kv_refs[0].shape[1]
-    for h in range(pack * len(kv_refs)):
-        span = slice(h * HD, (h + 1) * HD)
-        kv_refs[h // pack][0, h % pack] = rotated(keys[span]).astype(BF16)
-        kv_refs[h // pack][1, h % pack] = values[span].astype(BF16)
-
-
-def q_kernel(plan_ref, table_ref, seg_ref, segt_ref, side_ref, x_ref, gain_ref, bias_ref, w_ref, q_ref):
-    normed = normalised(x_ref, gain_ref, bias_ref)
-    rotated = rotations(plan_ref, table_ref, seg_ref, segt_ref, side_ref)
-    queries = lax.dot_general(w_ref[0], normed, NT, preferred_element_type=F32)
+    queries = lax.dot_general(wq_ref[0], normed, NT, preferred_element_type=F32)
     aug = lax.broadcasted_iota(jnp.int32, (AUG - HD, TILE), 0)
     barred = jnp.where(aug == jnp.broadcast_to(segt_ref[...], aug.shape), 0.0, jnp.where(aug <= 16, -BIG, 0.0))
     for h in range(q_ref.shape[0]):
-        query = rotated(queries[h * HD : (h + 1) * HD]) * (HD**-0.5 * LOG2E)
+        span = slice(h * HD, (h + 1) * HD)
+        kv_ref[0, h] = rotated(keys[span]).astype(BF16)
+        kv_ref[1, h] = values[span].astype(BF16)
+        query = rotated(queries[span]) * (HD**-0.5 * LOG2E)
         q_ref[h] = jnp.concatenate([query, barred], axis=0).astype(BF16)
 
 
@@ -414,12 +407,12 @@
     table = jnp.asarray(rope_table())
     w_left, w_right = beside(w_out, "tp")
     inputs = (patches, seg, grid_sides.reshape(1, count), split_plan, ln_gain, ln_bias, w_qkv, table)
-    (kv,) = qkv_call(kv_kernel, "keys_values", [(1, 0, local), (2, 0, local)], [(2, heads, HD, count)], *inputs)
+    rows = [(1, 0, local), (2, 0, local), (0, 0, local)]
+    kv, q = qkv_call(qkv_kernel, "qkv", rows, [(2, heads, HD, count), (heads, AUG, count)], *inputs)
     far = lax.ppermute(kv, "req", swaps(range(1, peers - 1, 2)))
     near = lax.ppermute(kv, "req", swaps(range(0, peers - 1, 2)))
     parity = (lax.axis_index("req") % 2).astype(jnp.int32).reshape(1, 1)
     plan = jnp.concatenate([split_plan, parity], axis=1)
-    (q,) = qkv_call(q_kernel, "queries", [(0, 0, local)], [(heads, AUG, count)], *inputs)
     acc, top = own_call(seg, q, kv)
     acc, top = near_call(plan, seg, q, acc, top, near)
     top, w_left, w_right = lax.optimization_barrier((top, w_left, w_right))

time: 110 us -> 107 us (0.973)
  Pallas kernels: 39.3 us -> 34.4 us
  local copies, waits for them, and re-layouts: 0.18 us -> 2.4 us
    ppermute x1, waiting for transfers between devices: 0.01 us -> 4.74 us  [on_device(): far = lax.ppermute(kv, 'req', swaps(range(1, peers - 1, 2)))]
    ppermute x3, waiting for transfers between devices: 5.79 us -> 1.3 us  [beyond(): lax.ppermute(left[:half], axis, ring(axis, 1))]
    pallas_call x2 -> x1, Pallas kernels: 13.3 us -> 9.02 us  [qkv_call(): pl.pallas_call(kernel, grid=(count // TILE,), in_specs=[pl.BlockSpec(memo...]
    unnamed x16 -> x22, local copies, waits for them, and re-layouts: 0.05 us -> 2.27 us
  transfers between devices with their start and end apart: 14 -> 14, of which waited for: 4 -> 4; matrix products, arithmetic and copies ran while one was open for 0% -> 0% of each run, Pallas kernels for 31% -> 27%
where the time goes in v7:
time: 107 us
  blocking collectives  35.4 us (33%)
  Pallas kernels  34.4 us (32%)
  starting transfers between devices  22.5 us (21%)
  waiting for transfers between devices  12 us (11%)
  local copies, waits for them, and re-layouts  2.4 us (2%)
    all_to_all x1, blocking collectives, on_device(): lax.all_to_all(send.reshape(peers, lanes, cols), 'req', split_axis=0, con...  35.4 us
    pallas_call x1, Pallas kernels, qkv_call(): pl.pallas_call(kernel, grid=(count // TILE,), in_specs=[pl.BlockSpec(memo...  9.02 us
    ppermute x3, starting transfers between devices, beyond(): lax.ppermute(right[half:], axis, ring(axis, -1))  7.61 us
    pallas_call x2, Pallas kernels, gather_call(): pl.pallas_call(functools.partial(gather_kernel, parts, rows), in_specs=[v...  6.81 us
    ppermute x3, starting transfers between devices, beside(): lax.ppermute(block, axis, ring(axis, -1))  6.43 us
    ppermute x3, waiting for transfers between devices, beside(): lax.ppermute(block, axis, ring(axis, 1))  5.97 us
    pallas_call x1, Pallas kernels, own_call(): pl.pallas_call(own_kernel, in_specs=[smem] + [vmem] * 3, out_specs=[vmem,...  5.37 us
    ppermute x1, waiting for transfers between devices, on_device(): far = lax.ppermute(kv, 'req', swaps(range(1, peers - 1, 2)))  4.74 us
  transfers between devices with their start and end apart: 14, of which 4 were waited for; matrix products, arithmetic and copies ran while one was open for 0% of the time, Pallas kernels for 27%

profile of v7, /device:TPU:1, one launch (start us, length us, event | category | flops | bytes accessed | tf_op | source)
XLA Modules:
  0.0 107.1 jit_solution(6902587382365292479)
XLA Ops:
  0.0 2.1 %collective-permute-start.1 = (bf16[352,1408]{1,0:T(8,128)(2,1)}, bf16[352,1408]{1,0:T(8,128)(2,1)S(1)}, u32[]{:S(2)}, u32[]{:S(2)}) collective-permute-start(bf16[352,1408]{1,0:T(8,128)(2,1)} %refs_5_.1), channel_id=1, source_target_pairs={{0,1},{1,2},{2,3},{3,0},{4,5},{5,6},{6,7},{7,4},{8,9},{9,10},{10,1... | collective-permute-start | bytes 2973704 | tf_op jit(solution)/shard_map/ppermute | solution.py:391
  2.1 1.4 %collective-permute-start.2 = (bf16[352,1408]{1,0:T(8,128)(2,1)}, bf16[352,1408]{1,0:T(8,128)(2,1)S(1)}, u32[]{:S(2)}, u32[]{:S(2)}) collective-permute-start(bf16[352,1408]{1,0:T(8,128)(2,1)} %refs_5_.1), channel_id=1, source_target_pairs={{0,3},{1,0},{2,1},{3,2},{4,7},{5,4},{6,5},{7,6},{8,11},{9,8},{10,9... | collective-permute-start | bytes 2973704 | tf_op jit(solution)/shard_map/ppermute | solution.py:391
  3.6 9.0 %qkv.1 = (bf16[2,4,88,1024]{3,2,1,0:T(8,128)(2,1)}, bf16[4,128,1024]{2,1,0:T(8,128)(2,1)S(1)}) custom-call(s32[1,2]{1,0:T(1,128)} %plan_ref.1, bf16[176,192]{1,0:T(8,128)(2,1)} %constant.37.clone.table_ref, s32[1,1024]{1,0:T(1,128)} %bitcast.10, s32[1,1024]{1,0:T(1,128)} %bitcast.11, s32[1,1024]{1,0:T(1,128)} %bitcast.20, bf16[1024,1408]{1,0:T(8,128)(2,1)} %base_ref.1, ...), custom_call_target="tpu_custom_call" | custom-call | flops 3045064704 | bytes 1048576 | tf_op jit(solution)/shard_map/qkv/pallas_call | solution.py:116
  13.6 2.9 %collective-permute-start = (bf16[2,4,88,1024]{3,2,1,0:T(8,128)(2,1)}, bf16[2,4,88,1024]{3,2,1,0:T(8,128)(2,1)S(1)}, u32[]{:S(2)}, u32[]{:S(2)}) collective-permute-start(bf16[2,4,88,1024]{3,2,1,0:T(8,128)(2,1)} %get-tuple-element.23.kv_ref), channel_id=1, source_target_pairs={{0,4},{4,0},{8,12},{12,8},{16,20},{20,16},{24,28},{28,24},{32,36},... | collective-permute-start | bytes 4325384 | tf_op jit(solution)/shard_map/ppermute | solution.py:413
  16.5 1.9 %collective-permute-start.3 = (bf16[2,4,88,1024]{3,2,1,0:T(8,128)(2,1)}, bf16[2,4,88,1024]{3,2,1,0:T(8,128)(2,1)}, u32[]{:S(2)}, u32[]{:S(2)}) collective-permute-start(bf16[2,4,88,1024]{3,2,1,0:T(8,128)(2,1)} %get-tuple-element.23.kv_ref), channel_id=1, source_target_pairs={{4,8},{8,4},{12,16},{16,12},{20,24},{24,20},{28,32},{32,28},{36,40... | collective-permute-start | bytes 4325384 | tf_op jit(solution)/shard_map/ppermute | solution.py:412
  18.5 1.2 %copy-done.3 = bf16[4,128,1024]{2,1,0:T(8,128)(2,1)S(1)} copy-done((bf16[4,128,1024]{2,1,0:T(8,128)(2,1)S(1)}, bf16[4,128,1024]{2,1,0:T(8,128)(2,1)}, u32[]{:S(2)}) %copy-start.3) | copy-done | bytes 1048600
  19.8 5.4 %own_keys.1 = (f32[4,96,1024]{2,1,0:T(8,128)S(1)}, f32[8,1024]{1,0:T(8,128)S(1)}) custom-call(s32[1,1024]{1,0:T(1,128)S(1)} %bitcast.12, s32[1,1024]{1,0:T(1,128)S(1)} %bitcast.13, bf16[4,128,1024]{2,1,0:T(8,128)(2,1)S(1)} %copy-done.3, bf16[2,4,88,1024]{3,2,1,0:T(8,128)(2,1)} %get-tuple-element.23.kv_ref), custom_call_target="tpu_custom_call" | custom-call | flops 17179869184 | bytes 1048576 | tf_op jit(solution)/shard_map/own_keys/pallas_call | solution.py:224
  25.2 4.5 %near_keys.1 = (f32[4,96,1024]{2,1,0:T(8,128)S(1)}, f32[8,1024]{1,0:T(8,128)S(1)}) custom-call(s32[1,3]{1,0:T(1,128)S(1)} %pad_add_fusion.plan_ref, s32[1,1024]{1,0:T(1,128)S(1)} %bitcast.14, bf16[4,128,1024]{2,1,0:T(8,128)(2,1)S(1)} %copy-done.4, f32[4,96,1024]{2,1,0:T(8,128)S(1)} %get-tuple-element.24.acc_in, f32[8,1024]{1,0:T(8,128)S(1)} %get-tuple-element.25.top_in, ...), custom_call_target="tpu_custom_call" | custom-call | flops 268435456 | bytes 1048576 | tf_op jit(solution)/shard_map/near_keys/pallas_call | solution.py:249
  29.9 2.7 %collective-permute-start.5 = (bf16[176,1408]{1,0:T(8,128)(2,1)S(1)}, bf16[176,1408]{1,0:T(8,128)(2,1)S(1)}, u32[]{:S(2)}, u32[]{:S(2)}) collective-permute-start(bf16[176,1408]{1,0:T(8,128)(2,1)S(1)} %slice.19), channel_id=1, source_target_pairs={{0,3},{1,0},{2,1},{3,2},{4,7},{5,4},{6,5},{7,6},{8,11},{9,8},{10,9... | collective-permute-start | bytes 1486856 | tf_op jit(solution)/shard_map/ppermute | solution.py:396
  32.6 4.7 %collective-permute-done.3.kv_ref = bf16[2,4,88,1024]{3,2,1,0:T(8,128)(2,1)} collective-permute-done((bf16[2,4,88,1024]{3,2,1,0:T(8,128)(2,1)}, bf16[2,4,88,1024]{3,2,1,0:T(8,128)(2,1)}, u32[]{:S(2)}, u32[]{:S(2)}) %collective-permute-start.3) | collective-permute-done | bytes 1441824 | tf_op jit(solution)/shard_map/ppermute | solution.py:412
  37.3 1.5 %far_keys.2.refs_0_ = bf16[176,1024]{1,0:T(8,128)(2,1)S(1)} custom-call(s32[1,3]{1,0:T(1,128)S(1)} %pad_add_fusion.plan_ref, s32[1,1024]{1,0:T(1,128)S(1)} %bitcast.15, bf16[4,128,1024]{2,1,0:T(8,128)(2,1)S(1)} %copy-done.4, f32[4,96,1024]{2,1,0:T(8,128)S(1)} %get-tuple-element.30.acc_in, f32[8,1024]{1,0:T(8,128)S(1)} %get-tuple-element.28.top_in, ...), custom_call_target="tpu_custom_call" | custom-call | flops 3221225472 | bytes 1048576 | tf_op jit(solution)/shard_map/far_keys/pallas_call | solution.py:274
  38.9 2.7 %collective-permute-start.7 = (bf16[176,1024]{1,0:T(8,128)(2,1)S(1)}, bf16[176,1024]{1,0:T(8,128)(2,1)S(1)}, u32[]{:S(2)}, u32[]{:S(2)}) collective-permute-start(bf16[176,1024]{1,0:T(8,128)(2,1)S(1)} %far_keys.2.refs_0_), channel_id=1, source_target_pairs={{0,3},{1,0},{2,1},{3,2},{4,7},{5,4},{6,5},{7,6},{8,11},{9,8},{10,9... | collective-permute-start | bytes 1081352 | tf_op jit(solution)/shard_map/ppermute | solution.py:391
  41.6 1.5 %far_keys.3.refs_1_ = bf16[176,1024]{1,0:T(8,128)(2,1)S(1)} custom-call(s32[1,3]{1,0:T(1,128)S(1)} %pad_add_fusion.plan_ref, s32[1,1024]{1,0:T(1,128)S(1)} %bitcast.16, bf16[4,128,1024]{2,1,0:T(8,128)(2,1)S(1)} %copy-done.4, f32[4,96,1024]{2,1,0:T(8,128)S(1)} %get-tuple-element.30.acc_in, f32[8,1024]{1,0:T(8,128)S(1)} %get-tuple-element.28.top_in, ...), custom_call_target="tpu_custom_call" | custom-call | flops 3221225472 | bytes 1048576 | tf_op jit(solution)/shard_map/far_keys/pallas_call | solution.py:274
  43.5 2.3 %collective-permute-start.9 = (bf16[176,1024]{1,0:T(8,128)(2,1)S(1)}, bf16[176,1024]{1,0:T(8,128)(2,1)S(1)}, u32[]{:S(2)}, u32[]{:S(2)}) collective-permute-start(bf16[176,1024]{1,0:T(8,128)(2,1)S(1)} %far_keys.3.refs_1_), channel_id=1, source_target_pairs={{0,3},{1,0},{2,1},{3,2},{4,7},{5,4},{6,5},{7,6},{8,11},{9,8},{10,9... | collective-permute-start | bytes 1081352 | tf_op jit(solution)/shard_map/ppermute | solution.py:391
  45.9 4.8 %collective-permute-done.6.refs_2_ = bf16[176,1024]{1,0:T(8,128)(2,1)S(1)} collective-permute-done((bf16[176,1024]{1,0:T(8,128)(2,1)S(1)}, bf16[176,1024]{1,0:T(8,128)(2,1)S(1)}, u32[]{:S(2)}, u32[]{:S(2)}) %collective-permute-start.6) | collective-permute-done | bytes 360480 | tf_op jit(solution)/shard_map/ppermute | solution.py:391
  51.0 2.7 %collective-permute-start.11 = (bf16[80,1024]{1,0:T(8,128)(2,1)S(1)}, bf16[80,1024]{1,0:T(8,128)(2,1)S(1)}, u32[]{:S(2)}, u32[]{:S(2)}) collective-permute-start(bf16[80,1024]{1,0:T(8,128)(2,1)S(1)} %slice.25), channel_id=1, source_target_pairs={{0,3},{1,0},{2,1},{3,2},{4,7},{5,4},{6,5},{7,6},{8,11},{9,8},{10,9... | collective-permute-start | bytes 491528 | tf_op jit(solution)/shard_map/ppermute | solution.py:396
  53.7 3.5 %output.2.base_ref = f32[1024,1408]{1,0:T(8,128)S(1)} custom-call(bf16[1024,1408]{1,0:T(8,128)(2,1)S(1)} %copy-done, bf16[176,1024]{1,0:T(8,128)(2,1)S(1)} %far_keys.2.refs_0_, bf16[176,1024]{1,0:T(8,128)(2,1)S(1)} %far_keys.3.refs_1_, bf16[176,1024]{1,0:T(8,128)(2,1)S(1)} %collective-permute-done.6.refs_2_, ...), custom_call_target="tpu_custom_call" | custom-call | flops 253755392 | bytes 65536 | tf_op jit(solution)/shard_map/output/pallas_call | solution.py:306
  57.2 1.2 %collective-permute-done.8.refs_2_ = bf16[176,1024]{1,0:T(8,128)(2,1)S(1)} collective-permute-done((bf16[176,1024]{1,0:T(8,128)(2,1)S(1)}, bf16[176,1024]{1,0:T(8,128)(2,1)S(1)}, u32[]{:S(2)}, u32[]{:S(2)}) %collective-permute-start.8) | collective-permute-done | bytes 360480 | tf_op jit(solution)/shard_map/ppermute | solution.py:391
  59.1 2.1 %collective-permute-start.13 = (bf16[80,1024]{1,0:T(8,128)(2,1)S(1)}, bf16[80,1024]{1,0:T(8,128)(2,1)S(1)}, u32[]{:S(2)}, u32[]{:S(2)}) collective-permute-start(bf16[80,1024]{1,0:T(8,128)(2,1)S(1)} %slice.23), channel_id=1, source_target_pairs={{0,3},{1,0},{2,1},{3,2},{4,7},{5,4},{6,5},{7,6},{8,11},{9,8},{10,9... | collective-permute-start | bytes 491528 | tf_op jit(solution)/shard_map/ppermute | solution.py:396
  61.3 1.3 %collective-permute-done.10.refs_0_ = bf16[96,1024]{1,0:T(8,128)(2,1)S(1)} collective-permute-done((bf16[96,1024]{1,0:T(8,128)(2,1)S(1)}, bf16[96,1024]{1,0:T(8,128)(2,1)S(1)}, u32[]{:S(2)}, u32[]{:S(2)}) %collective-permute-start.10) | collective-permute-done | bytes 196640 | tf_op jit(solution)/shard_map/ppermute | solution.py:396
  62.6 3.4 %output.3.base_ref = f32[1024,1408]{1,0:T(8,128)S(1)} custom-call(f32[1024,1408]{1,0:T(8,128)S(1)} %output.2.base_ref, bf16[96,1024]{1,0:T(8,128)(2,1)S(1)} %collective-permute-done.10.refs_0_, bf16[80,1024]{1,0:T(8,128)(2,1)S(1)} %collective-permute-done.11.refs_1_, bf16[176,1024]{1,0:T(8,128)(2,1)S(1)} %collective-permute-done.8.refs_2_, ...), custom_call_target="tpu_custom_call" | custom-call | flops 190316544 | bytes 65536 | tf_op jit(solution)/shard_map/output/pallas_call | solution.py:306
  66.0 3.6 %project.1 = bf16[512,640]{1,0:T(8,128)(2,1)S(1)} custom-call(s32[1,256]{1,0:T(1,128)S(1)} %bitcast.17, s32[1,256]{1,0:T(1,128)S(1)} %bitcast.18, f32[1024,1408]{1,0:T(8,128)S(1)} %output.3.base_ref, bf16[96,1024]{1,0:T(8,128)(2,1)S(1)} %collective-permute-done.12.refs_0_, bf16[80,1024]{1,0:T(8,128)(2,1)S(1)} %collective-permute-done.13.refs_1_, ...), custom_call_target="tpu_custom_call" | custom-call | flops 3221225472 | bytes 8388608 | tf_op jit(solution)/shard_map/project/pallas_call | solution.py:349
  69.6 35.4 %all_to_all.5 = bf16[64,8,640]{2,1,0:T(8,128)(2,1)} all-to-all(bf16[64,8,640]{2,1,0:T(8,128)(2,1)S(1)} %bitcast.9), channel_id=1, replica_groups=mesh['req'=64,'tp'=4] {'req'}, dimensions={0} | all-to-all | bytes 1310720 | tf_op jit(solution)/shard_map/all_to_all | solution.py:446
  105.0 2.1 %place.1 = bf16[256,512]{1,0:T(8,128)(2,1)} custom-call(bf16[512,640]{1,0:T(8,128)(2,1)} %bitcast.19), custom_call_target="tpu_custom_call" | custom-call | tf_op jit(solution)/shard_map/place/pallas_call | solution.py:372
  (45 shorter events, 2.8 us)
Async XLA Ops:
  0.0 29.7 %collective-permute-start.1 = (bf16[352,1408]{1,0:T(8,128)(2,1)}, bf16[352,1408]{1,0:T(8,128)(2,1)S(1)}, u32[]{:S(2)}, u32[]{:S(2)}) collective-permute-start(bf16[352,1408]{1,0:T(8,128)(2,1)} %refs_5_.1), channel_id=1, source_target_pairs={{0,1},{1,2},{2,3},{3,0},{4,5},{5,6},{6,7},{7,4},{8,9},{9,10},{10,1... | collective-permute-start | bytes 2973704 | tf_op jit(solution)/shard_map/ppermute | solution.py:391
  2.1 27.5 %collective-permute-start.2 = (bf16[352,1408]{1,0:T(8,128)(2,1)}, bf16[352,1408]{1,0:T(8,128)(2,1)S(1)}, u32[]{:S(2)}, u32[]{:S(2)}) collective-permute-start(bf16[352,1408]{1,0:T(8,128)(2,1)} %refs_5_.1), channel_id=1, source_target_pairs={{0,3},{1,0},{2,1},{3,2},{4,7},{5,4},{6,5},{7,6},{8,11},{9,8},{10,9... | collective-permute-start | bytes 2973704 | tf_op jit(solution)/shard_map/ppermute | solution.py:391
  3.6 14.9 %copy-start.8 = (s32[1,2]{1,0:T(1,128)S(1)}, s32[1,2]{1,0:T(1,128)}, u32[]{:S(2)}) copy-start(s32[1,2]{1,0:T(1,128)} %plan_ref.1) | copy-start | bytes 28
  3.6 15.0 %copy-start.5 = (s32[1024]{0:T(1024)S(1)}, s32[1024]{0:T(1024)}, u32[]{:S(2)}) copy-start(s32[1024]{0:T(1024)} %param.13) | copy-start | bytes 12292
  13.6 11.6 %collective-permute-start = (bf16[2,4,88,1024]{3,2,1,0:T(8,128)(2,1)}, bf16[2,4,88,1024]{3,2,1,0:T(8,128)(2,1)S(1)}, u32[]{:S(2)}, u32[]{:S(2)}) collective-permute-start(bf16[2,4,88,1024]{3,2,1,0:T(8,128)(2,1)} %get-tuple-element.23.kv_ref), channel_id=1, source_target_pairs={{0,4},{4,0},{8,12},{12,8},{16,20},{20,16},{24,28},{28,24},{32,36},... | collective-permute-start | bytes 4325384 | tf_op jit(solution)/shard_map/ppermute | solution.py:413
  16.5 20.8 %collective-permute-start.3 = (bf16[2,4,88,1024]{3,2,1,0:T(8,128)(2,1)}, bf16[2,4,88,1024]{3,2,1,0:T(8,128)(2,1)}, u32[]{:S(2)}, u32[]{:S(2)}) collective-permute-start(bf16[2,4,88,1024]{3,2,1,0:T(8,128)(2,1)} %get-tuple-element.23.kv_ref), channel_id=1, source_target_pairs={{4,8},{8,4},{12,16},{16,12},{20,24},{24,20},{28,32},{32,28},{36,40... | collective-permute-start | bytes 4325384 | tf_op jit(solution)/shard_map/ppermute | solution.py:412
  18.5 1.2 %copy-start.3 = (bf16[4,128,1024]{2,1,0:T(8,128)(2,1)S(1)}, bf16[4,128,1024]{2,1,0:T(8,128)(2,1)}, u32[]{:S(2)}) copy-start(bf16[4,128,1024]{2,1,0:T(8,128)(2,1)} %copy-done.2) | copy-start | bytes 3145732
  19.8 5.4 %copy-start.4 = (bf16[4,128,1024]{2,1,0:T(8,128)(2,1)S(1)}, bf16[4,128,1024]{2,1,0:T(8,128)(2,1)}, u32[]{:S(2)}) copy-start(bf16[4,128,1024]{2,1,0:T(8,128)(2,1)} %copy-done.2) | copy-start | bytes 3145732
  29.7 13.4 %collective-permute-start.4 = (bf16[176,1408]{1,0:T(8,128)(2,1)S(1)}, bf16[176,1408]{1,0:T(8,128)(2,1)S(1)}, u32[]{:S(2)}, u32[]{:S(2)}) collective-permute-start(bf16[176,1408]{1,0:T(8,128)(2,1)S(1)} %slice.18), channel_id=1, source_target_pairs={{0,1},{1,2},{2,3},{3,0},{4,5},{5,6},{6,7},{7,4},{8,9},{9,10},{10,1... | collective-permute-start | bytes 1486856 | tf_op jit(solution)/shard_map/ppermute | solution.py:396
  29.9 13.2 %collective-permute-start.5 = (bf16[176,1408]{1,0:T(8,128)(2,1)S(1)}, bf16[176,1408]{1,0:T(8,128)(2,1)S(1)}, u32[]{:S(2)}, u32[]{:S(2)}) collective-permute-start(bf16[176,1408]{1,0:T(8,128)(2,1)S(1)} %slice.19), channel_id=1, source_target_pairs={{0,3},{1,0},{2,1},{3,2},{4,7},{5,4},{6,5},{7,6},{8,11},{9,8},{10,9... | collective-permute-start | bytes 1486856 | tf_op jit(solution)/shard_map/ppermute | solution.py:396
  38.8 14.9 %copy-start = (bf16[1024,1408]{1,0:T(8,128)(2,1)S(1)}, bf16[1024,1408]{1,0:T(8,128)(2,1)}, u32[]{:S(2)}) copy-start(bf16[1024,1408]{1,0:T(8,128)(2,1)} %base_ref.1) | copy-start | bytes 8650756
  38.8 14.9 %copy-start.1 = (bf16[352,1408]{1,0:T(8,128)(2,1)S(1)}, bf16[352,1408]{1,0:T(8,128)(2,1)}, u32[]{:S(2)}) copy-start(bf16[352,1408]{1,0:T(8,128)(2,1)} %refs_5_.1) | copy-start | bytes 2973700
  38.8 11.8 %collective-permute-start.6 = (bf16[176,1024]{1,0:T(8,128)(2,1)S(1)}, bf16[176,1024]{1,0:T(8,128)(2,1)S(1)}, u32[]{:S(2)}, u32[]{:S(2)}) collective-permute-start(bf16[176,1024]{1,0:T(8,128)(2,1)S(1)} %far_keys.2.refs_0_), channel_id=1, source_target_pairs={{0,1},{1,2},{2,3},{3,0},{4,5},{5,6},{6,7},{7,4},{8,9},{9,10},{10,1... | collective-permute-start | bytes 1081352 | tf_op jit(solution)/shard_map/ppermute | solution.py:391
  38.9 12.0 %collective-permute-start.7 = (bf16[176,1024]{1,0:T(8,128)(2,1)S(1)}, bf16[176,1024]{1,0:T(8,128)(2,1)S(1)}, u32[]{:S(2)}, u32[]{:S(2)}) collective-permute-start(bf16[176,1024]{1,0:T(8,128)(2,1)S(1)} %far_keys.2.refs_0_), channel_id=1, source_target_pairs={{0,3},{1,0},{2,1},{3,2},{4,7},{5,4},{6,5},{7,6},{8,11},{9,8},{10,9... | collective-permute-start | bytes 1081352 | tf_op jit(solution)/shard_map/ppermute | solution.py:391
  43.1 15.3 %collective-permute-start.8 = (bf16[176,1024]{1,0:T(8,128)(2,1)S(1)}, bf16[176,1024]{1,0:T(8,128)(2,1)S(1)}, u32[]{:S(2)}, u32[]{:S(2)}) collective-permute-start(bf16[176,1024]{1,0:T(8,128)(2,1)S(1)} %far_keys.3.refs_1_), channel_id=1, source_target_pairs={{0,1},{1,2},{2,3},{3,0},{4,5},{5,6},{6,7},{7,4},{8,9},{9,10},{10,1... | collective-permute-start | bytes 1081352 | tf_op jit(solution)/shard_map/ppermute | solution.py:391
  43.5 14.8 %collective-permute-start.9 = (bf16[176,1024]{1,0:T(8,128)(2,1)S(1)}, bf16[176,1024]{1,0:T(8,128)(2,1)S(1)}, u32[]{:S(2)}, u32[]{:S(2)}) collective-permute-start(bf16[176,1024]{1,0:T(8,128)(2,1)S(1)} %far_keys.3.refs_1_), channel_id=1, source_target_pairs={{0,3},{1,0},{2,1},{3,2},{4,7},{5,4},{6,5},{7,6},{8,11},{9,8},{10,9... | collective-permute-start | bytes 1081352 | tf_op jit(solution)/shard_map/ppermute | solution.py:391
  50.7 11.9 %collective-permute-start.10 = (bf16[96,1024]{1,0:T(8,128)(2,1)S(1)}, bf16[96,1024]{1,0:T(8,128)(2,1)S(1)}, u32[]{:S(2)}, u32[]{:S(2)}) collective-permute-start(bf16[96,1024]{1,0:T(8,128)(2,1)S(1)} %slice.24), channel_id=1, source_target_pairs={{0,1},{1,2},{2,3},{3,0},{4,5},{5,6},{6,7},{7,4},{8,9},{9,10},{10,1... | collective-permute-start | bytes 589832 | tf_op jit(solution)/shard_map/ppermute | solution.py:396
  51.0 10.3 %copy-start.7 = (s32[256]{0:T(256)S(1)}, s32[256]{0:T(256)}, u32[]{:S(2)}) copy-start(s32[256]{0:T(256)} %param.16) | copy-start | bytes 3076
  51.0 10.3 %collective-permute-start.11 = (bf16[80,1024]{1,0:T(8,128)(2,1)S(1)}, bf16[80,1024]{1,0:T(8,128)(2,1)S(1)}, u32[]{:S(2)}, u32[]{:S(2)}) collective-permute-start(bf16[80,1024]{1,0:T(8,128)(2,1)S(1)} %slice.25), channel_id=1, source_target_pairs={{0,3},{1,0},{2,1},{3,2},{4,7},{5,4},{6,5},{7,6},{8,11},{9,8},{10,9... | collective-permute-start | bytes 491528 | tf_op jit(solution)/shard_map/ppermute | solution.py:396
  58.4 7.6 %collective-permute-start.12 = (bf16[96,1024]{1,0:T(8,128)(2,1)S(1)}, bf16[96,1024]{1,0:T(8,128)(2,1)S(1)}, u32[]{:S(2)}, u32[]{:S(2)}) collective-permute-start(bf16[96,1024]{1,0:T(8,128)(2,1)S(1)} %slice.22), channel_id=1, source_target_pairs={{0,1},{1,2},{2,3},{3,0},{4,5},{5,6},{6,7},{7,4},{8,9},{9,10},{10,1... | collective-permute-start | bytes 589832 | tf_op jit(solution)/shard_map/ppermute | solution.py:396
  59.1 6.8 %collective-permute-start.13 = (bf16[80,1024]{1,0:T(8,128)(2,1)S(1)}, bf16[80,1024]{1,0:T(8,128)(2,1)S(1)}, u32[]{:S(2)}, u32[]{:S(2)}) collective-permute-start(bf16[80,1024]{1,0:T(8,128)(2,1)S(1)} %slice.23), channel_id=1, source_target_pairs={{0,3},{1,0},{2,1},{3,2},{4,7},{5,4},{6,5},{7,6},{8,11},{9,8},{10,9... | collective-permute-start | bytes 491528 | tf_op jit(solution)/shard_map/ppermute | solution.py:396
  61.2 4.7 %slice-start = ((s8[5767168]{0:T(1024)(128)(4,1)}), s8[4194304]{0:T(1024)(128)(4,1)S(1)}, s32[]{:S(2)}) async-start(s8[5767168]{0:T(1024)(128)(4,1)} %bitcast.7), calls=%async_computation.1 | async-start | bytes 8388608
  61.3 4.7 %slice-start.1 = ((s8[5767168]{0:T(1024)(128)(4,1)}), s8[1572864]{0:T(1024)(128)(4,1)S(1)}, s32[]{:S(2)}) async-start(s8[5767168]{0:T(1024)(128)(4,1)} %bitcast.7), calls=%async_computation.2 | async-start | bytes 3145728
  61.3 4.7 %copy-start.6 = (s32[256]{0:T(256)S(1)}, s32[256]{0:T(256)}, u32[]{:S(2)}) copy-start(s32[256]{0:T(256)} %param.17) | copy-start | bytes 3076
  (1 other events, 1.0 us)

commit v8 on v7

--- a/solution.py
+++ b/solution.py
@@ -130,7 +130,7 @@
         out_specs=[
             pl.BlockSpec(shape[:-1] + (TILE,), lambda i, n=len(shape): (0,) * (n - 1) + (i,)) for shape in outs
         ],
-        out_shape=[jax.ShapeDtypeStruct(shape, BF16) for shape in outs],
+        out_shape=[pltpu.HBM(shape, BF16) for shape in outs],
         compiler_params=pltpu.CompilerParams(vmem_limit_bytes=12 << 20),
         cost_estimate=pl.CostEstimate(flops=flops // 1, bytes_accessed=1 << 20, transcendentals=0),
         name=name,

time: 107 us -> 106 us (level)
  transfers between devices with their start and end apart: 14 -> 14, of which waited for: 4 -> 5; matrix products, arithmetic and copies ran while one was open for 0% -> 0% of each run, Pallas kernels for 27% -> 26%
where the time goes in v8:
time: 106 us
  blocking collectives  34.5 us (33%)
  Pallas kernels  33.6 us (32%)
  starting transfers between devices  22.5 us (21%)
  waiting for transfers between devices  12.1 us (11%)
  local copies, waits for them, and re-layouts  2.76 us (3%)
    all_to_all x1, blocking collectives, on_device(): lax.all_to_all(send.reshape(peers, lanes, cols), 'req', split_axis=0, con...  34.5 us
    pallas_call x1, Pallas kernels, qkv_call(): pl.pallas_call(kernel, grid=(count // TILE,), in_specs=[pl.BlockSpec(memo...  9.08 us
    ppermute x3, starting transfers between devices, beyond(): lax.ppermute(right[half:], axis, ring(axis, -1))  7.55 us
    pallas_call x2, Pallas kernels, gather_call(): pl.pallas_call(functools.partial(gather_kernel, parts, rows), in_specs=[v...  6.82 us
    ppermute x3, waiting for transfers between devices, beside(): lax.ppermute(block, axis, ring(axis, 1))  6.24 us
    ppermute x3, starting transfers between devices, beside(): lax.ppermute(block, axis, ring(axis, -1))  6.12 us
    pallas_call x1, Pallas kernels, own_call(): pl.pallas_call(own_kernel, in_specs=[smem] + [vmem] * 3, out_specs=[vmem,...  4.52 us
    pallas_call x1, Pallas kernels, near_call(): pl.pallas_call(near_kernel, in_specs=[smem, smem, vmem, vmem, vmem, vmem]...  4.49 us
  transfers between devices with their start and end apart: 14, of which 5 were waited for; matrix products, arithmetic and copies ran while one was open for 0% of the time, Pallas kernels for 26%

profile of v8, /device:TPU:1, one launch (start us, length us, event | category | flops | bytes accessed | tf_op | source)
XLA Modules:
  0.0 105.7 jit_solution(8691693865403785747)
XLA Ops:
  0.0 2.1 %collective-permute-start.1 = (bf16[352,1408]{1,0:T(8,128)(2,1)}, bf16[352,1408]{1,0:T(8,128)(2,1)S(1)}, u32[]{:S(2)}, u32[]{:S(2)}) collective-permute-start(bf16[352,1408]{1,0:T(8,128)(2,1)} %refs_5_.1), channel_id=1, source_target_pairs={{0,1},{1,2},{2,3},{3,0},{4,5},{5,6},{6,7},{7,4},{8,9},{9,10},{10,1... | collective-permute-start | bytes 2973704 | tf_op jit(solution)/shard_map/ppermute | solution.py:391
  2.1 1.4 %collective-permute-start.2 = (bf16[352,1408]{1,0:T(8,128)(2,1)}, bf16[352,1408]{1,0:T(8,128)(2,1)S(1)}, u32[]{:S(2)}, u32[]{:S(2)}) collective-permute-start(bf16[352,1408]{1,0:T(8,128)(2,1)} %refs_5_.1), channel_id=1, source_target_pairs={{0,3},{1,0},{2,1},{3,2},{4,7},{5,4},{6,5},{7,6},{8,11},{9,8},{10,9... | collective-permute-start | bytes 2973704 | tf_op jit(solution)/shard_map/ppermute | solution.py:391
  3.6 9.1 %qkv.1 = (bf16[2,4,88,1024]{3,2,1,0:T(8,128)(2,1)}, bf16[4,128,1024]{2,1,0:T(8,128)(2,1)}) custom-call(s32[1,2]{1,0:T(1,128)} %plan_ref.1, bf16[176,192]{1,0:T(8,128)(2,1)} %constant.37.clone.table_ref, s32[1,1024]{1,0:T(1,128)} %bitcast.10, s32[1,1024]{1,0:T(1,128)} %bitcast.11, s32[1,1024]{1,0:T(1,128)} %bitcast.20, bf16[1024,1408]{1,0:T(8,128)(2,1)} %base_ref.1, ...), custom_call_target="tpu_custom_call" | custom-call | flops 3045064704 | bytes 1048576 | tf_op jit(solution)/shard_map/qkv/pallas_call | solution.py:116
  12.7 2.9 %collective-permute-start = (bf16[2,4,88,1024]{3,2,1,0:T(8,128)(2,1)}, bf16[2,4,88,1024]{3,2,1,0:T(8,128)(2,1)S(1)}, u32[]{:S(2)}, u32[]{:S(2)}) collective-permute-start(bf16[2,4,88,1024]{3,2,1,0:T(8,128)(2,1)} %get-tuple-element.23.kv_ref), channel_id=1, source_target_pairs={{0,4},{4,0},{8,12},{12,8},{16,20},{20,16},{24,28},{28,24},{32,36},... | collective-permute-start | bytes 4325384 | tf_op jit(solution)/shard_map/ppermute | solution.py:413
  15.6 1.9 %collective-permute-start.3 = (bf16[2,4,88,1024]{3,2,1,0:T(8,128)(2,1)}, bf16[2,4,88,1024]{3,2,1,0:T(8,128)(2,1)}, u32[]{:S(2)}, u32[]{:S(2)}) collective-permute-start(bf16[2,4,88,1024]{3,2,1,0:T(8,128)(2,1)} %get-tuple-element.23.kv_ref), channel_id=1, source_target_pairs={{4,8},{8,4},{12,16},{16,12},{20,24},{24,20},{28,32},{32,28},{36,40... | collective-permute-start | bytes 4325384 | tf_op jit(solution)/shard_map/ppermute | solution.py:412
  17.6 1.2 %copy-done.2 = bf16[4,128,1024]{2,1,0:T(8,128)(2,1)S(1)} copy-done((bf16[4,128,1024]{2,1,0:T(8,128)(2,1)S(1)}, bf16[4,128,1024]{2,1,0:T(8,128)(2,1)}, u32[]{:S(2)}) %copy-start.2) | copy-done | bytes 1048600
  18.8 1.4 %copy-done.6 = bf16[2,4,88,1024]{3,2,1,0:T(8,128)(2,1)S(1)} copy-done((bf16[2,4,88,1024]{3,2,1,0:T(8,128)(2,1)S(1)}, bf16[2,4,88,1024]{3,2,1,0:T(8,128)(2,1)}, u32[]{:S(2)}) %copy-start.6) | copy-done | bytes 1441816
  20.2 4.5 %own_keys.1 = (f32[4,96,1024]{2,1,0:T(8,128)S(1)}, f32[8,1024]{1,0:T(8,128)S(1)}) custom-call(s32[1,1024]{1,0:T(1,128)S(1)} %bitcast.12, s32[1,1024]{1,0:T(1,128)S(1)} %bitcast.13, bf16[4,128,1024]{2,1,0:T(8,128)(2,1)S(1)} %copy-done.2, bf16[2,4,88,1024]{3,2,1,0:T(8,128)(2,1)S(1)} %copy-done.6), custom_call_target="tpu_custom_call" | custom-call | flops 17179869184 | bytes 1048576 | tf_op jit(solution)/shard_map/own_keys/pallas_call | solution.py:224
  24.7 4.5 %near_keys.1 = (f32[4,96,1024]{2,1,0:T(8,128)S(1)}, f32[8,1024]{1,0:T(8,128)S(1)}) custom-call(s32[1,3]{1,0:T(1,128)S(1)} %pad_add_fusion.plan_ref, s32[1,1024]{1,0:T(1,128)S(1)} %bitcast.14, bf16[4,128,1024]{2,1,0:T(8,128)(2,1)S(1)} %copy-done.3, f32[4,96,1024]{2,1,0:T(8,128)S(1)} %get-tuple-element.24.acc_in, f32[8,1024]{1,0:T(8,128)S(1)} %get-tuple-element.25.top_in, ...), custom_call_target="tpu_custom_call" | custom-call | flops 268435456 | bytes 1048576 | tf_op jit(solution)/shard_map/near_keys/pallas_call | solution.py:249
  29.4 2.7 %collective-permute-start.5 = (bf16[176,1408]{1,0:T(8,128)(2,1)S(1)}, bf16[176,1408]{1,0:T(8,128)(2,1)S(1)}, u32[]{:S(2)}, u32[]{:S(2)}) collective-permute-start(bf16[176,1408]{1,0:T(8,128)(2,1)S(1)} %slice.19), channel_id=1, source_target_pairs={{0,3},{1,0},{2,1},{3,2},{4,7},{5,4},{6,5},{7,6},{8,11},{9,8},{10,9... | collective-permute-start | bytes 1486856 | tf_op jit(solution)/shard_map/ppermute | solution.py:396
  32.2 4.2 %collective-permute-done.3.kv_ref = bf16[2,4,88,1024]{3,2,1,0:T(8,128)(2,1)} collective-permute-done((bf16[2,4,88,1024]{3,2,1,0:T(8,128)(2,1)}, bf16[2,4,88,1024]{3,2,1,0:T(8,128)(2,1)}, u32[]{:S(2)}, u32[]{:S(2)}) %collective-permute-start.3) | collective-permute-done | bytes 1441824 | tf_op jit(solution)/shard_map/ppermute | solution.py:412
  36.4 1.5 %far_keys.2.refs_0_ = bf16[176,1024]{1,0:T(8,128)(2,1)S(1)} custom-call(s32[1,3]{1,0:T(1,128)S(1)} %pad_add_fusion.plan_ref, s32[1,1024]{1,0:T(1,128)S(1)} %bitcast.15, bf16[4,128,1024]{2,1,0:T(8,128)(2,1)S(1)} %copy-done.3, f32[4,96,1024]{2,1,0:T(8,128)S(1)} %get-tuple-element.30.acc_in, f32[8,1024]{1,0:T(8,128)S(1)} %get-tuple-element.28.top_in, ...), custom_call_target="tpu_custom_call" | custom-call | flops 3221225472 | bytes 1048576 | tf_op jit(solution)/shard_map/far_keys/pallas_call | solution.py:274
  38.0 2.7 %collective-permute-start.7 = (bf16[176,1024]{1,0:T(8,128)(2,1)S(1)}, bf16[176,1024]{1,0:T(8,128)(2,1)S(1)}, u32[]{:S(2)}, u32[]{:S(2)}) collective-permute-start(bf16[176,1024]{1,0:T(8,128)(2,1)S(1)} %far_keys.2.refs_0_), channel_id=1, source_target_pairs={{0,3},{1,0},{2,1},{3,2},{4,7},{5,4},{6,5},{7,6},{8,11},{9,8},{10,9... | collective-permute-start | bytes 1081352 | tf_op jit(solution)/shard_map/ppermute | solution.py:391
  40.7 1.5 %far_keys.3.refs_1_ = bf16[176,1024]{1,0:T(8,128)(2,1)S(1)} custom-call(s32[1,3]{1,0:T(1,128)S(1)} %pad_add_fusion.plan_ref, s32[1,1024]{1,0:T(1,128)S(1)} %bitcast.16, bf16[4,128,1024]{2,1,0:T(8,128)(2,1)S(1)} %copy-done.3, f32[4,96,1024]{2,1,0:T(8,128)S(1)} %get-tuple-element.30.acc_in, f32[8,1024]{1,0:T(8,128)S(1)} %get-tuple-element.28.top_in, ...), custom_call_target="tpu_custom_call" | custom-call | flops 3221225472 | bytes 1048576 | tf_op jit(solution)/shard_map/far_keys/pallas_call | solution.py:274
  43.1 2.0 %collective-permute-start.9 = (bf16[176,1024]{1,0:T(8,128)(2,1)S(1)}, bf16[176,1024]{1,0:T(8,128)(2,1)S(1)}, u32[]{:S(2)}, u32[]{:S(2)}) collective-permute-start(bf16[176,1024]{1,0:T(8,128)(2,1)S(1)} %far_keys.3.refs_1_), channel_id=1, source_target_pairs={{0,3},{1,0},{2,1},{3,2},{4,7},{5,4},{6,5},{7,6},{8,11},{9,8},{10,9... | collective-permute-start | bytes 1081352 | tf_op jit(solution)/shard_map/ppermute | solution.py:391
  45.1 5.0 %collective-permute-done.6.refs_2_ = bf16[176,1024]{1,0:T(8,128)(2,1)S(1)} collective-permute-done((bf16[176,1024]{1,0:T(8,128)(2,1)S(1)}, bf16[176,1024]{1,0:T(8,128)(2,1)S(1)}, u32[]{:S(2)}, u32[]{:S(2)}) %collective-permute-start.6) | collective-permute-done | bytes 360480 | tf_op jit(solution)/shard_map/ppermute | solution.py:391
  50.5 2.7 %collective-permute-start.11 = (bf16[80,1024]{1,0:T(8,128)(2,1)S(1)}, bf16[80,1024]{1,0:T(8,128)(2,1)S(1)}, u32[]{:S(2)}, u32[]{:S(2)}) collective-permute-start(bf16[80,1024]{1,0:T(8,128)(2,1)S(1)} %slice.25), channel_id=1, source_target_pairs={{0,3},{1,0},{2,1},{3,2},{4,7},{5,4},{6,5},{7,6},{8,11},{9,8},{10,9... | collective-permute-start | bytes 491528 | tf_op jit(solution)/shard_map/ppermute | solution.py:396
  53.2 3.5 %output.2.base_ref = f32[1024,1408]{1,0:T(8,128)S(1)} custom-call(bf16[1024,1408]{1,0:T(8,128)(2,1)S(1)} %copy-done, bf16[176,1024]{1,0:T(8,128)(2,1)S(1)} %far_keys.2.refs_0_, bf16[176,1024]{1,0:T(8,128)(2,1)S(1)} %far_keys.3.refs_1_, bf16[176,1024]{1,0:T(8,128)(2,1)S(1)} %collective-permute-done.6.refs_2_, ...), custom_call_target="tpu_custom_call" | custom-call | flops 253755392 | bytes 65536 | tf_op jit(solution)/shard_map/output/pallas_call | solution.py:306
  58.7 2.1 %collective-permute-start.13 = (bf16[80,1024]{1,0:T(8,128)(2,1)S(1)}, bf16[80,1024]{1,0:T(8,128)(2,1)S(1)}, u32[]{:S(2)}, u32[]{:S(2)}) collective-permute-start(bf16[80,1024]{1,0:T(8,128)(2,1)S(1)} %slice.23), channel_id=1, source_target_pairs={{0,3},{1,0},{2,1},{3,2},{4,7},{5,4},{6,5},{7,6},{8,11},{9,8},{10,9... | collective-permute-start | bytes 491528 | tf_op jit(solution)/shard_map/ppermute | solution.py:396
  60.8 1.3 %collective-permute-done.10.refs_0_ = bf16[96,1024]{1,0:T(8,128)(2,1)S(1)} collective-permute-done((bf16[96,1024]{1,0:T(8,128)(2,1)S(1)}, bf16[96,1024]{1,0:T(8,128)(2,1)S(1)}, u32[]{:S(2)}, u32[]{:S(2)}) %collective-permute-start.10) | collective-permute-done | bytes 196640 | tf_op jit(solution)/shard_map/ppermute | solution.py:396
  62.1 3.4 %output.3.base_ref = f32[1024,1408]{1,0:T(8,128)S(1)} custom-call(f32[1024,1408]{1,0:T(8,128)S(1)} %output.2.base_ref, bf16[96,1024]{1,0:T(8,128)(2,1)S(1)} %collective-permute-done.10.refs_0_, bf16[80,1024]{1,0:T(8,128)(2,1)S(1)} %collective-permute-done.11.refs_1_, bf16[176,1024]{1,0:T(8,128)(2,1)S(1)} %collective-permute-done.8.refs_2_, ...), custom_call_target="tpu_custom_call" | custom-call | flops 190316544 | bytes 65536 | tf_op jit(solution)/shard_map/output/pallas_call | solution.py:306
  65.5 3.6 %project.1 = bf16[512,640]{1,0:T(8,128)(2,1)S(1)} custom-call(s32[1,256]{1,0:T(1,128)S(1)} %bitcast.17, s32[1,256]{1,0:T(1,128)S(1)} %bitcast.18, f32[1024,1408]{1,0:T(8,128)S(1)} %output.3.base_ref, bf16[96,1024]{1,0:T(8,128)(2,1)S(1)} %collective-permute-done.12.refs_0_, bf16[80,1024]{1,0:T(8,128)(2,1)S(1)} %collective-permute-done.13.refs_1_, ...), custom_call_target="tpu_custom_call" | custom-call | flops 3221225472 | bytes 8388608 | tf_op jit(solution)/shard_map/project/pallas_call | solution.py:349
  69.2 34.5 %all_to_all.5 = bf16[64,8,640]{2,1,0:T(8,128)(2,1)} all-to-all(bf16[64,8,640]{2,1,0:T(8,128)(2,1)S(1)} %bitcast.9), channel_id=1, replica_groups=mesh['req'=64,'tp'=4] {'req'}, dimensions={0} | all-to-all | bytes 1310720 | tf_op jit(solution)/shard_map/all_to_all | solution.py:446
  103.6 2.1 %place.1 = bf16[256,512]{1,0:T(8,128)(2,1)} custom-call(bf16[512,640]{1,0:T(8,128)(2,1)} %bitcast.19), custom_call_target="tpu_custom_call" | custom-call | tf_op jit(solution)/shard_map/place/pallas_call | solution.py:372
  (45 shorter events, 3.6 us)
Async XLA Ops:
  0.0 29.2 %collective-permute-start.1 = (bf16[352,1408]{1,0:T(8,128)(2,1)}, bf16[352,1408]{1,0:T(8,128)(2,1)S(1)}, u32[]{:S(2)}, u32[]{:S(2)}) collective-permute-start(bf16[352,1408]{1,0:T(8,128)(2,1)} %refs_5_.1), channel_id=1, source_target_pairs={{0,1},{1,2},{2,3},{3,0},{4,5},{5,6},{6,7},{7,4},{8,9},{9,10},{10,1... | collective-permute-start | bytes 2973704 | tf_op jit(solution)/shard_map/ppermute | solution.py:391
  2.1 27.1 %collective-permute-start.2 = (bf16[352,1408]{1,0:T(8,128)(2,1)}, bf16[352,1408]{1,0:T(8,128)(2,1)S(1)}, u32[]{:S(2)}, u32[]{:S(2)}) collective-permute-start(bf16[352,1408]{1,0:T(8,128)(2,1)} %refs_5_.1), channel_id=1, source_target_pairs={{0,3},{1,0},{2,1},{3,2},{4,7},{5,4},{6,5},{7,6},{8,11},{9,8},{10,9... | collective-permute-start | bytes 2973704 | tf_op jit(solution)/shard_map/ppermute | solution.py:391
  3.6 13.9 %copy-start.8 = (s32[1,2]{1,0:T(1,128)S(1)}, s32[1,2]{1,0:T(1,128)}, u32[]{:S(2)}) copy-start(s32[1,2]{1,0:T(1,128)} %plan_ref.1) | copy-start | bytes 28
  3.6 14.0 %copy-start.4 = (s32[1024]{0:T(1024)S(1)}, s32[1024]{0:T(1024)}, u32[]{:S(2)}) copy-start(s32[1024]{0:T(1024)} %param.13) | copy-start | bytes 12292
  12.7 12.0 %collective-permute-start = (bf16[2,4,88,1024]{3,2,1,0:T(8,128)(2,1)}, bf16[2,4,88,1024]{3,2,1,0:T(8,128)(2,1)S(1)}, u32[]{:S(2)}, u32[]{:S(2)}) collective-permute-start(bf16[2,4,88,1024]{3,2,1,0:T(8,128)(2,1)} %get-tuple-element.23.kv_ref), channel_id=1, source_target_pairs={{0,4},{4,0},{8,12},{12,8},{16,20},{20,16},{24,28},{28,24},{32,36},... | collective-permute-start | bytes 4325384 | tf_op jit(solution)/shard_map/ppermute | solution.py:413
  15.6 20.8 %collective-permute-start.3 = (bf16[2,4,88,1024]{3,2,1,0:T(8,128)(2,1)}, bf16[2,4,88,1024]{3,2,1,0:T(8,128)(2,1)}, u32[]{:S(2)}, u32[]{:S(2)}) collective-permute-start(bf16[2,4,88,1024]{3,2,1,0:T(8,128)(2,1)} %get-tuple-element.23.kv_ref), channel_id=1, source_target_pairs={{4,8},{8,4},{12,16},{16,12},{20,24},{24,20},{28,32},{32,28},{36,40... | collective-permute-start | bytes 4325384 | tf_op jit(solution)/shard_map/ppermute | solution.py:412
  18.8 1.4 %copy-start.6 = (bf16[2,4,88,1024]{3,2,1,0:T(8,128)(2,1)S(1)}, bf16[2,4,88,1024]{3,2,1,0:T(8,128)(2,1)}, u32[]{:S(2)}) copy-start(bf16[2,4,88,1024]{3,2,1,0:T(8,128)(2,1)} %get-tuple-element.23.kv_ref) | copy-start | bytes 4325380
  20.2 4.5 %copy-start.3 = (bf16[4,128,1024]{2,1,0:T(8,128)(2,1)S(1)}, bf16[4,128,1024]{2,1,0:T(8,128)(2,1)}, u32[]{:S(2)}) copy-start(bf16[4,128,1024]{2,1,0:T(8,128)(2,1)} %get-tuple-element.22.q_ref) | copy-start | bytes 3145732
  29.3 13.2 %collective-permute-start.4 = (bf16[176,1408]{1,0:T(8,128)(2,1)S(1)}, bf16[176,1408]{1,0:T(8,128)(2,1)S(1)}, u32[]{:S(2)}, u32[]{:S(2)}) collective-permute-start(bf16[176,1408]{1,0:T(8,128)(2,1)S(1)} %slice.18), channel_id=1, source_target_pairs={{0,1},{1,2},{2,3},{3,0},{4,5},{5,6},{6,7},{7,4},{8,9},{9,10},{10,1... | collective-permute-start | bytes 1486856 | tf_op jit(solution)/shard_map/ppermute | solution.py:396
  29.4 13.0 %collective-permute-start.5 = (bf16[176,1408]{1,0:T(8,128)(2,1)S(1)}, bf16[176,1408]{1,0:T(8,128)(2,1)S(1)}, u32[]{:S(2)}, u32[]{:S(2)}) collective-permute-start(bf16[176,1408]{1,0:T(8,128)(2,1)S(1)} %slice.19), channel_id=1, source_target_pairs={{0,3},{1,0},{2,1},{3,2},{4,7},{5,4},{6,5},{7,6},{8,11},{9,8},{10,9... | collective-permute-start | bytes 1486856 | tf_op jit(solution)/shard_map/ppermute | solution.py:396
  37.9 15.4 %copy-start = (bf16[1024,1408]{1,0:T(8,128)(2,1)S(1)}, bf16[1024,1408]{1,0:T(8,128)(2,1)}, u32[]{:S(2)}) copy-start(bf16[1024,1408]{1,0:T(8,128)(2,1)} %base_ref.1) | copy-start | bytes 8650756
  37.9 15.4 %copy-start.1 = (bf16[352,1408]{1,0:T(8,128)(2,1)S(1)}, bf16[352,1408]{1,0:T(8,128)(2,1)}, u32[]{:S(2)}) copy-start(bf16[352,1408]{1,0:T(8,128)(2,1)} %refs_5_.1) | copy-start | bytes 2973700
  37.9 12.3 %collective-permute-start.6 = (bf16[176,1024]{1,0:T(8,128)(2,1)S(1)}, bf16[176,1024]{1,0:T(8,128)(2,1)S(1)}, u32[]{:S(2)}, u32[]{:S(2)}) collective-permute-start(bf16[176,1024]{1,0:T(8,128)(2,1)S(1)} %far_keys.2.refs_0_), channel_id=1, source_target_pairs={{0,1},{1,2},{2,3},{3,0},{4,5},{5,6},{6,7},{7,4},{8,9},{9,10},{10,1... | collective-permute-start | bytes 1081352 | tf_op jit(solution)/shard_map/ppermute | solution.py:391
  38.0 12.5 %collective-permute-start.7 = (bf16[176,1024]{1,0:T(8,128)(2,1)S(1)}, bf16[176,1024]{1,0:T(8,128)(2,1)S(1)}, u32[]{:S(2)}, u32[]{:S(2)}) collective-permute-start(bf16[176,1024]{1,0:T(8,128)(2,1)S(1)} %far_keys.2.refs_0_), channel_id=1, source_target_pairs={{0,3},{1,0},{2,1},{3,2},{4,7},{5,4},{6,5},{7,6},{8,11},{9,8},{10,9... | collective-permute-start | bytes 1081352 | tf_op jit(solution)/shard_map/ppermute | solution.py:391
  42.5 15.4 %collective-permute-start.8 = (bf16[176,1024]{1,0:T(8,128)(2,1)S(1)}, bf16[176,1024]{1,0:T(8,128)(2,1)S(1)}, u32[]{:S(2)}, u32[]{:S(2)}) collective-permute-start(bf16[176,1024]{1,0:T(8,128)(2,1)S(1)} %far_keys.3.refs_1_), channel_id=1, source_target_pairs={{0,1},{1,2},{2,3},{3,0},{4,5},{5,6},{6,7},{7,4},{8,9},{9,10},{10,1... | collective-permute-start | bytes 1081352 | tf_op jit(solution)/shard_map/ppermute | solution.py:391
  43.1 14.8 %collective-permute-start.9 = (bf16[176,1024]{1,0:T(8,128)(2,1)S(1)}, bf16[176,1024]{1,0:T(8,128)(2,1)S(1)}, u32[]{:S(2)}, u32[]{:S(2)}) collective-permute-start(bf16[176,1024]{1,0:T(8,128)(2,1)S(1)} %far_keys.3.refs_1_), channel_id=1, source_target_pairs={{0,3},{1,0},{2,1},{3,2},{4,7},{5,4},{6,5},{7,6},{8,11},{9,8},{10,9... | collective-permute-start | bytes 1081352 | tf_op jit(solution)/shard_map/ppermute | solution.py:391
  50.2 11.9 %collective-permute-start.10 = (bf16[96,1024]{1,0:T(8,128)(2,1)S(1)}, bf16[96,1024]{1,0:T(8,128)(2,1)S(1)}, u32[]{:S(2)}, u32[]{:S(2)}) collective-permute-start(bf16[96,1024]{1,0:T(8,128)(2,1)S(1)} %slice.24), channel_id=1, source_target_pairs={{0,1},{1,2},{2,3},{3,0},{4,5},{5,6},{6,7},{7,4},{8,9},{9,10},{10,1... | collective-permute-start | bytes 589832 | tf_op jit(solution)/shard_map/ppermute | solution.py:396
  50.5 10.3 %copy-start.7 = (s32[256]{0:T(256)S(1)}, s32[256]{0:T(256)}, u32[]{:S(2)}) copy-start(s32[256]{0:T(256)} %param.16) | copy-start | bytes 3076
  50.5 10.3 %collective-permute-start.11 = (bf16[80,1024]{1,0:T(8,128)(2,1)S(1)}, bf16[80,1024]{1,0:T(8,128)(2,1)S(1)}, u32[]{:S(2)}, u32[]{:S(2)}) collective-permute-start(bf16[80,1024]{1,0:T(8,128)(2,1)S(1)} %slice.25), channel_id=1, source_target_pairs={{0,3},{1,0},{2,1},{3,2},{4,7},{5,4},{6,5},{7,6},{8,11},{9,8},{10,9... | collective-permute-start | bytes 491528 | tf_op jit(solution)/shard_map/ppermute | solution.py:396
  57.9 7.6 %collective-permute-start.12 = (bf16[96,1024]{1,0:T(8,128)(2,1)S(1)}, bf16[96,1024]{1,0:T(8,128)(2,1)S(1)}, u32[]{:S(2)}, u32[]{:S(2)}) collective-permute-start(bf16[96,1024]{1,0:T(8,128)(2,1)S(1)} %slice.22), channel_id=1, source_target_pairs={{0,1},{1,2},{2,3},{3,0},{4,5},{5,6},{6,7},{7,4},{8,9},{9,10},{10,1... | collective-permute-start | bytes 589832 | tf_op jit(solution)/shard_map/ppermute | solution.py:396
  58.7 6.8 %collective-permute-start.13 = (bf16[80,1024]{1,0:T(8,128)(2,1)S(1)}, bf16[80,1024]{1,0:T(8,128)(2,1)S(1)}, u32[]{:S(2)}, u32[]{:S(2)}) collective-permute-start(bf16[80,1024]{1,0:T(8,128)(2,1)S(1)} %slice.23), channel_id=1, source_target_pairs={{0,3},{1,0},{2,1},{3,2},{4,7},{5,4},{6,5},{7,6},{8,11},{9,8},{10,9... | collective-permute-start | bytes 491528 | tf_op jit(solution)/shard_map/ppermute | solution.py:396
  60.8 4.7 %slice-start = ((s8[5767168]{0:T(1024)(128)(4,1)}), s8[4194304]{0:T(1024)(128)(4,1)S(1)}, s32[]{:S(2)}) async-start(s8[5767168]{0:T(1024)(128)(4,1)} %bitcast.7), calls=%async_computation.1 | async-start | bytes 8388608
  60.8 4.7 %slice-start.1 = ((s8[5767168]{0:T(1024)(128)(4,1)}), s8[1572864]{0:T(1024)(128)(4,1)S(1)}, s32[]{:S(2)}) async-start(s8[5767168]{0:T(1024)(128)(4,1)} %bitcast.7), calls=%async_computation.2 | async-start | bytes 3145728
  60.8 4.7 %copy-start.5 = (s32[256]{0:T(256)S(1)}, s32[256]{0:T(256)}, u32[]{:S(2)}) copy-start(s32[256]{0:T(256)} %param.17) | copy-start | bytes 3076
  (1 other events, 1.2 us)
